TPU v7x, 32 devices: a whole 2x2x4 slice. The times are simulated.
32 devices in a mesh: row: 8 (over z, y), col: 4 (over x, core).
Axes of the slice: x: 2, y: 2, z: 4, core: 2. Of those that a mesh axis runs over, the one named last changes fastest.
Arguments:
- image_states: bfloat16 [64, 3072], P(('row', 'col')), may hold values from -6 to 6
- latent: float32 [64, 64], P(('row', 'col')), may hold values from -6 to 6
- text_keys: bfloat16 [1024, 3072], P('row', 'col')
- text_values: bfloat16 [1024, 3072], P('row', 'col'), may hold values from -6 to 6
- mod_table: float32 [4, 8, 3072], replicated, may hold values from -3 to 3
- timestep: int32 [4], replicated, may hold values from 0 to 3
- grid_size: int32 [4, 2], replicated, may hold values from 1 to 8, as said below
- rope_offset: int32 [4, 2], replicated, may hold values from 0 to 63
- w_qkv: bfloat16 [3072, 9216], P(None, 'row'), may hold values from -0.109375 to 0.109375
- q_gain: float32 [128], replicated, may hold values from 0.1 to 1.9
- k_gain: float32 [128], replicated, may hold values from 0.5 to 4
- w_out: bfloat16 [3072, 3072], P('col', 'row'), may hold values from -0.109375 to 0.109375
- w_fc1: bfloat16 [3072, 12288], P(None, 'row'), may hold values from -0.109375 to 0.109375
- w_fc2: bfloat16 [12288, 3072], P('row'), may hold values from -0.0546875 to 0.0546875
- w_final: bfloat16 [3072, 64], replicated, may hold values from -0.109375 to 0.109375
Outputs:
- velocity: float32 [64, 64], P(('row', 'col'))
- next_latent: float32 [64, 64], P(('row', 'col'))
Inputs may be any that keep to these rules, and one draw needn't show every extreme that they name: `grid_size`: column 0 is a request's grid height, at most 2; column 1 its grid width, at most 8; in every draw some request has height 2 and some request width 8.
All inputs are finite; a program needn't handle non-finite values.
Results may differ from a plain program's by a relative error of at most 0.008.
Values may be sent and summed in bfloat16 or wider, within the bound.
No kernel may reach another device: no remote copies, remote signals or barrier semaphores. Data moves between devices by JAX's collectives and lax.ppermute only.
A program may use at most 128 MiB of HBM per device.

v0:
```python
import jax
import jax.numpy as jnp
from jax import lax
from jax.sharding import PartitionSpec as P

REQ = 4
TXT = 256
STEPS = 4


eps_norm = 1e-06
blend = 0.25
mask_floor = -1e30


def with_halo(cells, sides, width):
    for axis, dim in sides:
        count = lax.axis_size(axis)
        ends = count - 1
        head = lax.slice_in_dim(cells, 0, width, axis=dim)
        tail = lax.slice_in_dim(cells, cells.shape[dim] - width, cells.shape[dim], axis=dim)
        cells = jnp.concatenate(
            [
                lax.ppermute(tail, axis, [(i, (i + 1) % count) for i in range(ends)]),
                cells,
                lax.ppermute(head, axis, [((i + 1) % count, i) for i in range(ends)]),
            ],
            axis=dim,
        )
    return cells


def layer_norm(values):
    mean_value = jnp.mean(values, -1, keepdims=True)
    centred = values - mean_value
    return centred * lax.rsqrt(jnp.mean(centred * centred, -1, keepdims=True) + eps_norm)


def modulate(values, shift_vec, scale_vec):
    return (layer_norm(values) * (1.0 + scale_vec) + shift_vec).astype(jnp.bfloat16)


def rope_tables(pos_h, pos_w, head_size):
    time_half = head_size // 16
    axis_dim = (head_size - head_size // 8) // 2
    freq_index = jnp.arange(axis_dim // 2, dtype=jnp.float32)
    frequency = 10000.0 ** (-2.0 * freq_index / axis_dim)
    angles = jnp.concatenate(
        [
            jnp.zeros((pos_h.shape[0], time_half), jnp.float32),
            pos_h[:, None] * frequency[None, :],
            pos_w[:, None] * frequency[None, :],
        ],
        1,
    )
    return (jnp.cos(angles), jnp.sin(angles))


def norm_rope(values, gain_vec, cosine_table, sine_table, head_count, head_size):
    row_total = values.shape[0]
    per_head = values.astype(jnp.float32).reshape(row_total, head_count, head_size)
    per_head = (
        per_head * lax.rsqrt(jnp.mean(per_head * per_head, -1, keepdims=True) + eps_norm) * gain_vec
    )
    paired = per_head.reshape(row_total, head_count, head_size // 2, 2)
    even_part = paired[..., 0]
    odd_part = paired[..., 1]
    cos_wide = cosine_table[:, None, :]
    sin_wide = sine_table[:, None, :]
    turned = jnp.stack(
        [even_part * cos_wide - odd_part * sin_wide, even_part * sin_wide + odd_part * cos_wide], -1
    )
    return turned.reshape(row_total, head_count * head_size).astype(jnp.bfloat16)


def on_device(
    image_states,
    latent,
    text_keys,
    text_values,
    mod_table,
    timestep,
    grid_size,
    rope_offset,
    w_qkv,
    q_gain,
    k_gain,
    w_out,
    w_fc1,
    w_fc2,
    w_final,
):
    col_total = lax.axis_size("col")
    row_pos = lax.axis_index("row")
    col_pos = lax.axis_index("col")
    tile_w = image_states.shape[0]
    width = image_states.shape[1]
    head_size = q_gain.shape[0]
    head_count = width // head_size
    local_heads = head_count // col_total
    request = row_pos % REQ
    grid_row = row_pos // REQ
    grid_col = col_pos * tile_w + jnp.arange(tile_w, dtype=jnp.int32)
    req_slots = jnp.arange(REQ, dtype=jnp.int32)
    req_onehot = req_slots == request
    limits = jnp.sum(jnp.where(req_onehot[:, None], grid_size, 0), 0)
    offsets = jnp.sum(jnp.where(req_onehot[:, None], rope_offset, 0), 0)
    step_now = jnp.sum(jnp.where(req_onehot, timestep, 0))
    token_ok = (grid_row < limits[0]) & (grid_col < limits[1])
    modulation = lax.dynamic_index_in_dim(mod_table, step_now, 0, keepdims=False)
    states = image_states.astype(jnp.float32)
    normed = modulate(states, modulation[0], modulation[1])
    joined_cols = jnp.dot(
        lax.all_gather(normed, "row", axis=0, tiled=True), w_qkv, preferred_element_type=jnp.float32
    ).astype(jnp.bfloat16)
    joined = lax.all_to_all(joined_cols, "row", split_axis=0, concat_axis=1, tiled=True)
    pos_h = jnp.zeros((tile_w,), jnp.float32) + (grid_row + offsets[0]).astype(jnp.float32)
    pos_w = (grid_col + offsets[1]).astype(jnp.float32)
    cosine_table, sine_table = rope_tables(pos_h, pos_w, head_size)
    queries = norm_rope(joined[:, :width], q_gain, cosine_table, sine_table, head_count, head_size)
    image_keys = norm_rope(
        joined[:, width : 2 * width], k_gain, cosine_table, sine_table, head_count, head_size
    )
    q_heads, k_heads, v_heads = (
        lax.all_to_all(queries, "col", split_axis=1, concat_axis=0, tiled=True),
        lax.all_to_all(image_keys, "col", split_axis=1, concat_axis=0, tiled=True),
        lax.all_to_all(joined[:, 2 * width :], "col", split_axis=1, concat_axis=0, tiled=True),
    )
    image_rows = k_heads.shape[0]
    text_rows = text_keys.shape[0]
    shard_rows = image_rows + text_rows
    q_block = q_heads.reshape(image_rows, local_heads, head_size)
    key_rows = jnp.concatenate([k_heads, text_keys], 0)
    value_rows = jnp.concatenate([v_heads, text_values], 0)
    run_max = jnp.full((image_rows, local_heads), mask_floor, jnp.float32)
    key_piece = lax.all_gather(key_rows, "row", axis=0, tiled=True)
    value_piece = lax.all_gather(value_rows, "row", axis=0, tiled=True)
    piece_rows = key_piece.shape[0]
    global_row = jnp.arange(piece_rows, dtype=jnp.int32)
    shard_id = global_row // shard_rows
    within = global_row % shard_rows
    is_image = within < image_rows
    source_col = within // tile_w
    source_cell = within % tile_w
    image_req = shard_id % REQ
    text_req = (shard_id * text_rows + within - image_rows) // TXT
    key_req = jnp.where(is_image, image_req, text_req)
    key_onehot = key_req[:, None] == req_slots[None, :]
    key_height = jnp.sum(jnp.where(key_onehot, grid_size[:, 0][None, :], 0), 1)
    key_width = jnp.sum(jnp.where(key_onehot, grid_size[:, 1][None, :], 0), 1)
    image_ok = (shard_id // REQ < key_height) & (source_col * tile_w + source_cell < key_width)
    key_ok = (key_req == request) & (jnp.logical_not(is_image) | image_ok)
    scores = jnp.einsum(
        "qhd,khd->qhk",
        q_block,
        key_piece.reshape(piece_rows, local_heads, head_size),
        preferred_element_type=jnp.float32,
    ) * head_size ** (-0.5)
    new_max = jnp.maximum(run_max, jnp.max(jnp.where(key_ok, scores, mask_floor), -1))
    weights = jnp.where(key_ok, jnp.exp(scores - new_max[..., None]), 0.0)
    new_sum = jnp.sum(weights, -1)
    new_acc = jnp.einsum(
        "qhk,khd->qhd",
        weights.astype(jnp.bfloat16),
        value_piece.reshape(piece_rows, local_heads, head_size),
        preferred_element_type=jnp.float32,
    )
    mixed = (
        (new_acc / new_sum[..., None])
        .astype(jnp.bfloat16)
        .reshape(image_rows, local_heads * head_size)
    )
    partial_out = jnp.dot(
        mixed, lax.all_gather(w_out, "row", axis=1, tiled=True), preferred_element_type=jnp.float32
    )
    attended = lax.psum_scatter(
        partial_out.astype(jnp.bfloat16), "col", scatter_dimension=0, tiled=True
    ).astype(jnp.float32)
    first_res = (states + modulation[2] * attended).astype(jnp.bfloat16)
    normed_two = modulate(first_res.astype(jnp.float32), modulation[3], modulation[4])
    all_rows = lax.all_gather(normed_two, "row", axis=0, tiled=True)
    hidden = jax.nn.gelu(
        jnp.dot(all_rows, w_fc1, preferred_element_type=jnp.float32), approximate=True
    ).astype(jnp.bfloat16)
    every_term = jnp.dot(hidden, w_fc2, preferred_element_type=jnp.float32)
    every_sum = lax.psum(every_term, "row")
    mlp_out = lax.dynamic_slice_in_dim(every_sum, row_pos * tile_w, tile_w, 0)
    second_res = first_res.astype(jnp.float32) + modulation[5] * mlp_out
    normed_three = modulate(second_res, modulation[6], modulation[7])
    raw_velocity = jnp.dot(normed_three, w_final, preferred_element_type=jnp.float32)
    masked = jnp.where(token_ok[:, None], raw_velocity, 0.0)
    padded = with_halo(masked, (("col", 0),), 1)
    left_side = padded[:-2]
    right_side = padded[2:]
    velocity = jnp.where(
        token_ok[:, None], masked + blend * (left_side + right_side - 2.0 * masked), 0.0
    )
    next_latent = latent + -1.0 / STEPS * velocity
    return (velocity, next_latent)


def solution(mesh):
    placed = (
        P(("row", "col"), None),
        P(("row", "col"), None),
        P("row", "col"),
        P("row", "col"),
        P(),
        P(),
        P(),
        P(),
        P(None, "row"),
        P(),
        P(),
        P("col", "row"),
        P(None, "row"),
        P("row", None),
        P(),
    )
    return jax.shard_map(
        on_device,
        mesh=mesh,
        in_specs=placed,
        out_specs=(P(("row", "col"), None), P(("row", "col"), None)),
        check_vma=False,
    )
```

profile of v0, /device:TPU:0, one launch (start us, length us, event | category | flops | bytes accessed | tf_op | source)
XLA Modules:
  0.0 411.7 jit_solution(1863781639350607465)
XLA Ops:
  12.3 2.2 dynamic-slice_add_fusion
  15.3 32.3 %all-gather = bf16[8,2,3072]{2,1,0:T(2,128)(2,1)S(1)} all-gather(bf16[1,2,3072]{2,1,0:T(2,128)(2,1)S(1)} %fusion.50), channel_id=1, replica_groups=mesh['row'=8,'col'=4] {'row'}, dimensions={0}, use_global_device_ids=true | all-gather | bytes 110592 | tf_op jit(solution)/shard_map/all_gather | solution.py:114
  47.7 4.0 convolution_convert_fusion.1
  52.4 5.5 %all-to-all-start = ((bf16[8,2,1152]{2,1,0:T(2,128)(2,1)}), bf16[8,2,1152]{2,1,0:T(2,128)(2,1)S(1)}, u32[]{:S(2)}, u32[]{:S(2)}) async-start(bf16[8,2,1152]{2,1,0:T(2,128)(2,1)} %all_to_all.50), calls=%async_computation | async-start | bytes 73728 | tf_op jit(solution)/shard_map/all_to_all | solution.py:116
  61.9 2.8 all-to-all-done
  67.5 2.3 reshape.264
  71.7 5.2 %slice_multiply_fusion.5 = (f32[2,24,64,1]{3,2,1,0:T(8,128)}, f32[2,24,64,1]{3,2,1,0:T(8,128)}, f32[2,24,64,1]{3,2,1,0:T(8,128)}, f32[2,24,64,1]{3,2,1,0:T(8,128...) fusion(f32[2,24,64,2]{3,2,1,0:T(8,128)S(1)} %multiply_multiply_, ...), kind=kLoop, calls=%fused_computation.11 | loop fusion | flops 24576 | bytes 148480 | tf_op jit(solution)/shard_map/mul | solution.py:71
  76.9 2.5 copy.52
  79.4 2.5 copy.53
  81.9 2.5 copy.54
  84.5 2.5 copy.55
  89.1 2.0 copy.56
  91.1 2.1 convert_element_type.69
  93.2 6.9 %all_to_all.67 = bf16[2,4,768]{2,0,1:T(2,128)(2,1)} all-to-all(bf16[2,4,768]{2,0,1:T(2,128)(2,1)S(1)} %copy.57), channel_id=1, replica_groups=mesh['row'=8,'col'=4] {'col'}, dimensions={1} | all-to-all | bytes 24576 | tf_op jit(solution)/shard_map/all_to_all | solution.py:126
  100.8 1.6 pad_maximum_fusion.1
  102.5 7.8 %all_to_all.68 = bf16[2,4,768]{2,0,1:T(2,128)(2,1)} all-to-all(bf16[2,4,768]{2,0,1:T(2,128)(2,1)} %bitcast.72), channel_id=1, replica_groups=mesh['row'=8,'col'=4] {'col'}, dimensions={1} | all-to-all | bytes 24576 | tf_op jit(solution)/shard_map/all_to_all | solution.py:127
  113.5 2.5 copy.59
  116.0 2.5 copy.60
  122.6 3.3 all-to-all-start.3
  127.4 2.3 all-to-all-done.3
  129.7 15.6 %all-gather.8.cloned.1.call-done = bf16[1088,768]{1,0:T(8,128)(2,1)} async-done(((bf16[136,768]{1,0:T(8,128)(2,1)}), bf16[1088,768]{1,0:T(8,128)(2,1)}) %all-gather.8.cloned.1.call-update) | async-done | bytes 1671184 | tf_op jit(solution)/shard_map/all_gather | solution.py:136
  145.3 3.8 copy.58
  149.1 42.3 %all-gather.6.cloned.1.call-done = bf16[1088,768]{1,0:T(8,128)(2,1)} async-done(((bf16[136,768]{1,0:T(8,128)(2,1)}), bf16[1088,768]{1,0:T(8,128)(2,1)}) %all-gather.6.cloned.1.call-update) | async-done | bytes 1671184 | tf_op jit(solution)/shard_map/all_gather | solution.py:137
  191.4 2.7 copy.51
  194.1 1.9 select_reduce_fusion
  196.2 77.1 %all-gather.10.cloned.1.call-done = bf16[768,3072]{1,0:T(8,128)(2,1)} async-done(((bf16[768,384]{1,0:T(8,128)(2,1)}), bf16[768,3072]{1,0:T(8,128)(2,1)}) %all-gather.10.cloned.1.call-update) | async-done | bytes 4718608 | tf_op jit(solution)/shard_map/all_gather | solution.py:174
  273.4 3.7 convolution_convert_fusion
  277.0 11.0 %all-reduce = bf16[8,3072]{1,0:T(8,128)(2,1)S(1)} all-reduce(bf16[8,3072]{1,0:T(8,128)(2,1)S(1)} %convolution_convert_fusion), channel_id=2, replica_groups=mesh['row'=8,'col'=4] {'col'}, use_global_device_ids=true, to_apply=%region_11.12.clone | all-reduce | flops 24576 | bytes 98304
  288.5 30.5 %all-gather.1 = bf16[8,2,3072]{2,1,0:T(2,128)(2,1)S(1)} all-gather(bf16[1,2,3072]{2,1,0:T(2,128)(2,1)S(1)} %fusion.51), channel_id=1, replica_groups=mesh['row'=8,'col'=4] {'row'}, dimensions={0}, use_global_device_ids=true | all-gather | bytes 110592 | tf_op jit(solution)/shard_map/all_gather | solution.py:181
  319.2 9.6 %fusion.22 = f32[16,3072]{1,0:T(8,128)} fusion(bf16[1536,3072]{1,0:T(8,128)(2,1)} %param.28, bf16[16,3072]{1,0:T(8,128)(2,1)S(1)} %reshape.272, bf16[3072,1536]{1,0:T(8,128)(2,1)} %param.27), kind=kOutput, calls=%fused_computation.37 | convolution fusion | flops 302211072 | bytes 19169280 | tf_op jit(solution)/shard_map/dot_general | solution.py:185
  330.0 66.9 %all-reduce.3.cloned.1.call-done = f32[16,3072]{1,0:T(8,128)} async-done(((f32[16,3072]{1,0:T(8,128)}), f32[16,3072]{1,0:T(8,128)}) %all-reduce.3.cloned.1.call-update) | async-done | bytes 196624 | tf_op jit(solution)/shard_map/psum | solution.py:186
  401.1 3.4 collective-permute-done.1
  (113 shorter events, 29.7 us)
Async XLA Ops:
  7.2 391.0 %copy-start = (bf16[3072,64]{0,1:T(8,128)(2,1)S(1)}, bf16[3072,64]{0,1:T(8,128)(2,1)}, u32[]{:S(2)}) copy-start(bf16[3072,64]{0,1:T(8,128)(2,1)} %param.29) | copy-start | bytes 1179652
  47.7 10.3 %copy-start.12 = (s32[4,2]{0,1:T(2,128)S(1)}, s32[4,2]{0,1:T(2,128)}, u32[]{:S(2)}) copy-start(s32[4,2]{0,1:T(2,128)} %param.21) | copy-start | bytes 100
  47.7 10.3 %copy-start.13 = (s32[4,2]{0,1:T(2,128)S(1)}, s32[4,2]{0,1:T(2,128)}, u32[]{:S(2)}) copy-start(s32[4,2]{0,1:T(2,128)} %param.22) | copy-start | bytes 100
  47.7 12.7 %copy-start.15 = (f32[128]{0:T(128)S(1)}, f32[128]{0:T(128)}, u32[]{:S(2)}) copy-start(f32[128]{0:T(128)} %param.24) | copy-start | bytes 1540
  47.7 13.4 %copy-start.16 = (f32[128]{0:T(128)S(1)}, f32[128]{0:T(128)}, u32[]{:S(2)}) copy-start(f32[128]{0:T(128)} %param.25) | copy-start | bytes 1540
  52.4 12.2 %all-to-all-start = ((bf16[8,2,1152]{2,1,0:T(2,128)(2,1)}), bf16[8,2,1152]{2,1,0:T(2,128)(2,1)S(1)}, u32[]{:S(2)}, u32[]{:S(2)}) async-start(bf16[8,2,1152]{2,1,0:T(2,128)(2,1)} %all_to_all.50), calls=%async_computation | async-start | bytes 73728 | tf_op jit(solution)/shard_map/all_to_all | solution.py:116
  57.9 87.4 %all-gather.8.cloned.1.call-start = ((), (), s32[]{:S(2)}) async-start(), calls=%async_computation.5 | async-start | bytes 1880064 | tf_op jit(solution)/shard_map/all_gather | solution.py:136
  70.5 1.0 copy-start.2
  102.5 89.0 %all-gather.6.cloned.1.call-start = ((), (), s32[]{:S(2)}) async-start(), calls=%async_computation.4 | async-start | bytes 1880064 | tf_op jit(solution)/shard_map/all_gather | solution.py:137
  112.6 160.8 %all-gather.10.cloned.1.call-start = ((), (), s32[]{:S(2)}) async-start(), calls=%async_computation.6 | async-start | bytes 5308416 | tf_op jit(solution)/shard_map/all_gather | solution.py:174
  119.7 0.7 copy-start.3
  119.7 0.8 copy-start.4
  119.7 0.8 copy-start.5
  119.7 6.5 %copy-start.17 = (u32[32]{0:T(128)S(1)}, u32[32]{0:T(128)}, u32[]{:S(2)}) copy-start(u32[32]{0:T(128)} %constant.158) | copy-start | bytes 388
  122.6 7.1 %all-to-all-start.3 = ((bf16[2,4,768]{2,0,1:T(2,128)(2,1)}), bf16[2,4,768]{2,0,1:T(2,128)(2,1)S(1)}, u32[]{:S(2)}, u32[]{:S(2)}) async-start(bf16[2,4,768]{2,0,1:T(2,128)(2,1)} %copy.64), calls=%async_computation.3 | async-start | bytes 24576 | tf_op jit(solution)/shard_map/all_to_all | solution.py:125
  125.9 271.1 %all-reduce.3.cloned.1.call-start = ((), (), s32[]{:S(2)}) async-start(), calls=%async_computation.7 | async-start | bytes 393216 | tf_op jit(solution)/shard_map/psum | solution.py:186
  273.4 14.6 %copy-start.1 = (bf16[2,3072]{1,0:T(2,128)(2,1)S(1)}, bf16[2,3072]{1,0:T(2,128)(2,1)}, u32[]{:S(2)}) copy-start(bf16[2,3072]{1,0:T(2,128)(2,1)} %param.15) | copy-start | bytes 36868
  273.4 14.6 %copy-start.9 = (f32[1,1,3072]{2,1,0:T(1,128)S(1)}, f32[1,1,3072]{2,1,0:T(1,128)}, u32[]{:S(2)}) copy-start(f32[1,1,3072]{2,1,0:T(1,128)} %get-tuple-element.30) | copy-start | bytes 36868
  273.4 15.0 %copy-start.7 = (f32[1,1,3072]{2,1,0:T(1,128)S(1)}, f32[1,1,3072]{2,1,0:T(1,128)}, u32[]{:S(2)}) copy-start(f32[1,1,3072]{2,1,0:T(1,128)} %get-tuple-element.25) | copy-start | bytes 36868
  273.4 15.0 %copy-start.8 = (f32[1,1,3072]{2,1,0:T(1,128)S(1)}, f32[1,1,3072]{2,1,0:T(1,128)}, u32[]{:S(2)}) copy-start(f32[1,1,3072]{2,1,0:T(1,128)} %get-tuple-element.26) | copy-start | bytes 36868
  319.1 77.8 %copy-start.6 = (f32[1,1,3072]{2,1,0:T(1,128)S(1)}, f32[1,1,3072]{2,1,0:T(1,128)}, u32[]{:S(2)}) copy-start(f32[1,1,3072]{2,1,0:T(1,128)} %get-tuple-element.27) | copy-start | bytes 36868
  319.1 79.1 %copy-start.10 = (f32[1,1,3072]{2,1,0:T(1,128)S(1)}, f32[1,1,3072]{2,1,0:T(1,128)}, u32[]{:S(2)}) copy-start(f32[1,1,3072]{2,1,0:T(1,128)} %get-tuple-element.24) | copy-start | bytes 36868
  319.1 79.1 %copy-start.11 = (f32[1,1,3072]{2,1,0:T(1,128)S(1)}, f32[1,1,3072]{2,1,0:T(1,128)}, u32[]{:S(2)}) copy-start(f32[1,1,3072]{2,1,0:T(1,128)} %get-tuple-element.31) | copy-start | bytes 36868
  319.1 85.4 %copy-start.14 = (f32[2,64]{1,0:T(2,128)S(1)}, f32[2,64]{1,0:T(2,128)}, u32[]{:S(2)}) copy-start(f32[2,64]{1,0:T(2,128)} %param.16) | copy-start | bytes 1540
  398.5 2.6 collective-permute-start
  399.8 4.7 %collective-permute-start.1 = (f32[1,64]{1,0:T(1,128)S(1)}, f32[1,64]{1,0:T(1,128)S(1)}, u32[]{:S(2)}, u32[]{:S(2)}) collective-permute-start(f32[1,64]{1,0:T(1,128)S(1)} %get-tuple-element.46), channel_id=1, source_target_pairs={{1,0},{2,1},{3,2},{5,4},{6,5},{7,6},{9,8},{10,9},{11,10},{13,12},{... | collective-permute-start | bytes 776 | tf_op jit(solution)/shard_map/ppermute | solution.py:26
Sparse Core Ops, SparseCore 0:
  102.6 42.6 all-gather.7
  147.5 43.8 all-gather.5
  193.5 79.8 all-gather.9
  328.9 67.9 all-reduce.2
where the time goes:
time: 415 us; the launch traced here: 412 us
  waiting for transfers between devices  211 us (51%)
  blocking collectives  88.4 us (21%)
  local copies, waits for them, and re-layouts  38.6 us (9%)
  other arithmetic  24.4 us (6%)
  matrix products  19.5 us (5%)
  between operations  18 us (4%)
  starting transfers between devices  11.7 us (3%)
    all_gather x1, waiting for transfers between devices, on_device(): lax.all_gather(w_out, 'row', axis=1, tiled=True)  77.1 us
    psum x1, waiting for transfers between devices, on_device(): every_sum = lax.psum(every_term, 'row')  66.9 us
    all_gather x1, waiting for transfers between devices, on_device(): value_piece = lax.all_gather(value_rows, 'row', axis=0, tiled=True)  42.3 us
    all_gather x1, blocking collectives, on_device(): lax.all_gather(normed, 'row', axis=0, tiled=True)  32.3 us
    all_gather x1, blocking collectives, on_device(): all_rows = lax.all_gather(normed_two, 'row', axis=0, tiled=True)  30.5 us
    all_gather x1, waiting for transfers between devices, on_device(): key_piece = lax.all_gather(key_rows, 'row', axis=0, tiled=True)  15.6 us
    unnamed x1, blocking collectives  11 us
    dot_general x1, matrix products, on_device(): every_term = jnp.dot(hidden, w_fc2, preferred_element_type=jnp.float32)  9.61 us
  transfers between devices with their start and end apart: 8, of which 7 were waited for; matrix products, arithmetic and copies ran while one was open for 6% of the time, Pallas kernels for 0%

commit v1 on v0

--- a/solution.py
+++ b/solution.py
@@ -1,6 +1,10 @@
+import math
+
 import jax
 import jax.numpy as jnp
 from jax import lax
+from jax.experimental import pallas as pl
+from jax.experimental.pallas import tpu as pltpu
 from jax.sharding import PartitionSpec as P
 
 REQ = 4
@@ -199,6 +203,375 @@
     return (velocity, next_latent)
 
 
+bf16 = jnp.bfloat16
+QKV_CHUNKS = 6
+FC_CHUNKS = 6
+f32 = jnp.float32
+VMEM_SPEC = pl.BlockSpec(memory_space=pltpu.VMEM)
+SMEM_SPEC = pl.BlockSpec(memory_space=pltpu.SMEM)
+HBM_SPEC = pl.BlockSpec(memory_space=pltpu.HBM)
+
+
+def start_copies(pairs, sems):
+    copies = [pltpu.make_async_copy(source, target, sems.at[i]) for i, (source, target) in enumerate(pairs)]
+    for copy in copies:
+        copy.start()
+    return copies
+
+
+def row_chunks(source, target, count):
+    size = source.shape[0] // count
+    return [(source.at[pl.ds(i * size, size), :], target.at[pl.ds(i * size, size), :]) for i in range(count)]
+
+
+def chunked_dot(values, weights, copies):
+    size = weights.shape[0] // len(copies)
+    total = None
+    for i, copy in enumerate(copies):
+        copy.wait()
+        term = jnp.dot(
+            values[:, i * size : (i + 1) * size], weights[i * size : (i + 1) * size, :], preferred_element_type=f32
+        )
+        total = term if total is None else total + term
+    return total
+
+
+def lane_mean(values):
+    return jnp.mean(values, -1, keepdims=True)
+
+
+def norm_rows(values):
+    centred = values - lane_mean(values)
+    return centred * lax.rsqrt(lane_mean(centred * centred) + eps_norm)
+
+
+def per_request(mod_ref, step_ref, slot, rows_each, start, size):
+    pieces = [
+        jnp.broadcast_to(mod_ref[step_ref[q], pl.ds(slot, 1), pl.ds(start, size)], (rows_each, size))
+        for q in range(REQ)
+    ]
+    row = lax.broadcasted_iota(jnp.int32, (REQ * rows_each, size), 0) // rows_each
+    whole = jnp.concatenate([pieces[0]] * REQ, 0)
+    for q in range(1, REQ):
+        whole = jnp.where(row == q, jnp.concatenate([pieces[q]] * REQ, 0), whole)
+    return whole
+
+
+def qkv_kernel(step_ref, tokens_ref, mod_hbm, w_hbm, out_ref, order_ref, mod_ref, w_ref, sems):
+    row = lax.axis_index("row")
+    depth = order_ref.shape[1]
+    size = out_ref.shape[2]
+    mod_copy, *w_copies = start_copies([(mod_hbm, mod_ref)] + row_chunks(w_hbm, w_ref, QKV_CHUNKS), sems)
+    for q in range(REQ):
+        for g in range(2):
+            order_ref[4 * q + 2 * g : 4 * q + 2 * g + 2, :] = tokens_ref[REQ * g + q].astype(f32)
+    out_ref[...] = jnp.zeros_like(out_ref)
+    normed = norm_rows(order_ref[...])
+    mod_copy.wait()
+    shift = per_request(mod_ref, step_ref, 0, 4, 0, depth)
+    scale = per_request(mod_ref, step_ref, 1, 4, 0, depth)
+    normed = (normed * (1.0 + scale) + shift).astype(bf16)
+    whole = chunked_dot(normed, w_ref, w_copies).astype(bf16)
+    for piece in range(w_ref.shape[1] // size):
+        group = lax.rem(row * 3 + piece, 8)
+        place = lax.rem(group, 2) * 4 + group // 2
+        for q in range(REQ):
+            out_ref[8 * q + place] = whole[4 * q : 4 * q + 4, piece * size : (piece + 1) * size]
+
+
+def attention_kernel(
+    size_ref, offset_ref, rows_ref, own_k_hbm, own_v_hbm, other_k_hbm, other_v_hbm, q_gain_ref, k_gain_ref, out_ref,
+    q_ref, k_ref, v_ref, text_k_ref, text_v_ref, sems,
+):
+    row = lax.axis_index("row")
+    col = lax.axis_index("col")
+    req = row // 2
+    side = lax.rem(row, 2)
+    group = 2 * col + side
+    width = q_ref.shape[1]
+    head = q_gain_ref.shape[1]
+    heads = width // head
+    count = q_ref.shape[0]
+    half_rows = own_k_hbm.shape[0]
+    own = pl.ds(pl.multiple_of(side * width, width), width)
+    top_rows = pl.ds(0, half_rows)
+    low_rows = pl.ds(half_rows, half_rows)
+    copies = start_copies(
+        [
+            (own_k_hbm.at[:, own], text_k_ref.at[top_rows, :]),
+            (other_k_hbm, text_k_ref.at[low_rows, :]),
+            (own_v_hbm.at[:, own], text_v_ref.at[top_rows, :]),
+            (other_v_hbm, text_v_ref.at[low_rows, :]),
+        ],
+        sems,
+    )
+    for which, ref in enumerate((q_ref, k_ref, v_ref)):
+        source = (8 * which + group) // 3
+        for s in range(4):
+            ref[4 * s : 4 * s + 4, :] = rows_ref[source, s].astype(f32)
+    token = lax.broadcasted_iota(jnp.int32, (count, 1), 0)
+    pos_h = lax.rem(token, 4) // 2
+    pos_w = (token // 4) * 2 + lax.rem(token, 2)
+    lane = lax.broadcasted_iota(jnp.int32, (count, head), 1)
+    pair = lane // 2
+    time_half = head // 16
+    axis_dim = (head - head // 8) // 2
+    half = axis_dim // 2
+    in_h = (pair >= time_half) & (pair < time_half + half)
+    index = jnp.where(in_h, pair - time_half, pair - time_half - half).astype(f32)
+    frequency = jnp.exp(index * f32(-2.0 * math.log(10000.0) / axis_dim))
+    spot = jnp.where(in_h, pos_h + offset_ref[0, req], pos_w + offset_ref[1, req]).astype(f32)
+    angle = jnp.where(pair < time_half, 0.0, spot * frequency)
+    cosine = jnp.cos(angle)
+    sine = jnp.sin(angle)
+    even = lax.rem(lane, 2) == 0
+    sine = jnp.where(even, -sine, sine)
+
+    def turned(values, gain):
+        values = values * lax.rsqrt(lane_mean(values * values) + eps_norm) * gain
+        swapped = jnp.where(even, pltpu.roll(values, head - 1, 1), pltpu.roll(values, 1, 1))
+        return (values * cosine + swapped * sine).astype(bf16)
+
+    key = lax.broadcasted_iota(jnp.int32, (count, count), 1)
+    key_ok = (lax.rem(key, 4) // 2 < size_ref[0, req]) & ((key // 4) * 2 + lax.rem(key, 2) < size_ref[1, req])
+    contract = (((1,), (1,)), ((), ()))
+    scale = head ** (-0.5)
+    queries = [turned(q_ref[:, h * head : (h + 1) * head], q_gain_ref[...]) for h in range(heads)]
+    keys = [turned(k_ref[:, h * head : (h + 1) * head], k_gain_ref[...]) for h in range(heads)]
+    for copy in copies:
+        copy.wait()
+    for h in range(heads):
+        cols = slice(h * head, (h + 1) * head)
+        v = v_ref[:, cols].astype(bf16)
+        s_text = lax.dot_general(queries[h], text_k_ref[:, cols], contract, preferred_element_type=f32) * scale
+        s_image = lax.dot_general(queries[h], keys[h], contract, preferred_element_type=f32) * scale
+        s_image = jnp.where(key_ok, s_image, mask_floor)
+        top = jnp.maximum(jnp.max(s_text, -1, keepdims=True), jnp.max(s_image, -1, keepdims=True))
+        w_text = jnp.exp(s_text - top)
+        w_image = jnp.where(key_ok, jnp.exp(s_image - top), 0.0)
+        total = jnp.sum(w_text, -1, keepdims=True) + jnp.sum(w_image, -1, keepdims=True)
+        summed = jnp.dot(w_text.astype(bf16), text_v_ref[:, cols], preferred_element_type=f32) + jnp.dot(
+            w_image.astype(bf16), v, preferred_element_type=f32
+        )
+        mixed = (summed / total).astype(bf16)
+        for s in range(4):
+            for r in range(8):
+                out_ref[4 * r + s, :, cols] = mixed[4 * s : 4 * s + 4, :]
+
+
+def out_kernel(
+    step_ref, mixed_ref, tokens_ref, mod_hbm, w0_hbm, w1_hbm, w2_hbm, w3_hbm, out_ref, rows_ref, states_ref, mod_ref,
+    w_ref, sems,
+):
+    row = lax.axis_index("row")
+    col = lax.axis_index("col")
+    depth, width = w0_hbm.shape
+    piece = mixed_ref.shape[2]
+    start = pl.multiple_of(row * width, width)
+    mod_copy, *w_copies = start_copies(
+        [(mod_hbm, mod_ref)]
+        + [
+            (w_hbm, w_ref.at[pl.ds(pl.multiple_of(jnp.bitwise_xor(col, d) * depth, depth), depth), :])
+            for d, w_hbm in enumerate((w0_hbm, w1_hbm, w2_hbm, w3_hbm))
+        ],
+        sems,
+    )
+    for r in range(8):
+        for s in range(4):
+            at = (2 * s + r % 2) * piece
+            rows_ref[4 * (r // 2) : 4 * (r // 2) + 4, at : at + piece] = mixed_ref[4 * r + s].astype(f32)
+    for q in range(REQ):
+        for g in range(2):
+            states_ref[4 * q + 2 * g : 4 * q + 2 * g + 2, :] = tokens_ref[REQ * g + q, :, pl.ds(start, width)].astype(f32)
+    mixed = rows_ref[...].astype(bf16)
+    mod_copy.wait()
+    gate = per_request(mod_ref, step_ref, 2, 4, start, width)
+    for copy in w_copies:
+        copy.wait()
+    attended = jnp.dot(mixed, w_ref[...], preferred_element_type=f32)
+    first = (states_ref[...] + gate * attended).astype(bf16)
+    for r in range(8):
+        out_ref[r] = first
+
+
+def mlp_kernel(
+    step_ref, first_ref, mod_hbm, w1_hbm, w2_hbm, out_ref, rows_ref, mod_ref, w1_ref, w2_ref, sems
+):
+    row = lax.axis_index("row")
+    depth = rows_ref.shape[1]
+    piece = first_ref.shape[2]
+    mod_copy, *w_copies = start_copies(
+        [(mod_hbm, mod_ref)] + row_chunks(w1_hbm, w1_ref, FC_CHUNKS) + row_chunks(w2_hbm, w2_ref, FC_CHUNKS), sems
+    )
+    for r in range(8):
+        rows_ref[:, r * piece : (r + 1) * piece] = first_ref[r].astype(f32)
+    normed = norm_rows(rows_ref[...])
+    mod_copy.wait()
+    shift = per_request(mod_ref, step_ref, 3, 4, 0, depth)
+    scale = per_request(mod_ref, step_ref, 4, 4, 0, depth)
+    normed = (normed * (1.0 + scale) + shift).astype(bf16)
+    hidden = jax.nn.gelu(chunked_dot(normed, w1_ref, w_copies[:FC_CHUNKS]), approximate=True).astype(bf16)
+    added = chunked_dot(hidden, w2_ref, w_copies[FC_CHUNKS:])
+    gate = per_request(mod_ref, step_ref, 5, 4, 0, depth)
+    mine = jnp.where(row == 0, 1.0, 0.0)
+    term = gate * added + mine * rows_ref[...]
+    for q in range(REQ):
+        for g in range(2):
+            out_ref[REQ * g + q] = term[4 * q + 2 * g : 4 * q + 2 * g + 2, :]
+
+
+def final_kernel(step_ref, size_ref, terms_ref, mod_hbm, w_hbm, out_ref, mod_ref, w_ref, sems):
+    row = lax.axis_index("row")
+    col = lax.axis_index("col")
+    req = lax.rem(row, REQ)
+    step = step_ref[req]
+    mod_copy, w_copy = start_copies([(mod_hbm.at[step], mod_ref), (w_hbm, w_ref)], sems)
+    second = terms_ref[0]
+    for r in range(1, 8):
+        second = second + terms_ref[r]
+    normed = norm_rows(second)
+    mod_copy.wait()
+    normed = (normed * (1.0 + mod_ref[7:8, :]) + mod_ref[6:7, :]).astype(bf16)
+    w_copy.wait()
+    raw = lax.dot_general(normed, w_ref[...], (((1,), (1,)), ((), ())), preferred_element_type=f32)
+    out_ref[...] = jnp.where(live_rows(size_ref, row, col, raw.shape), raw, 0.0)
+
+
+def live_rows(size_ref, row, col, shape):
+    req = lax.rem(row, REQ)
+    grid_col = col * shape[0] + lax.broadcasted_iota(jnp.int32, shape, 0)
+    return (row // REQ < size_ref[0, req]) & (grid_col < size_ref[1, req])
+
+
+def blend_kernel(size_ref, masked_ref, before_ref, after_ref, latent_ref, velocity_ref, next_ref):
+    masked = masked_ref[...]
+    count = masked.shape[0]
+    left = jnp.concatenate([before_ref[count - 1 :, :], masked[: count - 1, :]], 0)
+    right = jnp.concatenate([masked[1:, :], after_ref[:1, :]], 0)
+    live = live_rows(size_ref, lax.axis_index("row"), lax.axis_index("col"), masked.shape)
+    velocity = jnp.where(live, masked + blend * (left + right - 2.0 * masked), 0.0)
+    velocity_ref[...] = velocity
+    next_ref[...] = latent_ref[...] + -1.0 / STEPS * velocity
+
+
+def call(kernel, shape, dtype, specs, scratch=(), grid=(), out_spec=None, limit=None):
+    return pl.pallas_call(
+        kernel,
+        out_shape=jax.ShapeDtypeStruct(shape, dtype),
+        grid_spec=pltpu.PrefetchScalarGridSpec(
+            num_scalar_prefetch=0,
+            grid=grid,
+            in_specs=specs,
+            out_specs=out_spec if out_spec is not None else VMEM_SPEC,
+            scratch_shapes=list(scratch),
+        ),
+        compiler_params=pltpu.CompilerParams(vmem_limit_bytes=limit),
+    )
+
+
+def exchange(values, axes):
+    return lax.all_to_all(values, axes, split_axis=0, concat_axis=0, tiled=True)
+
+
+def compact_on_device(
+    image_states, latent, text_keys, text_values, mod_table, timestep, grid_size, rope_offset,
+    w_qkv, q_gain, k_gain, w_out, w_fc1, w_fc2, w_final,
+):
+    rows = lax.axis_size("row")
+    cols = lax.axis_size("col")
+    row = lax.axis_index("row")
+    tile_w, width = image_states.shape
+    head = q_gain.shape[0]
+    piece = width // 8
+    tokens = rows * tile_w
+    both = ("row", "col")
+
+    gathered = exchange(jnp.broadcast_to(image_states[None], (rows, tile_w, width)), "row")
+
+    give = (1 - row % 2) * piece
+    swap = [(i, i ^ 1) for i in range(rows)]
+    other_k = lax.ppermute(lax.dynamic_slice_in_dim(text_keys, give, piece, 1), "row", swap)
+    other_v = lax.ppermute(lax.dynamic_slice_in_dim(text_values, give, piece, 1), "row", swap)
+    w_x = lax.ppermute(w_out, "col", [(i, i ^ 2) for i in range(cols)])
+    near = [(i, i ^ 1) for i in range(cols)]
+    w_k = lax.ppermute(w_out, "col", near)
+
+    sems = lambda count: pltpu.SemaphoreType.DMA((count,))
+    mod_space = pltpu.VMEM(mod_table.shape, f32)
+    pieces = call(
+        qkv_kernel,
+        (rows * cols, 4, piece),
+        bf16,
+        [SMEM_SPEC, VMEM_SPEC, HBM_SPEC, HBM_SPEC],
+        [pltpu.VMEM((tokens, width), f32), mod_space, pltpu.VMEM(w_qkv.shape, bf16), sems(QKV_CHUNKS + 1)],
+        limit=16 << 20,
+    )(timestep, gathered, mod_table, w_qkv)
+    got = exchange(pieces, both).reshape(rows, cols, 4, piece)
+    text_space = pltpu.VMEM((2 * text_keys.shape[0], piece), bf16)
+    mixed = call(
+        attention_kernel,
+        (rows * cols, 4, piece),
+        bf16,
+        [SMEM_SPEC, SMEM_SPEC, VMEM_SPEC] + [HBM_SPEC] * 4 + [VMEM_SPEC] * 2,
+        [pltpu.VMEM((tokens, piece), f32)] * 3 + [text_space] * 2 + [sems(4)],
+        limit=8 << 20,
+    )(
+        grid_size.T, rope_offset.T, got, text_keys, text_values, other_k, other_v,
+        q_gain.reshape(1, head), k_gain.reshape(1, head),
+    )
+    mixed, w_x = lax.optimization_barrier((mixed, w_x))
+    w_xk = lax.ppermute(w_x, "col", near)
+    all_mixed = exchange(mixed, both)
+    first = call(
+        out_kernel,
+        (rows, tokens, piece),
+        bf16,
+        [SMEM_SPEC, VMEM_SPEC, VMEM_SPEC] + [HBM_SPEC] * 5,
+        [
+            pltpu.VMEM((tokens, width), f32),
+            pltpu.VMEM((tokens, piece), f32),
+            mod_space,
+            pltpu.VMEM((width, piece), bf16),
+            sems(5),
+        ],
+        limit=16 << 20,
+    )(timestep, all_mixed, gathered, mod_table, w_out, w_k, w_x, w_xk)
+    all_first = exchange(first, "row")
+    terms = call(
+        mlp_kernel,
+        (rows, tile_w, width),
+        f32,
+        [SMEM_SPEC, VMEM_SPEC] + [HBM_SPEC] * 3,
+        [
+            pltpu.VMEM((tokens, width), f32),
+            mod_space,
+            pltpu.VMEM(w_fc1.shape, bf16),
+            pltpu.VMEM(w_fc2.shape, bf16),
+            sems(2 * FC_CHUNKS + 1),
+        ],
+        limit=40 << 20,
+    )(timestep, all_first, mod_table, w_fc1, w_fc2)
+    all_terms = exchange(terms, "row")
+    masked = call(
+        final_kernel,
+        (tile_w, w_final.shape[1]),
+        f32,
+        [SMEM_SPEC, SMEM_SPEC, VMEM_SPEC, HBM_SPEC, HBM_SPEC],
+        [pltpu.VMEM(mod_table.shape[1:], f32), pltpu.VMEM(w_final.shape[::-1], bf16), sems(2)],
+        limit=8 << 20,
+    )(timestep, grid_size.T, all_terms, mod_table, w_final.T)
+    before = lax.ppermute(masked, "col", [(i, i + 1) for i in range(cols - 1)])
+    after = lax.ppermute(masked, "col", [(i + 1, i) for i in range(cols - 1)])
+    result = jax.ShapeDtypeStruct(latent.shape, f32)
+    return pl.pallas_call(
+        blend_kernel,
+        out_shape=(result, result),
+        in_specs=[SMEM_SPEC] + [VMEM_SPEC] * 4,
+        out_specs=(VMEM_SPEC, VMEM_SPEC),
+        compiler_params=pltpu.CompilerParams(vmem_limit_bytes=8 << 20),
+    )(grid_size.T, masked, before, after, latent)
+
+
 def solution(mesh):
     placed = (
         P(("row", "col"), None),
@@ -217,8 +590,9 @@
         P("row", None),
         P(),
     )
+    compact = mesh.shape["row"] == 2 * REQ and mesh.shape["col"] == 4
     return jax.shard_map(
-        on_device,
+        compact_on_device if compact else on_device,
         mesh=mesh,
         in_specs=placed,
         out_specs=(P(("row", "col"), None), P(("row", "col"), None)),

time: 415 us -> 96.2 us (0.23)
  waiting for transfers between devices: 211 us -> 17.9 us
  blocking collectives: 88.4 us -> 19.7 us
  other arithmetic: 24.4 us -> 0 us
  local copies, waits for them, and re-layouts: 38.6 us -> 16.1 us
  matrix products: 19.5 us -> 0 us
  Pallas kernels: 0 us -> 17.4 us
  between operations: 18 us -> 0.78 us
  starting transfers between devices: 11.7 us -> 23.6 us
    all_gather x3 -> x0, waiting for transfers between devices: 135 us -> none  [the longest x1 77.1 us: on_device(): lax.all_gather(w_out, 'row', axis=1, tiled=True)]
    psum x1 -> x0, waiting for transfers between devices: 66.9 us -> none  [on_device(): every_sum = lax.psum(every_term, 'row')]
    all_gather x2 -> x0, blocking collectives: 62.9 us -> none  [the longest x1 32.3 us: on_device(): lax.all_gather(normed, 'row', axis=0, tiled=True)]
    dot_general x5 -> x0, matrix products: 19.5 us -> none  [the longest x1 9.61 us: on_device(): every_term = jnp.dot(hidden, w_fc2, preferred_element_type=jnp.float32)]
    mul x10 -> x0, local copies, waits for them, and re-layouts: 18.3 us -> none  [the longest x2 5.06 us: norm_rope(): even_part * cos_wide - odd_part * sin_wide]
    pallas_call x0 -> x6, Pallas kernels: none -> 17.4 us  [the longest x1 5.55 us: compact_on_device(): call(mlp_kernel, (rows, tile_w, width), f32, [SMEM_SPEC, VMEM_SPEC] + [HB...]
    unnamed x39 -> x32, local copies, waits for them, and re-layouts: 0.98 us -> 12.9 us
    unnamed x1 -> x0, blocking collectives: 11 us -> none
  transfers between devices with their start and end apart: 8 -> 10, of which waited for: 7 -> 5; matrix products, arithmetic and copies ran while one was open for 6% -> 3% of each run, Pallas kernels for 0% -> 8%
where the time goes in v1:
time: 96.2 us; the launch traced here: 95.4 us
  starting transfers between devices  23.6 us (25%)
  blocking collectives  19.7 us (20%)
  waiting for transfers between devices  17.9 us (19%)
  Pallas kernels  17.4 us (18%)
  local copies, waits for them, and re-layouts  16.1 us (17%)
    all_to_all x2, blocking collectives, exchange(): return lax.all_to_all(values, axes, split_axis=0, concat_axis=0, tiled=True)  19.7 us
    all_to_all x3, waiting for transfers between devices, exchange(): return lax.all_to_all(values, axes, split_axis=0, concat_axis=0, tiled=True)  13.3 us
    unnamed x32, local copies, waits for them, and re-layouts  12.9 us
    all_to_all x3, starting transfers between devices, exchange(): return lax.all_to_all(values, axes, split_axis=0, concat_axis=0, tiled=True)  12.3 us
    pallas_call x1, Pallas kernels, compact_on_device(): call(mlp_kernel, (rows, tile_w, width), f32, [SMEM_SPEC, VMEM_SPEC] + [HB...  5.55 us
    pallas_call x1, Pallas kernels, compact_on_device(): call(qkv_kernel, (rows * cols, 4, piece), bf16, [SMEM_SPEC, VMEM_SPEC, HB...  4.88 us
    ppermute x1, waiting for transfers between devices, compact_on_device(): lax.ppermute(lax.dynamic_slice_in_dim(text_keys, give, piece, 1), 'row',...  3.81 us
    ppermute x1, starting transfers between devices, compact_on_device(): before = lax.ppermute(masked, 'col', [(i, i + 1) for i in range(cols - 1)])  3.03 us
  transfers between devices with their start and end apart: 10, of which 5 were waited for; matrix products, arithmetic and copies ran while one was open for 3% of the time, Pallas kernels for 8%

profile of v1, /device:TPU:0, one launch (start us, length us, event | category | flops | bytes accessed | tf_op | source)
XLA Modules:
  0.0 95.4 jit_solution(6922306741231753530)
XLA Ops:
  0.7 3.0 %collective-permute-start.2 = (bf16[768,384]{1,0:T(8,128)(2,1)}, bf16[768,384]{1,0:T(8,128)(2,1)S(1)}, u32[]{:S(2)}, u32[]{:S(2)}) collective-permute-start(bf16[768,384]{1,0:T(8,128)(2,1)} %w0_hbm.1), channel_id=1, source_target_pairs={{0,2},{1,3},{2,0},{3,1},{4,6},{5,7},{6,4},{7,5},{8,10},{9,11},{10,... | collective-permute-start | bytes 1769480 | tf_op jit(solution)/shard_map/ppermute | solution.py:495
  3.7 1.4 %broadcast_in_dim.2 = bf16[8,2,3072]{2,1,0:T(2,128)(2,1)} broadcast(bf16[2,3072]{1,0:T(2,128)(2,1)} %param.15), dimensions={1,2} | broadcast | bytes 110592 | tf_op jit(solution)/shard_map/broadcast_in_dim | solution.py:489
  5.1 5.8 %all-to-all-start = ((bf16[8,2,3072]{2,1,0:T(2,128)(2,1)}), bf16[8,2,3072]{2,1,0:T(2,128)(2,1)S(1)}, u32[]{:S(2)}, u32[]{:S(2)}) async-start(bf16[8,2,3072]{2,1,0:T(2,128)(2,1)} %broadcast_in_dim.2), calls=%async_computation | async-start | bytes 196608 | tf_op jit(solution)/shard_map/all_to_all | solution.py:473
  10.9 0.9 constant_dynamic-slice_fusion
  11.8 2.1 %collective-permute-start.1 = (bf16[128,384]{1,0:T(8,128)(2,1)S(1)}, bf16[128,384]{1,0:T(8,128)(2,1)S(1)}, u32[]{:S(2)}, u32[]{:S(2)}) collective-permute-start(bf16[128,384]{1,0:T(8,128)(2,1)S(1)} %constant_dynamic-slice_fusion), channel_id=1, source_target_pairs={{0,4},{4,0},{8,12},{12,8},{16,20},{20,16},{24,28},{28,24},{1,5},{5... | collective-permute-start | bytes 294920 | tf_op jit(solution)/shard_map/ppermute | solution.py:494
  13.9 4.1 %all-to-all-done.tokens_ref = bf16[8,2,3072]{2,1,0:T(2,128)(2,1)S(1)} async-done(((bf16[8,2,3072]{2,1,0:T(2,128)(2,1)}), bf16[8,2,3072]{2,1,0:T(2,128)(2,1)S(1)}, u32[]{:S(2)}, u32[]{:S(2)}) %all-to-all-start) | async-done | bytes 98336 | tf_op jit(solution)/shard_map/all_to_all | solution.py:473
  18.0 3.0 %copy-done.1 = bf16[3072,1152]{1,0:T(8,128)(2,1)S(1)} copy-done((bf16[3072,1152]{1,0:T(8,128)(2,1)S(1)}, bf16[3072,1152]{1,0:T(8,128)(2,1)}, u32[]{:S(2)}) %copy-start.1) | copy-done | bytes 7077912
  21.0 1.0 %copy-done.2 = f32[4,8,3072]{2,1,0:T(8,128)S(1)} copy-done((f32[4,8,3072]{2,1,0:T(8,128)S(1)}, f32[4,8,3072]{2,1,0:T(8,128)}, u32[]{:S(2)}) %copy-start.2) | copy-done | bytes 393240
  22.0 0.7 copy-done.10
  22.7 4.9 %shard_map.158 = bf16[32,4,384]{2,1,0:T(4,128)(2,1)} custom-call(s32[4]{0:T(128)S(1)} %copy-done.10, bf16[8,2,3072]{2,1,0:T(2,128)(2,1)S(1)} %all-to-all-done.tokens_ref, f32[4,8,3072]{2,1,0:T(8,128)S(1)} %copy-done.2, bf16[3072,1152]{1,0:T(8,128)(2,1)S(1)} %copy-done.1), custom_call_target="tpu_custom_call" | custom-call | tf_op jit(solution)/shard_map/pallas_call | solution.py:501
  27.6 2.6 %all-to-all-start.1 = ((bf16[32,4,384]{2,1,0:T(4,128)(2,1)}), bf16[32,4,384]{2,1,0:T(4,128)(2,1)S(1)}, u32[]{:S(2)}, u32[]{:S(2)}) async-start(bf16[32,4,384]{2,1,0:T(4,128)(2,1)} %shard_map.158), calls=%async_computation.1 | async-start | bytes 196608 | tf_op jit(solution)/shard_map/all_to_all | solution.py:473
  30.2 0.9 constant_dynamic-slice_fusion.1
  31.1 1.7 %collective-permute-start = (bf16[128,384]{1,0:T(8,128)(2,1)S(1)}, bf16[128,384]{1,0:T(8,128)(2,1)S(1)}, u32[]{:S(2)}, u32[]{:S(2)}) collective-permute-start(bf16[128,384]{1,0:T(8,128)(2,1)S(1)} %constant_dynamic-slice_fusion.1), channel_id=1, source_target_pairs={{0,4},{4,0},{8,12},{12,8},{16,20},{20,16},{24,28},{28,24},{1,5},{5... | collective-permute-start | bytes 294920 | tf_op jit(solution)/shard_map/ppermute | solution.py:493
  32.8 3.8 %collective-permute-done.other_k_hbm = bf16[128,384]{1,0:T(8,128)(2,1)S(1)} collective-permute-done((bf16[128,384]{1,0:T(8,128)(2,1)S(1)}, bf16[128,384]{1,0:T(8,128)(2,1)S(1)}, u32[]{:S(2)}, u32[]{:S(2)}) %collective-permute-start) | collective-permute-done | bytes 98336 | tf_op jit(solution)/shard_map/ppermute | solution.py:493
  36.6 1.4 %all-to-all-done.1 = bf16[32,4,384]{2,1,0:T(4,128)(2,1)S(1)} async-done(((bf16[32,4,384]{2,1,0:T(4,128)(2,1)}), bf16[32,4,384]{2,1,0:T(4,128)(2,1)S(1)}, u32[]{:S(2)}, u32[]{:S(2)}) %all-to-all-start.1) | async-done | bytes 98336 | tf_op jit(solution)/shard_map/all_to_all | solution.py:473
  38.0 0.9 copy-done.5
  38.9 0.9 copy-done.6
  39.8 0.7 copy-done.8
  40.5 0.7 copy-done.12
  42.5 2.7 %shard_map.159 = bf16[32,4,384]{2,1,0:T(4,128)(2,1)} custom-call(s32[2,4]{1,0:T(2,128)S(1)} %bitcast.8, s32[2,4]{1,0:T(2,128)S(1)} %bitcast.11, bf16[8,4,4,384]{3,2,1,0:T(4,128)(2,1)S(1)} %bitcast.7, bf16[128,768]{1,0:T(8,128)(2,1)S(1)} %copy-done.5, bf16[128,768]{1,0:T(8,128)(2,1)S(1)} %copy-done.6, bf16[128,384]{1,0:T(8,128)(2,1)S(1)} %collective-permute-done.other_k_hbm, ...), custom_call_target="tpu_custom_call" | custom-call | tf_op jit(solution)/shard_map/pallas_call | solution.py:511
  45.4 3.9 %all-to-all-start.2 = ((bf16[32,4,384]{2,1,0:T(4,128)(2,1)}), bf16[32,4,384]{2,1,0:T(4,128)(2,1)S(1)}, u32[]{:S(2)}, u32[]{:S(2)}) async-start(bf16[32,4,384]{2,1,0:T(4,128)(2,1)} %shard_map.159), calls=%async_computation.2 | async-start | bytes 196608 | tf_op jit(solution)/shard_map/all_to_all | solution.py:473
  49.2 7.8 %all-to-all-done.2.mixed_ref = bf16[32,4,384]{2,1,0:T(4,128)(2,1)S(1)} async-done(((bf16[32,4,384]{2,1,0:T(4,128)(2,1)}), bf16[32,4,384]{2,1,0:T(4,128)(2,1)S(1)}, u32[]{:S(2)}, u32[]{:S(2)}) %all-to-all-start.2) | async-done | bytes 98336 | tf_op jit(solution)/shard_map/all_to_all | solution.py:473
  57.1 1.8 %shard_map.160 = bf16[8,16,384]{2,1,0:T(8,128)(2,1)S(1)} custom-call(s32[4]{0:T(128)S(1)} %copy-done.11, bf16[32,4,384]{2,1,0:T(4,128)(2,1)S(1)} %all-to-all-done.2.mixed_ref, bf16[8,2,3072]{2,1,0:T(2,128)(2,1)S(1)} %all-to-all-done.tokens_ref, f32[4,8,3072]{2,1,0:T(8,128)S(1)} %copy-done.3, bf16[768,384]{1,0:T(8,128)(2,1)S(1)} %copy-done.4, ...), custom_call_target="tpu_custom_call" | custom-call | tf_op jit(solution)/shard_map/pallas_call | solution.py:525
  58.8 9.5 %all_to_all.25.first_ref = bf16[8,16,384]{2,1,0:T(8,128)(2,1)S(1)} all-to-all(bf16[8,16,384]{2,1,0:T(8,128)(2,1)S(1)} %shard_map.160), channel_id=1, replica_groups=mesh['row'=8,'col'=4] {'row'}, dimensions={0} | all-to-all | bytes 196608 | tf_op jit(solution)/shard_map/all_to_all | solution.py:473
  68.3 3.7 %copy-done = bf16[3072,1536]{1,0:T(8,128)(2,1)S(1)} copy-done((bf16[3072,1536]{1,0:T(8,128)(2,1)S(1)}, bf16[3072,1536]{1,0:T(8,128)(2,1)}, u32[]{:S(2)}) %copy-start) | copy-done | bytes 9437208
  72.0 5.6 %shard_map.161 = f32[8,2,3072]{2,1,0:T(2,128)S(1)} custom-call(s32[4]{0:T(128)S(1)} %copy-done.11, bf16[8,16,384]{2,1,0:T(8,128)(2,1)S(1)} %all_to_all.25.first_ref, f32[4,8,3072]{2,1,0:T(8,128)S(1)} %copy-done.3, bf16[3072,1536]{1,0:T(8,128)(2,1)S(1)} %copy-done, bf16[1536,3072]{1,0:T(8,128)(2,1)} %w2_hbm.1), custom_call_target="tpu_custom_call" | custom-call | tf_op jit(solution)/shard_map/pallas_call | solution.py:540
  77.6 10.2 %all_to_all.26.terms_ref = f32[8,2,3072]{2,1,0:T(2,128)S(1)} all-to-all(f32[8,2,3072]{2,1,0:T(2,128)S(1)} %shard_map.161), channel_id=1, replica_groups=mesh['row'=8,'col'=4] {'row'}, dimensions={0} | all-to-all | bytes 393216 | tf_op jit(solution)/shard_map/all_to_all | solution.py:473
  87.8 1.4 %shard_map.162.masked_ref = f32[2,64]{1,0:T(2,128)S(1)} custom-call(s32[4]{0:T(128)S(1)} %copy-done.11, s32[2,4]{1,0:T(2,128)S(1)} %bitcast.9, f32[8,2,3072]{2,1,0:T(2,128)S(1)} %all_to_all.26.terms_ref, f32[4,8,3072]{2,1,0:T(8,128)S(1)} %copy-done.3, bf16[64,3072]{1,0:T(8,128)(2,1)S(1)} %bitcast.6), custom_call_target="tpu_custom_call" | custom-call | tf_op jit(solution)/shard_map/pallas_call | solution.py:555
  89.2 1.3 %collective-permute-start.6 = (f32[2,64]{1,0:T(2,128)S(1)}, f32[2,64]{1,0:T(2,128)S(1)}, u32[]{:S(2)}, u32[]{:S(2)}) collective-permute-start(f32[2,64]{1,0:T(2,128)S(1)} %shard_map.162.masked_ref), channel_id=1, source_target_pairs={{1,0},{2,1},{3,2},{5,4},{6,5},{7,6},{9,8},{10,9},{11,10},{13,12},{... | collective-permute-start | bytes 1544 | tf_op jit(solution)/shard_map/ppermute | solution.py:564
  90.5 3.0 %collective-permute-start.5 = (f32[2,64]{1,0:T(2,128)S(1)}, f32[2,64]{1,0:T(2,128)S(1)}, u32[]{:S(2)}, u32[]{:S(2)}) collective-permute-start(f32[2,64]{1,0:T(2,128)S(1)} %shard_map.162.masked_ref), channel_id=1, source_target_pairs={{0,1},{1,2},{2,3},{4,5},{5,6},{6,7},{8,9},{9,10},{10,11},{12,13},{... | collective-permute-start | bytes 1544 | tf_op jit(solution)/shard_map/ppermute | solution.py:563
  93.5 0.8 collective-permute-done.5.before_ref
  94.3 1.1 %shard_map.163 = (f32[2,64]{1,0:T(2,128)}, f32[2,64]{1,0:T(2,128)}) custom-call(s32[2,4]{1,0:T(2,128)S(1)} %bitcast.10, f32[2,64]{1,0:T(2,128)S(1)} %shard_map.162.masked_ref, f32[2,64]{1,0:T(2,128)S(1)} %collective-permute-done.5.before_ref, f32[2,64]{1,0:T(2,128)S(1)} %collective-permute-done.6.after_ref, f32[2,64]{1,0:T(2,128)S(1)} %copy-done.13), custom_call_target="tpu_custom_call" | custom-call | tf_op jit(solution)/shard_map/pallas_call | solution.py:566
  (31 shorter events, 1.5 us)
Async XLA Ops:
  0.6 56.4 %copy-start.11 = (s32[4]{0:T(128)S(1)}, s32[4]{0:T(128)}, u32[]{:S(2)}) copy-start(s32[4]{0:T(128)} %step_ref.7) | copy-start | bytes 52
  0.6 56.4 %copy-start.3 = (f32[4,8,3072]{2,1,0:T(8,128)S(1)}, f32[4,8,3072]{2,1,0:T(8,128)}, u32[]{:S(2)}) copy-start(f32[4,8,3072]{2,1,0:T(8,128)} %mod_hbm.7) | copy-start | bytes 1179652
  0.7 44.5 %collective-permute-start.2 = (bf16[768,384]{1,0:T(8,128)(2,1)}, bf16[768,384]{1,0:T(8,128)(2,1)S(1)}, u32[]{:S(2)}, u32[]{:S(2)}) collective-permute-start(bf16[768,384]{1,0:T(8,128)(2,1)} %w0_hbm.1), channel_id=1, source_target_pairs={{0,2},{1,3},{2,0},{3,1},{4,6},{5,7},{6,4},{7,5},{8,10},{9,11},{10,... | collective-permute-start | bytes 1769480 | tf_op jit(solution)/shard_map/ppermute | solution.py:495
  5.1 13.0 %all-to-all-start = ((bf16[8,2,3072]{2,1,0:T(2,128)(2,1)}), bf16[8,2,3072]{2,1,0:T(2,128)(2,1)S(1)}, u32[]{:S(2)}, u32[]{:S(2)}) async-start(bf16[8,2,3072]{2,1,0:T(2,128)(2,1)} %broadcast_in_dim.2), calls=%async_computation | async-start | bytes 196608 | tf_op jit(solution)/shard_map/all_to_all | solution.py:473
  11.8 21.0 %collective-permute-start.1 = (bf16[128,384]{1,0:T(8,128)(2,1)S(1)}, bf16[128,384]{1,0:T(8,128)(2,1)S(1)}, u32[]{:S(2)}, u32[]{:S(2)}) collective-permute-start(bf16[128,384]{1,0:T(8,128)(2,1)S(1)} %constant_dynamic-slice_fusion), channel_id=1, source_target_pairs={{0,4},{4,0},{8,12},{12,8},{16,20},{20,16},{24,28},{28,24},{1,5},{5... | collective-permute-start | bytes 294920 | tf_op jit(solution)/shard_map/ppermute | solution.py:494
  18.0 3.0 %copy-start.1 = (bf16[3072,1152]{1,0:T(8,128)(2,1)S(1)}, bf16[3072,1152]{1,0:T(8,128)(2,1)}, u32[]{:S(2)}) copy-start(bf16[3072,1152]{1,0:T(8,128)(2,1)} %w_hbm.1) | copy-start | bytes 21233668
  21.0 1.0 %copy-start.2 = (f32[4,8,3072]{2,1,0:T(8,128)S(1)}, f32[4,8,3072]{2,1,0:T(8,128)}, u32[]{:S(2)}) copy-start(f32[4,8,3072]{2,1,0:T(8,128)} %mod_hbm.7) | copy-start | bytes 1179652
  22.0 0.7 copy-start.10
  22.7 34.4 %copy-start.4 = (bf16[768,384]{1,0:T(8,128)(2,1)S(1)}, bf16[768,384]{1,0:T(8,128)(2,1)}, u32[]{:S(2)}) copy-start(bf16[768,384]{1,0:T(8,128)(2,1)} %w0_hbm.1) | copy-start | bytes 1769476
  27.6 10.4 %all-to-all-start.1 = ((bf16[32,4,384]{2,1,0:T(4,128)(2,1)}), bf16[32,4,384]{2,1,0:T(4,128)(2,1)S(1)}, u32[]{:S(2)}, u32[]{:S(2)}) async-start(bf16[32,4,384]{2,1,0:T(4,128)(2,1)} %shard_map.158), calls=%async_computation.1 | async-start | bytes 196608 | tf_op jit(solution)/shard_map/all_to_all | solution.py:473
  31.1 5.5 %collective-permute-start = (bf16[128,384]{1,0:T(8,128)(2,1)S(1)}, bf16[128,384]{1,0:T(8,128)(2,1)S(1)}, u32[]{:S(2)}, u32[]{:S(2)}) collective-permute-start(bf16[128,384]{1,0:T(8,128)(2,1)S(1)} %constant_dynamic-slice_fusion.1), channel_id=1, source_target_pairs={{0,4},{4,0},{8,12},{12,8},{16,20},{20,16},{24,28},{28,24},{1,5},{5... | collective-permute-start | bytes 294920 | tf_op jit(solution)/shard_map/ppermute | solution.py:493
  32.8 16.4 %collective-permute-start.3 = (bf16[768,384]{1,0:T(8,128)(2,1)}, bf16[768,384]{1,0:T(8,128)(2,1)S(1)}, u32[]{:S(2)}, u32[]{:S(2)}) collective-permute-start(bf16[768,384]{1,0:T(8,128)(2,1)} %w0_hbm.1), channel_id=1, source_target_pairs={{0,1},{1,0},{2,3},{3,2},{4,5},{5,4},{6,7},{7,6},{8,9},{9,8},{10,11... | collective-permute-start | bytes 1769480 | tf_op jit(solution)/shard_map/ppermute | solution.py:497
  38.0 0.9 copy-start.5
  38.9 0.9 copy-start.6
  39.8 0.7 copy-start.8
  40.5 0.7 copy-start.12
  41.2 0.7 copy-start.14
  41.9 0.7 copy-start.15
  45.2 11.9 %collective-permute-start.4 = (bf16[768,384]{1,0:T(8,128)(2,1)S(1)}, bf16[768,384]{1,0:T(8,128)(2,1)S(1)}, u32[]{:S(2)}, u32[]{:S(2)}) collective-permute-start(bf16[768,384]{1,0:T(8,128)(2,1)S(1)} %collective-permute-done.2.w2_hbm), channel_id=1, source_target_pairs={{0,1},{1,0},{2,3},{3,2},{4,5},{5,4},{6,7},{7,6},{8,9},{9,8},{10,11... | collective-permute-start | bytes 1769480 | tf_op jit(solution)/shard_map/ppermute | solution.py:523
  45.4 11.7 %all-to-all-start.2 = ((bf16[32,4,384]{2,1,0:T(4,128)(2,1)}), bf16[32,4,384]{2,1,0:T(4,128)(2,1)S(1)}, u32[]{:S(2)}, u32[]{:S(2)}) async-start(bf16[32,4,384]{2,1,0:T(4,128)(2,1)} %shard_map.159), calls=%async_computation.2 | async-start | bytes 196608 | tf_op jit(solution)/shard_map/all_to_all | solution.py:473
  68.3 3.7 %copy-start = (bf16[3072,1536]{1,0:T(8,128)(2,1)S(1)}, bf16[3072,1536]{1,0:T(8,128)(2,1)}, u32[]{:S(2)}) copy-start(bf16[3072,1536]{1,0:T(8,128)(2,1)} %w1_hbm.1) | copy-start | bytes 28311556
  72.0 15.8 %copy-start.7 = (bf16[3072,64]{0,1:T(8,128)(2,1)S(1)}, bf16[3072,64]{0,1:T(8,128)(2,1)}, u32[]{:S(2)}) copy-start(bf16[3072,64]{0,1:T(8,128)(2,1)} %param.29) | copy-start | bytes 1179652
  72.0 15.8 %copy-start.9 = (s32[4,2]{0,1:T(2,128)S(1)}, s32[4,2]{0,1:T(2,128)}, u32[]{:S(2)}) copy-start(s32[4,2]{0,1:T(2,128)} %param.21) | copy-start | bytes 100
  72.0 22.3 %copy-start.13 = (f32[2,64]{1,0:T(2,128)S(1)}, f32[2,64]{1,0:T(2,128)}, u32[]{:S(2)}) copy-start(f32[2,64]{1,0:T(2,128)} %latent_ref.1) | copy-start | bytes 1540
  89.2 4.3 %collective-permute-start.6 = (f32[2,64]{1,0:T(2,128)S(1)}, f32[2,64]{1,0:T(2,128)S(1)}, u32[]{:S(2)}, u32[]{:S(2)}) collective-permute-start(f32[2,64]{1,0:T(2,128)S(1)} %shard_map.162.masked_ref), channel_id=1, source_target_pairs={{1,0},{2,1},{3,2},{5,4},{6,5},{7,6},{9,8},{10,9},{11,10},{13,12},{... | collective-permute-start | bytes 1544 | tf_op jit(solution)/shard_map/ppermute | solution.py:564
  90.5 3.8 %collective-permute-start.5 = (f32[2,64]{1,0:T(2,128)S(1)}, f32[2,64]{1,0:T(2,128)S(1)}, u32[]{:S(2)}, u32[]{:S(2)}) collective-permute-start(f32[2,64]{1,0:T(2,128)S(1)} %shard_map.162.masked_ref), channel_id=1, source_target_pairs={{0,1},{1,2},{2,3},{4,5},{5,6},{6,7},{8,9},{9,10},{10,11},{12,13},{... | collective-permute-start | bytes 1544 | tf_op jit(solution)/shard_map/ppermute | solution.py:563

commit v2 on v1

--- a/solution.py
+++ b/solution.py
@@ -257,16 +257,19 @@
     return whole
 
 
-def qkv_kernel(step_ref, tokens_ref, mod_hbm, w_hbm, out_ref, order_ref, mod_ref, w_ref, sems):
+def qkv_kernel(step_hbm, tokens_ref, mod_hbm, w_hbm, out_ref, step_ref, order_ref, mod_ref, w_ref, sems):
     row = lax.axis_index("row")
     depth = order_ref.shape[1]
     size = out_ref.shape[2]
-    mod_copy, *w_copies = start_copies([(mod_hbm, mod_ref)] + row_chunks(w_hbm, w_ref, QKV_CHUNKS), sems)
+    step_copy, mod_copy, *w_copies = start_copies(
+        [(step_hbm, step_ref), (mod_hbm, mod_ref)] + row_chunks(w_hbm, w_ref, QKV_CHUNKS), sems
+    )
     for q in range(REQ):
         for g in range(2):
             order_ref[4 * q + 2 * g : 4 * q + 2 * g + 2, :] = tokens_ref[REQ * g + q].astype(f32)
     out_ref[...] = jnp.zeros_like(out_ref)
     normed = norm_rows(order_ref[...])
+    step_copy.wait()
     mod_copy.wait()
     shift = per_request(mod_ref, step_ref, 0, 4, 0, depth)
     scale = per_request(mod_ref, step_ref, 1, 4, 0, depth)
@@ -280,8 +283,8 @@
 
 
 def attention_kernel(
-    size_ref, offset_ref, rows_ref, own_k_hbm, own_v_hbm, other_k_hbm, other_v_hbm, q_gain_ref, k_gain_ref, out_ref,
-    q_ref, k_ref, v_ref, text_k_ref, text_v_ref, sems,
+    size_hbm, offset_hbm, rows_ref, own_k_hbm, own_v_hbm, other_k_hbm, other_v_hbm, q_gain_hbm, k_gain_hbm, out_ref,
+    size_ref, offset_ref, q_gain_ref, k_gain_ref, q_ref, k_ref, v_ref, text_k_ref, text_v_ref, sems,
 ):
     row = lax.axis_index("row")
     col = lax.axis_index("col")
@@ -289,15 +292,19 @@
     side = lax.rem(row, 2)
     group = 2 * col + side
     width = q_ref.shape[1]
-    head = q_gain_ref.shape[1]
+    head = q_gain_hbm.shape[1]
     heads = width // head
     count = q_ref.shape[0]
     half_rows = own_k_hbm.shape[0]
     own = pl.ds(pl.multiple_of(side * width, width), width)
     top_rows = pl.ds(0, half_rows)
     low_rows = pl.ds(half_rows, half_rows)
-    copies = start_copies(
+    *small, copy_k0, copy_k1, copy_v0, copy_v1 = start_copies(
         [
+            (offset_hbm, offset_ref),
+            (size_hbm, size_ref),
+            (q_gain_hbm, q_gain_ref),
+            (k_gain_hbm, k_gain_ref),
             (own_k_hbm.at[:, own], text_k_ref.at[top_rows, :]),
             (other_k_hbm, text_k_ref.at[low_rows, :]),
             (own_v_hbm.at[:, own], text_v_ref.at[top_rows, :]),
@@ -309,6 +316,8 @@
         source = (8 * which + group) // 3
         for s in range(4):
             ref[4 * s : 4 * s + 4, :] = rows_ref[source, s].astype(f32)
+    for copy in small:
+        copy.wait()
     token = lax.broadcasted_iota(jnp.int32, (count, 1), 0)
     pos_h = lax.rem(token, 4) // 2
     pos_w = (token // 4) * 2 + lax.rem(token, 2)
@@ -338,7 +347,7 @@
     scale = head ** (-0.5)
     queries = [turned(q_ref[:, h * head : (h + 1) * head], q_gain_ref[...]) for h in range(heads)]
     keys = [turned(k_ref[:, h * head : (h + 1) * head], k_gain_ref[...]) for h in range(heads)]
-    for copy in copies:
+    for copy in (copy_k0, copy_k1, copy_v0, copy_v1):
         copy.wait()
     for h in range(heads):
         cols = slice(h * head, (h + 1) * head)
@@ -360,16 +369,16 @@
 
 
 def out_kernel(
-    step_ref, mixed_ref, tokens_ref, mod_hbm, w0_hbm, w1_hbm, w2_hbm, w3_hbm, out_ref, rows_ref, states_ref, mod_ref,
-    w_ref, sems,
+    step_hbm, mixed_ref, tokens_ref, mod_hbm, w0_hbm, w1_hbm, w2_hbm, w3_hbm, out_ref, step_ref, rows_ref, states_ref,
+    mod_ref, w_ref, sems,
 ):
     row = lax.axis_index("row")
     col = lax.axis_index("col")
     depth, width = w0_hbm.shape
     piece = mixed_ref.shape[2]
     start = pl.multiple_of(row * width, width)
-    mod_copy, *w_copies = start_copies(
-        [(mod_hbm, mod_ref)]
+    step_copy, mod_copy, *w_copies = start_copies(
+        [(step_hbm, step_ref), (mod_hbm, mod_ref)]
         + [
             (w_hbm, w_ref.at[pl.ds(pl.multiple_of(jnp.bitwise_xor(col, d) * depth, depth), depth), :])
             for d, w_hbm in enumerate((w0_hbm, w1_hbm, w2_hbm, w3_hbm))
@@ -384,6 +393,7 @@
         for g in range(2):
             states_ref[4 * q + 2 * g : 4 * q + 2 * g + 2, :] = tokens_ref[REQ * g + q, :, pl.ds(start, width)].astype(f32)
     mixed = rows_ref[...].astype(bf16)
+    step_copy.wait()
     mod_copy.wait()
     gate = per_request(mod_ref, step_ref, 2, 4, start, width)
     for copy in w_copies:
@@ -395,17 +405,21 @@
 
 
 def mlp_kernel(
-    step_ref, first_ref, mod_hbm, w1_hbm, w2_hbm, out_ref, rows_ref, mod_ref, w1_ref, w2_ref, sems
+    step_hbm, first_ref, mod_hbm, w1_hbm, w2_hbm, out_ref, step_ref, rows_ref, mod_ref, w1_ref, w2_ref, sems
 ):
     row = lax.axis_index("row")
     depth = rows_ref.shape[1]
     piece = first_ref.shape[2]
-    mod_copy, *w_copies = start_copies(
-        [(mod_hbm, mod_ref)] + row_chunks(w1_hbm, w1_ref, FC_CHUNKS) + row_chunks(w2_hbm, w2_ref, FC_CHUNKS), sems
+    step_copy, mod_copy, *w_copies = start_copies(
+        [(step_hbm, step_ref), (mod_hbm, mod_ref)]
+        + row_chunks(w1_hbm, w1_ref, FC_CHUNKS)
+        + row_chunks(w2_hbm, w2_ref, FC_CHUNKS),
+        sems,
     )
     for r in range(8):
         rows_ref[:, r * piece : (r + 1) * piece] = first_ref[r].astype(f32)
     normed = norm_rows(rows_ref[...])
+    step_copy.wait()
     mod_copy.wait()
     shift = per_request(mod_ref, step_ref, 3, 4, 0, depth)
     scale = per_request(mod_ref, step_ref, 4, 4, 0, depth)
@@ -420,18 +434,22 @@
             out_ref[REQ * g + q] = term[4 * q + 2 * g : 4 * q + 2 * g + 2, :]
 
 
-def final_kernel(step_ref, size_ref, terms_ref, mod_hbm, w_hbm, out_ref, mod_ref, w_ref, sems):
+def final_kernel(step_hbm, size_hbm, terms_ref, mod_hbm, w_hbm, out_ref, step_ref, size_ref, mod_ref, w_ref, sems):
     row = lax.axis_index("row")
     col = lax.axis_index("col")
     req = lax.rem(row, REQ)
-    step = step_ref[req]
-    mod_copy, w_copy = start_copies([(mod_hbm.at[step], mod_ref), (w_hbm, w_ref)], sems)
+    step_copy, size_copy, mod_copy, w_copy = start_copies(
+        [(step_hbm, step_ref), (size_hbm, size_ref), (mod_hbm, mod_ref), (w_hbm, w_ref)], sems
+    )
     second = terms_ref[0]
     for r in range(1, 8):
         second = second + terms_ref[r]
     normed = norm_rows(second)
+    step_copy.wait()
     mod_copy.wait()
-    normed = (normed * (1.0 + mod_ref[7:8, :]) + mod_ref[6:7, :]).astype(bf16)
+    step = step_ref[req]
+    normed = (normed * (1.0 + mod_ref[step, 7:8, :]) + mod_ref[step, 6:7, :]).astype(bf16)
+    size_copy.wait()
     w_copy.wait()
     raw = lax.dot_general(normed, w_ref[...], (((1,), (1,)), ((), ())), preferred_element_type=f32)
     out_ref[...] = jnp.where(live_rows(size_ref, row, col, raw.shape), raw, 0.0)
@@ -443,14 +461,21 @@
     return (row // REQ < size_ref[0, req]) & (grid_col < size_ref[1, req])
 
 
-def blend_kernel(size_ref, masked_ref, before_ref, after_ref, latent_ref, velocity_ref, next_ref):
+def blend_kernel(size_hbm, masked_ref, near_ref, far_ref, latent_hbm, velocity_ref, next_ref, size_ref, latent_ref, sems):
+    col = lax.axis_index("col")
+    size_copy, latent_copy = start_copies([(size_hbm, size_ref), (latent_hbm, latent_ref)], sems)
     masked = masked_ref[...]
+    near = near_ref[...]
+    far = jnp.where((col == 1) | (col == 2), far_ref[...], 0.0)
+    odd = lax.rem(col, 2) == 1
     count = masked.shape[0]
-    left = jnp.concatenate([before_ref[count - 1 :, :], masked[: count - 1, :]], 0)
-    right = jnp.concatenate([masked[1:, :], after_ref[:1, :]], 0)
-    live = live_rows(size_ref, lax.axis_index("row"), lax.axis_index("col"), masked.shape)
+    left = jnp.concatenate([jnp.where(odd, near, far)[count - 1 :, :], masked[: count - 1, :]], 0)
+    right = jnp.concatenate([masked[1:, :], jnp.where(odd, far, near)[:1, :]], 0)
+    size_copy.wait()
+    live = live_rows(size_ref, lax.axis_index("row"), col, masked.shape)
     velocity = jnp.where(live, masked + blend * (left + right - 2.0 * masked), 0.0)
     velocity_ref[...] = velocity
+    latent_copy.wait()
     next_ref[...] = latent_ref[...] + -1.0 / STEPS * velocity
 
 
@@ -480,6 +505,7 @@
     rows = lax.axis_size("row")
     cols = lax.axis_size("col")
     row = lax.axis_index("row")
+    stay = lambda values: pltpu.with_memory_space_constraint(values, pltpu.HBM)
     tile_w, width = image_states.shape
     head = q_gain.shape[0]
     piece = width // 8
@@ -492,32 +518,39 @@
     swap = [(i, i ^ 1) for i in range(rows)]
     other_k = lax.ppermute(lax.dynamic_slice_in_dim(text_keys, give, piece, 1), "row", swap)
     other_v = lax.ppermute(lax.dynamic_slice_in_dim(text_values, give, piece, 1), "row", swap)
+    gathered, other_k, other_v = lax.optimization_barrier((gathered, other_k, other_v))
     w_x = lax.ppermute(w_out, "col", [(i, i ^ 2) for i in range(cols)])
     near = [(i, i ^ 1) for i in range(cols)]
     w_k = lax.ppermute(w_out, "col", near)
 
     sems = lambda count: pltpu.SemaphoreType.DMA((count,))
     mod_space = pltpu.VMEM(mod_table.shape, f32)
+    steps_space = pltpu.SMEM(timestep.shape, jnp.int32)
+    sizes_space = pltpu.SMEM(grid_size.shape[::-1], jnp.int32)
+    gain_space = pltpu.VMEM((1, head), f32)
+    steps = stay(timestep)
+    sizes = stay(grid_size.T)
+    mods = stay(mod_table)
     pieces = call(
         qkv_kernel,
         (rows * cols, 4, piece),
         bf16,
-        [SMEM_SPEC, VMEM_SPEC, HBM_SPEC, HBM_SPEC],
-        [pltpu.VMEM((tokens, width), f32), mod_space, pltpu.VMEM(w_qkv.shape, bf16), sems(QKV_CHUNKS + 1)],
+        [HBM_SPEC, VMEM_SPEC, HBM_SPEC, HBM_SPEC],
+        [steps_space, pltpu.VMEM((tokens, width), f32), mod_space, pltpu.VMEM(w_qkv.shape, bf16), sems(QKV_CHUNKS + 2)],
         limit=16 << 20,
-    )(timestep, gathered, mod_table, w_qkv)
+    )(steps, gathered, mods, stay(w_qkv))
     got = exchange(pieces, both).reshape(rows, cols, 4, piece)
     text_space = pltpu.VMEM((2 * text_keys.shape[0], piece), bf16)
     mixed = call(
         attention_kernel,
         (rows * cols, 4, piece),
         bf16,
-        [SMEM_SPEC, SMEM_SPEC, VMEM_SPEC] + [HBM_SPEC] * 4 + [VMEM_SPEC] * 2,
-        [pltpu.VMEM((tokens, piece), f32)] * 3 + [text_space] * 2 + [sems(4)],
+        [HBM_SPEC, HBM_SPEC, VMEM_SPEC] + [HBM_SPEC] * 6,
+        [sizes_space] * 2 + [gain_space] * 2 + [pltpu.VMEM((tokens, piece), f32)] * 3 + [text_space] * 2 + [sems(8)],
         limit=8 << 20,
     )(
-        grid_size.T, rope_offset.T, got, text_keys, text_values, other_k, other_v,
-        q_gain.reshape(1, head), k_gain.reshape(1, head),
+        sizes, stay(rope_offset.T), got, stay(text_keys), stay(text_values), other_k, other_v,
+        stay(q_gain.reshape(1, head)), stay(k_gain.reshape(1, head)),
     )
     mixed, w_x = lax.optimization_barrier((mixed, w_x))
     w_xk = lax.ppermute(w_x, "col", near)
@@ -526,50 +559,53 @@
         out_kernel,
         (rows, tokens, piece),
         bf16,
-        [SMEM_SPEC, VMEM_SPEC, VMEM_SPEC] + [HBM_SPEC] * 5,
+        [HBM_SPEC, VMEM_SPEC, VMEM_SPEC] + [HBM_SPEC] * 5,
         [
+            steps_space,
             pltpu.VMEM((tokens, width), f32),
             pltpu.VMEM((tokens, piece), f32),
             mod_space,
             pltpu.VMEM((width, piece), bf16),
-            sems(5),
+            sems(6),
         ],
         limit=16 << 20,
-    )(timestep, all_mixed, gathered, mod_table, w_out, w_k, w_x, w_xk)
+    )(steps, all_mixed, gathered, mods, stay(w_out), w_k, w_x, w_xk)
     all_first = exchange(first, "row")
     terms = call(
         mlp_kernel,
         (rows, tile_w, width),
         f32,
-        [SMEM_SPEC, VMEM_SPEC] + [HBM_SPEC] * 3,
+        [HBM_SPEC, VMEM_SPEC] + [HBM_SPEC] * 3,
         [
+            steps_space,
             pltpu.VMEM((tokens, width), f32),
             mod_space,
             pltpu.VMEM(w_fc1.shape, bf16),
             pltpu.VMEM(w_fc2.shape, bf16),
-            sems(2 * FC_CHUNKS + 1),
+            sems(2 * FC_CHUNKS + 2),
         ],
         limit=40 << 20,
-    )(timestep, all_first, mod_table, w_fc1, w_fc2)
+    )(steps, all_first, mods, stay(w_fc1), stay(w_fc2))
     all_terms = exchange(terms, "row")
     masked = call(
         final_kernel,
         (tile_w, w_final.shape[1]),
         f32,
-        [SMEM_SPEC, SMEM_SPEC, VMEM_SPEC, HBM_SPEC, HBM_SPEC],
-        [pltpu.VMEM(mod_table.shape[1:], f32), pltpu.VMEM(w_final.shape[::-1], bf16), sems(2)],
+        [HBM_SPEC, HBM_SPEC, VMEM_SPEC, HBM_SPEC, HBM_SPEC],
+        [steps_space, sizes_space, mod_space, pltpu.VMEM(w_final.shape[::-1], bf16), sems(4)],
         limit=8 << 20,
-    )(timestep, grid_size.T, all_terms, mod_table, w_final.T)
-    before = lax.ppermute(masked, "col", [(i, i + 1) for i in range(cols - 1)])
-    after = lax.ppermute(masked, "col", [(i + 1, i) for i in range(cols - 1)])
+    )(steps, sizes, all_terms, mods, stay(w_final.T))
+    beside = lax.ppermute(masked, "col", near)
+    across = lax.ppermute(masked, "col", [(i, i ^ 3) for i in range(cols)])
     result = jax.ShapeDtypeStruct(latent.shape, f32)
     return pl.pallas_call(
         blend_kernel,
         out_shape=(result, result),
-        in_specs=[SMEM_SPEC] + [VMEM_SPEC] * 4,
+        in_specs=[HBM_SPEC] + [VMEM_SPEC] * 3 + [HBM_SPEC],
         out_specs=(VMEM_SPEC, VMEM_SPEC),
+        scratch_shapes=[sizes_space, pltpu.VMEM(latent.shape, f32), sems(2)],
         compiler_params=pltpu.CompilerParams(vmem_limit_bytes=8 << 20),
-    )(grid_size.T, masked, before, after, latent)
+    )(sizes, masked, beside, across, stay(latent))
 
 
 def solution(mesh):

time: 96.2 us -> 83 us (0.86)
  local copies, waits for them, and re-layouts: 16.1 us -> 3.2 us
  starting transfers between devices: 23.6 us -> 18.3 us
  waiting for transfers between devices: 17.9 us -> 22.3 us
    unnamed x32 -> x0, local copies, waits for them, and re-layouts: 12.9 us -> none
    ppermute x2, starting transfers between devices: 4.32 us -> 0.64 us  [the longest x1 0.57 us: compact_on_device(): beside = lax.ppermute(masked, 'col', near)]
    ppermute x1, waiting for transfers between devices: 0.01 us -> 2.48 us  [compact_on_device(): lax.ppermute(lax.dynamic_slice_in_dim(text_values, give, piece, 1), 'row'...]
    all_to_all x3, waiting for transfers between devices: 13.3 us -> 15.3 us  [exchange(): return lax.all_to_all(values, axes, split_axis=0, concat_axis=0, tiled=True)]
    ppermute x1, waiting for transfers between devices: 3.81 us -> 2.11 us  [compact_on_device(): lax.ppermute(lax.dynamic_slice_in_dim(text_keys, give, piece, 1), 'row',...]
    ppermute x1, starting transfers between devices: 1.72 us -> 0.09 us  [compact_on_device(): lax.ppermute(lax.dynamic_slice_in_dim(text_keys, give, piece, 1), 'row',...]
    ppermute x2, waiting for transfers between devices: 0.79 us -> 2.41 us  [the longest x1 2.41 us: compact_on_device(): across = lax.ppermute(masked, 'col', [(i, i ^ 3) for i in range(cols)])]
  transfers between devices with their start and end apart: 10 -> 10, of which waited for: 5 -> 5; matrix products, arithmetic and copies ran while one was open for 3% -> 4% of each run, Pallas kernels for 8% -> 8%
where the time goes in v2:
time: 83 us; the launch traced here: 82.4 us
  waiting for transfers between devices  22.3 us (27%)
  blocking collectives  19.7 us (24%)
  starting transfers between devices  18.3 us (22%)
  Pallas kernels  18.1 us (22%)
  local copies, waits for them, and re-layouts  3.2 us (4%)
    all_to_all x2, blocking collectives, exchange(): return lax.all_to_all(values, axes, split_axis=0, concat_axis=0, tiled=True)  19.7 us
    all_to_all x3, waiting for transfers between devices, exchange(): return lax.all_to_all(values, axes, split_axis=0, concat_axis=0, tiled=True)  15.3 us
    all_to_all x3, starting transfers between devices, exchange(): return lax.all_to_all(values, axes, split_axis=0, concat_axis=0, tiled=True)  12 us
    pallas_call x1, Pallas kernels, compact_on_device(): call(mlp_kernel, (rows, tile_w, width), f32, [HBM_SPEC, VMEM_SPEC] + [HBM...  7 us
    pallas_call x1, Pallas kernels, compact_on_device(): call(qkv_kernel, (rows * cols, 4, piece), bf16, [HBM_SPEC, VMEM_SPEC, HBM...  4.17 us
    ppermute x1, starting transfers between devices, compact_on_device(): w_x = lax.ppermute(w_out, 'col', [(i, i ^ 2) for i in range(cols)])  3 us
    pallas_call x1, Pallas kernels, compact_on_device(): call(attention_kernel, (rows * cols, 4, piece), bf16, [HBM_SPEC, HBM_SPEC...  2.62 us
    ppermute x1, waiting for transfers between devices, compact_on_device(): lax.ppermute(lax.dynamic_slice_in_dim(text_values, give, piece, 1), 'row'...  2.48 us
  transfers between devices with their start and end apart: 10, of which 5 were waited for; matrix products, arithmetic and copies ran while one was open for 4% of the time, Pallas kernels for 8%

profile of v2, /device:TPU:0, one launch (start us, length us, event | category | flops | bytes accessed | tf_op | source)
XLA Modules:
  0.0 82.4 jit_solution(16552600930606140442)
XLA Ops:
  0.6 3.0 %collective-permute-start.2 = (bf16[768,384]{1,0:T(8,128)(2,1)}, bf16[768,384]{1,0:T(8,128)(2,1)S(1)}, u32[]{:S(2)}, u32[]{:S(2)}) collective-permute-start(bf16[768,384]{1,0:T(8,128)(2,1)} %w0_hbm.1), channel_id=1, source_target_pairs={{0,2},{1,3},{2,0},{3,1},{4,6},{5,7},{6,4},{7,5},{8,10},{9,11},{10,... | collective-permute-start | bytes 1769480 | tf_op jit(solution)/shard_map/ppermute | solution.py:522
  3.6 1.4 %broadcast_in_dim.2 = bf16[8,2,3072]{2,1,0:T(2,128)(2,1)} broadcast(bf16[2,3072]{1,0:T(2,128)(2,1)} %param.15), dimensions={1,2} | broadcast | bytes 110592 | tf_op jit(solution)/shard_map/broadcast_in_dim | solution.py:515
  5.0 5.8 %all-to-all-start = ((bf16[8,2,3072]{2,1,0:T(2,128)(2,1)}), bf16[8,2,3072]{2,1,0:T(2,128)(2,1)S(1)}, u32[]{:S(2)}, u32[]{:S(2)}) async-start(bf16[8,2,3072]{2,1,0:T(2,128)(2,1)} %broadcast_in_dim.2), calls=%async_computation | async-start | bytes 196608 | tf_op jit(solution)/shard_map/all_to_all | solution.py:498
  10.9 0.9 %constant_dynamic-slice_fusion = bf16[128,384]{1,0:T(8,128)(2,1)S(1)} fusion(bf16[128,768]{1,0:T(8,128)(2,1)} %own_v_hbm.1, s32[]{:T(128)S(6)} %select_n.12), kind=kLoop, calls=%fused_computation | loop fusion | bytes 196612 | tf_op jit(solution)/shard_map/dynamic_slice | solution.py:520
  11.8 2.1 %collective-permute-start.1 = (bf16[128,384]{1,0:T(8,128)(2,1)S(1)}, bf16[128,384]{1,0:T(8,128)(2,1)S(1)}, u32[]{:S(2)}, u32[]{:S(2)}) collective-permute-start(bf16[128,384]{1,0:T(8,128)(2,1)S(1)} %constant_dynamic-slice_fusion), channel_id=1, source_target_pairs={{0,4},{4,0},{8,12},{12,8},{16,20},{20,16},{24,28},{28,24},{1,5},{5... | collective-permute-start | bytes 294920 | tf_op jit(solution)/shard_map/ppermute | solution.py:520
  13.9 0.9 %constant_dynamic-slice_fusion.1 = bf16[128,384]{1,0:T(8,128)(2,1)S(1)} fusion(bf16[128,768]{1,0:T(8,128)(2,1)} %own_k_hbm.1, s32[]{:T(128)S(6)} %select_n.12), kind=kLoop, calls=%fused_computation.1 | loop fusion | bytes 196612 | tf_op jit(solution)/shard_map/dynamic_slice | solution.py:519
  14.8 0.1 collective-permute-start
  14.8 2.5 %collective-permute-done.1.other_v_hbm = bf16[128,384]{1,0:T(8,128)(2,1)S(1)} collective-permute-done((bf16[128,384]{1,0:T(8,128)(2,1)S(1)}, bf16[128,384]{1,0:T(8,128)(2,1)S(1)}, u32[]{:S(2)}, u32[]{:S(2)}) %collective-permute-start.1) | collective-permute-done | bytes 98336 | tf_op jit(solution)/shard_map/ppermute | solution.py:520
  17.3 2.1 %collective-permute-done.other_k_hbm = bf16[128,384]{1,0:T(8,128)(2,1)S(1)} collective-permute-done((bf16[128,384]{1,0:T(8,128)(2,1)S(1)}, bf16[128,384]{1,0:T(8,128)(2,1)S(1)}, u32[]{:S(2)}, u32[]{:S(2)}) %collective-permute-start) | collective-permute-done | bytes 98336 | tf_op jit(solution)/shard_map/ppermute | solution.py:519
  19.4 0.0 all-to-all-done.tokens_ref
  19.4 4.2 %shard_map.158 = bf16[32,4,384]{2,1,0:T(4,128)(2,1)} custom-call(s32[4]{0:T(128)} %step_hbm.7, bf16[8,2,3072]{2,1,0:T(2,128)(2,1)S(1)} %all-to-all-done.tokens_ref, f32[4,8,3072]{2,1,0:T(8,128)} %mod_hbm.7, bf16[3072,1152]{1,0:T(8,128)(2,1)} %w_hbm.1), custom_call_target="tpu_custom_call" | custom-call | tf_op jit(solution)/shard_map/pallas_call | solution.py:534
  23.6 3.6 %all-to-all-start.1 = ((bf16[32,4,384]{2,1,0:T(4,128)(2,1)}), bf16[32,4,384]{2,1,0:T(4,128)(2,1)S(1)}, u32[]{:S(2)}, u32[]{:S(2)}) async-start(bf16[32,4,384]{2,1,0:T(4,128)(2,1)} %shard_map.158), calls=%async_computation.1 | async-start | bytes 196608 | tf_op jit(solution)/shard_map/all_to_all | solution.py:498
  27.3 0.3 collective-permute-start.3
  27.6 7.5 %all-to-all-done.1 = bf16[32,4,384]{2,1,0:T(4,128)(2,1)S(1)} async-done(((bf16[32,4,384]{2,1,0:T(4,128)(2,1)}), bf16[32,4,384]{2,1,0:T(4,128)(2,1)S(1)}, u32[]{:S(2)}, u32[]{:S(2)}) %all-to-all-start.1) | async-done | bytes 98336 | tf_op jit(solution)/shard_map/all_to_all | solution.py:498
  35.1 2.6 %shard_map.159 = bf16[32,4,384]{2,1,0:T(4,128)(2,1)} custom-call(s32[2,4]{1,0:T(2,128)} %bitcast.8, s32[2,4]{1,0:T(2,128)} %bitcast.11, bf16[8,4,4,384]{3,2,1,0:T(4,128)(2,1)S(1)} %bitcast.6, bf16[128,768]{1,0:T(8,128)(2,1)} %own_k_hbm.1, bf16[128,768]{1,0:T(8,128)(2,1)} %own_v_hbm.1, bf16[128,384]{1,0:T(8,128)(2,1)S(1)} %collective-permute-done.other_k_hbm, ...), custom_call_target="tpu_custom_call" | custom-call | tf_op jit(solution)/shard_map/pallas_call | solution.py:544
  37.7 0.0 collective-permute-done.2.w2_hbm
  37.7 0.2 collective-permute-start.4
  37.9 2.6 %all-to-all-start.2 = ((bf16[32,4,384]{2,1,0:T(4,128)(2,1)}), bf16[32,4,384]{2,1,0:T(4,128)(2,1)S(1)}, u32[]{:S(2)}, u32[]{:S(2)}) async-start(bf16[32,4,384]{2,1,0:T(4,128)(2,1)} %shard_map.159), calls=%async_computation.2 | async-start | bytes 196608 | tf_op jit(solution)/shard_map/all_to_all | solution.py:498
  40.5 0.0 collective-permute-done.3.w1_hbm
  40.5 7.8 %all-to-all-done.2.mixed_ref = bf16[32,4,384]{2,1,0:T(4,128)(2,1)S(1)} async-done(((bf16[32,4,384]{2,1,0:T(4,128)(2,1)}), bf16[32,4,384]{2,1,0:T(4,128)(2,1)S(1)}, u32[]{:S(2)}, u32[]{:S(2)}) %all-to-all-start.2) | async-done | bytes 98336 | tf_op jit(solution)/shard_map/all_to_all | solution.py:498
  48.3 0.0 collective-permute-done.4.w3_hbm
  48.3 1.7 %shard_map.160 = bf16[8,16,384]{2,1,0:T(8,128)(2,1)S(1)} custom-call(s32[4]{0:T(128)} %step_hbm.7, bf16[32,4,384]{2,1,0:T(4,128)(2,1)S(1)} %all-to-all-done.2.mixed_ref, bf16[8,2,3072]{2,1,0:T(2,128)(2,1)S(1)} %all-to-all-done.tokens_ref, f32[4,8,3072]{2,1,0:T(8,128)} %mod_hbm.7, bf16[768,384]{1,0:T(8,128)(2,1)} %w0_hbm.1, ...), custom_call_target="tpu_custom_call" | custom-call | tf_op jit(solution)/shard_map/pallas_call | solution.py:558
  50.0 9.5 %all_to_all.25.first_ref = bf16[8,16,384]{2,1,0:T(8,128)(2,1)S(1)} all-to-all(bf16[8,16,384]{2,1,0:T(8,128)(2,1)S(1)} %shard_map.160), channel_id=1, replica_groups=mesh['row'=8,'col'=4] {'row'}, dimensions={0} | all-to-all | bytes 196608 | tf_op jit(solution)/shard_map/all_to_all | solution.py:498
  59.5 7.0 %shard_map.161 = f32[8,2,3072]{2,1,0:T(2,128)S(1)} custom-call(s32[4]{0:T(128)} %step_hbm.7, bf16[8,16,384]{2,1,0:T(8,128)(2,1)S(1)} %all_to_all.25.first_ref, f32[4,8,3072]{2,1,0:T(8,128)} %mod_hbm.7, bf16[3072,1536]{1,0:T(8,128)(2,1)} %w1_hbm.1, bf16[1536,3072]{1,0:T(8,128)(2,1)} %w2_hbm.1), custom_call_target="tpu_custom_call" | custom-call | tf_op jit(solution)/shard_map/pallas_call | solution.py:574
  66.5 10.2 %all_to_all.26.terms_ref = f32[8,2,3072]{2,1,0:T(2,128)S(1)} all-to-all(f32[8,2,3072]{2,1,0:T(2,128)S(1)} %shard_map.161), channel_id=1, replica_groups=mesh['row'=8,'col'=4] {'row'}, dimensions={0} | all-to-all | bytes 393216 | tf_op jit(solution)/shard_map/all_to_all | solution.py:498
  76.7 1.4 %shard_map.162.masked_ref = f32[2,64]{1,0:T(2,128)S(1)} custom-call(s32[4]{0:T(128)} %step_hbm.7, s32[2,4]{1,0:T(2,128)} %bitcast.9, f32[8,2,3072]{2,1,0:T(2,128)S(1)} %all_to_all.26.terms_ref, f32[4,8,3072]{2,1,0:T(8,128)} %mod_hbm.7, bf16[64,3072]{1,0:T(8,128)(2,1)} %bitcast.7), custom_call_target="tpu_custom_call" | custom-call | tf_op jit(solution)/shard_map/pallas_call | solution.py:590
  78.1 0.1 collective-permute-start.6
  78.1 0.6 collective-permute-start.5
  78.7 2.4 %collective-permute-done.6.far_ref = f32[2,64]{1,0:T(2,128)S(1)} collective-permute-done((f32[2,64]{1,0:T(2,128)S(1)}, f32[2,64]{1,0:T(2,128)S(1)}, u32[]{:S(2)}, u32[]{:S(2)}) %collective-permute-start.6) | collective-permute-done | bytes 544 | tf_op jit(solution)/shard_map/ppermute | solution.py:599
  81.1 0.0 collective-permute-done.5.near_ref
  81.1 1.3 %shard_map.163 = (f32[2,64]{1,0:T(2,128)}, f32[2,64]{1,0:T(2,128)}) custom-call(s32[2,4]{1,0:T(2,128)} %bitcast.10, f32[2,64]{1,0:T(2,128)S(1)} %shard_map.162.masked_ref, f32[2,64]{1,0:T(2,128)S(1)} %collective-permute-done.5.near_ref, f32[2,64]{1,0:T(2,128)S(1)} %collective-permute-done.6.far_ref, f32[2,64]{1,0:T(2,128)} %latent_hbm.1), custom_call_target="tpu_custom_call" | custom-call | tf_op jit(solution)/shard_map/pallas_call | solution.py:601
Async XLA Ops:
  0.6 37.1 %collective-permute-start.2 = (bf16[768,384]{1,0:T(8,128)(2,1)}, bf16[768,384]{1,0:T(8,128)(2,1)S(1)}, u32[]{:S(2)}, u32[]{:S(2)}) collective-permute-start(bf16[768,384]{1,0:T(8,128)(2,1)} %w0_hbm.1), channel_id=1, source_target_pairs={{0,2},{1,3},{2,0},{3,1},{4,6},{5,7},{6,4},{7,5},{8,10},{9,11},{10,... | collective-permute-start | bytes 1769480 | tf_op jit(solution)/shard_map/ppermute | solution.py:522
  5.0 14.4 %all-to-all-start = ((bf16[8,2,3072]{2,1,0:T(2,128)(2,1)}), bf16[8,2,3072]{2,1,0:T(2,128)(2,1)S(1)}, u32[]{:S(2)}, u32[]{:S(2)}) async-start(bf16[8,2,3072]{2,1,0:T(2,128)(2,1)} %broadcast_in_dim.2), calls=%async_computation | async-start | bytes 196608 | tf_op jit(solution)/shard_map/all_to_all | solution.py:498
  11.8 5.6 %collective-permute-start.1 = (bf16[128,384]{1,0:T(8,128)(2,1)S(1)}, bf16[128,384]{1,0:T(8,128)(2,1)S(1)}, u32[]{:S(2)}, u32[]{:S(2)}) collective-permute-start(bf16[128,384]{1,0:T(8,128)(2,1)S(1)} %constant_dynamic-slice_fusion), channel_id=1, source_target_pairs={{0,4},{4,0},{8,12},{12,8},{16,20},{20,16},{24,28},{28,24},{1,5},{5... | collective-permute-start | bytes 294920 | tf_op jit(solution)/shard_map/ppermute | solution.py:520
  14.8 4.7 %collective-permute-start = (bf16[128,384]{1,0:T(8,128)(2,1)S(1)}, bf16[128,384]{1,0:T(8,128)(2,1)S(1)}, u32[]{:S(2)}, u32[]{:S(2)}) collective-permute-start(bf16[128,384]{1,0:T(8,128)(2,1)S(1)} %constant_dynamic-slice_fusion.1), channel_id=1, source_target_pairs={{0,4},{4,0},{8,12},{12,8},{16,20},{20,16},{24,28},{28,24},{1,5},{5... | collective-permute-start | bytes 294920 | tf_op jit(solution)/shard_map/ppermute | solution.py:519
  23.6 11.5 %all-to-all-start.1 = ((bf16[32,4,384]{2,1,0:T(4,128)(2,1)}), bf16[32,4,384]{2,1,0:T(4,128)(2,1)S(1)}, u32[]{:S(2)}, u32[]{:S(2)}) async-start(bf16[32,4,384]{2,1,0:T(4,128)(2,1)} %shard_map.158), calls=%async_computation.1 | async-start | bytes 196608 | tf_op jit(solution)/shard_map/all_to_all | solution.py:498
  27.3 13.2 %collective-permute-start.3 = (bf16[768,384]{1,0:T(8,128)(2,1)}, bf16[768,384]{1,0:T(8,128)(2,1)S(1)}, u32[]{:S(2)}, u32[]{:S(2)}) collective-permute-start(bf16[768,384]{1,0:T(8,128)(2,1)} %w0_hbm.1), channel_id=1, source_target_pairs={{0,1},{1,0},{2,3},{3,2},{4,5},{5,4},{6,7},{7,6},{8,9},{9,8},{10,11... | collective-permute-start | bytes 1769480 | tf_op jit(solution)/shard_map/ppermute | solution.py:524
  37.7 10.6 %collective-permute-start.4 = (bf16[768,384]{1,0:T(8,128)(2,1)S(1)}, bf16[768,384]{1,0:T(8,128)(2,1)S(1)}, u32[]{:S(2)}, u32[]{:S(2)}) collective-permute-start(bf16[768,384]{1,0:T(8,128)(2,1)S(1)} %collective-permute-done.2.w2_hbm), channel_id=1, source_target_pairs={{0,1},{1,0},{2,3},{3,2},{4,5},{5,4},{6,7},{7,6},{8,9},{9,8},{10,11... | collective-permute-start | bytes 1769480 | tf_op jit(solution)/shard_map/ppermute | solution.py:556
  37.9 10.4 %all-to-all-start.2 = ((bf16[32,4,384]{2,1,0:T(4,128)(2,1)}), bf16[32,4,384]{2,1,0:T(4,128)(2,1)S(1)}, u32[]{:S(2)}, u32[]{:S(2)}) async-start(bf16[32,4,384]{2,1,0:T(4,128)(2,1)} %shard_map.159), calls=%async_computation.2 | async-start | bytes 196608 | tf_op jit(solution)/shard_map/all_to_all | solution.py:498
  78.1 3.1 %collective-permute-start.6 = (f32[2,64]{1,0:T(2,128)S(1)}, f32[2,64]{1,0:T(2,128)S(1)}, u32[]{:S(2)}, u32[]{:S(2)}) collective-permute-start(f32[2,64]{1,0:T(2,128)S(1)} %shard_map.162.masked_ref), channel_id=1, source_target_pairs={{0,3},{1,2},{2,1},{3,0},{4,7},{5,6},{6,5},{7,4},{8,11},{9,10},{10,... | collective-permute-start | bytes 1544 | tf_op jit(solution)/shard_map/ppermute | solution.py:599
  78.1 3.0 %collective-permute-start.5 = (f32[2,64]{1,0:T(2,128)S(1)}, f32[2,64]{1,0:T(2,128)S(1)}, u32[]{:S(2)}, u32[]{:S(2)}) collective-permute-start(f32[2,64]{1,0:T(2,128)S(1)} %shard_map.162.masked_ref), channel_id=1, source_target_pairs={{0,1},{1,0},{2,3},{3,2},{4,5},{5,4},{6,7},{7,6},{8,9},{9,8},{10,11... | collective-permute-start | bytes 1544 | tf_op jit(solution)/shard_map/ppermute | solution.py:598

commit v3 on v2

--- a/solution.py
+++ b/solution.py
@@ -282,8 +282,16 @@
             out_ref[8 * q + place] = whole[4 * q : 4 * q + 4, piece * size : (piece + 1) * size]
 
 
+def give_kernel(k_hbm, v_hbm, out_ref, sems):
+    size = out_ref.shape[2]
+    start = (1 - lax.rem(lax.axis_index("row"), 2)) * size
+    part = pl.ds(pl.multiple_of(start, size), size)
+    for copy in start_copies([(k_hbm.at[:, part], out_ref.at[0]), (v_hbm.at[:, part], out_ref.at[1])], sems):
+        copy.wait()
+
+
 def attention_kernel(
-    size_hbm, offset_hbm, rows_ref, own_k_hbm, own_v_hbm, other_k_hbm, other_v_hbm, q_gain_hbm, k_gain_hbm, out_ref,
+    size_hbm, offset_hbm, rows_ref, own_k_hbm, own_v_hbm, other_hbm, q_gain_hbm, k_gain_hbm, out_ref,
     size_ref, offset_ref, q_gain_ref, k_gain_ref, q_ref, k_ref, v_ref, text_k_ref, text_v_ref, sems,
 ):
     row = lax.axis_index("row")
@@ -306,9 +314,9 @@
             (q_gain_hbm, q_gain_ref),
             (k_gain_hbm, k_gain_ref),
             (own_k_hbm.at[:, own], text_k_ref.at[top_rows, :]),
-            (other_k_hbm, text_k_ref.at[low_rows, :]),
+            (other_hbm.at[0], text_k_ref.at[low_rows, :]),
             (own_v_hbm.at[:, own], text_v_ref.at[top_rows, :]),
-            (other_v_hbm, text_v_ref.at[low_rows, :]),
+            (other_hbm.at[1], text_v_ref.at[low_rows, :]),
         ],
         sems,
     )
@@ -434,7 +442,9 @@
             out_ref[REQ * g + q] = term[4 * q + 2 * g : 4 * q + 2 * g + 2, :]
 
 
-def final_kernel(step_hbm, size_hbm, terms_ref, mod_hbm, w_hbm, out_ref, step_ref, size_ref, mod_ref, w_ref, sems):
+def final_kernel(
+    step_hbm, size_hbm, terms_ref, mod_hbm, w_hbm, out_ref, live_ref, step_ref, size_ref, mod_ref, w_ref, sems
+):
     row = lax.axis_index("row")
     col = lax.axis_index("col")
     req = lax.rem(row, REQ)
@@ -450,20 +460,16 @@
     step = step_ref[req]
     normed = (normed * (1.0 + mod_ref[step, 7:8, :]) + mod_ref[step, 6:7, :]).astype(bf16)
     size_copy.wait()
+    grid_col = col * out_ref.shape[0] + lax.broadcasted_iota(jnp.int32, out_ref.shape, 0)
+    live = (row // REQ < size_ref[0, req]) & (grid_col < size_ref[1, req])
+    live_ref[...] = jnp.where(live, 1.0, 0.0)
     w_copy.wait()
     raw = lax.dot_general(normed, w_ref[...], (((1,), (1,)), ((), ())), preferred_element_type=f32)
-    out_ref[...] = jnp.where(live_rows(size_ref, row, col, raw.shape), raw, 0.0)
-
-
-def live_rows(size_ref, row, col, shape):
-    req = lax.rem(row, REQ)
-    grid_col = col * shape[0] + lax.broadcasted_iota(jnp.int32, shape, 0)
-    return (row // REQ < size_ref[0, req]) & (grid_col < size_ref[1, req])
-
-
-def blend_kernel(size_hbm, masked_ref, near_ref, far_ref, latent_hbm, velocity_ref, next_ref, size_ref, latent_ref, sems):
+    out_ref[...] = jnp.where(live, raw, 0.0)
+
+
+def blend_kernel(masked_ref, live_ref, near_ref, far_ref, latent_ref, velocity_ref, next_ref):
     col = lax.axis_index("col")
-    size_copy, latent_copy = start_copies([(size_hbm, size_ref), (latent_hbm, latent_ref)], sems)
     masked = masked_ref[...]
     near = near_ref[...]
     far = jnp.where((col == 1) | (col == 2), far_ref[...], 0.0)
@@ -471,11 +477,8 @@
     count = masked.shape[0]
     left = jnp.concatenate([jnp.where(odd, near, far)[count - 1 :, :], masked[: count - 1, :]], 0)
     right = jnp.concatenate([masked[1:, :], jnp.where(odd, far, near)[:1, :]], 0)
-    size_copy.wait()
-    live = live_rows(size_ref, lax.axis_index("row"), col, masked.shape)
-    velocity = jnp.where(live, masked + blend * (left + right - 2.0 * masked), 0.0)
+    velocity = jnp.where(live_ref[...] > 0.0, masked + blend * (left + right - 2.0 * masked), 0.0)
     velocity_ref[...] = velocity
-    latent_copy.wait()
     next_ref[...] = latent_ref[...] + -1.0 / STEPS * velocity
 
 
@@ -504,7 +507,6 @@
 ):
     rows = lax.axis_size("row")
     cols = lax.axis_size("col")
-    row = lax.axis_index("row")
     stay = lambda values: pltpu.with_memory_space_constraint(values, pltpu.HBM)
     tile_w, width = image_states.shape
     head = q_gain.shape[0]
@@ -512,15 +514,14 @@
     tokens = rows * tile_w
     both = ("row", "col")
 
-    gathered = exchange(jnp.broadcast_to(image_states[None], (rows, tile_w, width)), "row")
-
-    give = (1 - row % 2) * piece
-    swap = [(i, i ^ 1) for i in range(rows)]
-    other_k = lax.ppermute(lax.dynamic_slice_in_dim(text_keys, give, piece, 1), "row", swap)
-    other_v = lax.ppermute(lax.dynamic_slice_in_dim(text_values, give, piece, 1), "row", swap)
-    gathered, other_k, other_v = lax.optimization_barrier((gathered, other_k, other_v))
+    spread, w_out = lax.optimization_barrier((jnp.broadcast_to(image_states[None], (rows, tile_w, width)), w_out))
+    gathered = exchange(spread, "row")
+    given = call(
+        give_kernel, (2, text_keys.shape[0], piece), bf16, [HBM_SPEC] * 2, [pltpu.SemaphoreType.DMA((2,))], limit=4 << 20
+    )(stay(text_keys), stay(text_values))
+    other = lax.ppermute(given, "row", [(i, i ^ 1) for i in range(rows)])
+    near = [(i, i ^ 1) for i in range(cols)]
     w_x = lax.ppermute(w_out, "col", [(i, i ^ 2) for i in range(cols)])
-    near = [(i, i ^ 1) for i in range(cols)]
     w_k = lax.ppermute(w_out, "col", near)
 
     sems = lambda count: pltpu.SemaphoreType.DMA((count,))
@@ -539,17 +540,18 @@
         [steps_space, pltpu.VMEM((tokens, width), f32), mod_space, pltpu.VMEM(w_qkv.shape, bf16), sems(QKV_CHUNKS + 2)],
         limit=16 << 20,
     )(steps, gathered, mods, stay(w_qkv))
+    pieces, other, w_k = lax.optimization_barrier((pieces, other, w_k))
     got = exchange(pieces, both).reshape(rows, cols, 4, piece)
     text_space = pltpu.VMEM((2 * text_keys.shape[0], piece), bf16)
     mixed = call(
         attention_kernel,
         (rows * cols, 4, piece),
         bf16,
-        [HBM_SPEC, HBM_SPEC, VMEM_SPEC] + [HBM_SPEC] * 6,
+        [HBM_SPEC, HBM_SPEC, VMEM_SPEC] + [HBM_SPEC] * 5,
         [sizes_space] * 2 + [gain_space] * 2 + [pltpu.VMEM((tokens, piece), f32)] * 3 + [text_space] * 2 + [sems(8)],
         limit=8 << 20,
     )(
-        sizes, stay(rope_offset.T), got, stay(text_keys), stay(text_values), other_k, other_v,
+        sizes, stay(rope_offset.T), got, stay(text_keys), stay(text_values), other,
         stay(q_gain.reshape(1, head)), stay(k_gain.reshape(1, head)),
     )
     mixed, w_x = lax.optimization_barrier((mixed, w_x))
@@ -587,25 +589,24 @@
         limit=40 << 20,
     )(steps, all_first, mods, stay(w_fc1), stay(w_fc2))
     all_terms = exchange(terms, "row")
-    masked = call(
+    result = jax.ShapeDtypeStruct(latent.shape, f32)
+    masked, live = pl.pallas_call(
         final_kernel,
-        (tile_w, w_final.shape[1]),
-        f32,
-        [HBM_SPEC, HBM_SPEC, VMEM_SPEC, HBM_SPEC, HBM_SPEC],
-        [steps_space, sizes_space, mod_space, pltpu.VMEM(w_final.shape[::-1], bf16), sems(4)],
-        limit=8 << 20,
+        out_shape=(result, result),
+        in_specs=[HBM_SPEC, HBM_SPEC, VMEM_SPEC, HBM_SPEC, HBM_SPEC],
+        out_specs=(VMEM_SPEC, VMEM_SPEC),
+        scratch_shapes=[steps_space, sizes_space, mod_space, pltpu.VMEM(w_final.shape[::-1], bf16), sems(4)],
+        compiler_params=pltpu.CompilerParams(vmem_limit_bytes=8 << 20),
     )(steps, sizes, all_terms, mods, stay(w_final.T))
     beside = lax.ppermute(masked, "col", near)
     across = lax.ppermute(masked, "col", [(i, i ^ 3) for i in range(cols)])
-    result = jax.ShapeDtypeStruct(latent.shape, f32)
     return pl.pallas_call(
         blend_kernel,
         out_shape=(result, result),
-        in_specs=[HBM_SPEC] + [VMEM_SPEC] * 3 + [HBM_SPEC],
+        in_specs=[VMEM_SPEC] * 5,
         out_specs=(VMEM_SPEC, VMEM_SPEC),
-        scratch_shapes=[sizes_space, pltpu.VMEM(latent.shape, f32), sems(2)],
         compiler_params=pltpu.CompilerParams(vmem_limit_bytes=8 << 20),
-    )(sizes, masked, beside, across, stay(latent))
+    )(masked, live, beside, across, latent)
 
 
 def solution(mesh):

time: 83 us -> 77.4 us (0.933)
  blocking collectives: 19.7 us -> 50.5 us
  waiting for transfers between devices: 22.3 us -> 2.42 us
  starting transfers between devices: 18.3 us -> 5.49 us
  local copies, waits for them, and re-layouts: 3.2 us -> 0.77 us
  Pallas kernels: 18.1 us -> 17.1 us
    all_to_all x2 -> x5, blocking collectives: 19.7 us -> 50.5 us  [exchange(): return lax.all_to_all(values, axes, split_axis=0, concat_axis=0, tiled=True)]
    all_to_all x3 -> x0, waiting for transfers between devices: 15.3 us -> none  [exchange(): return lax.all_to_all(values, axes, split_axis=0, concat_axis=0, tiled=True)]
    all_to_all x3 -> x0, starting transfers between devices: 12 us -> none  [exchange(): return lax.all_to_all(values, axes, split_axis=0, concat_axis=0, tiled=True)]
    ppermute x2 -> x1, waiting for transfers between devices: 4.59 us -> 0.01 us  [compact_on_device(): other = lax.ppermute(given, 'row', [(i, i ^ 1) for i in range(rows)])]
    dynamic_slice x2 -> x0, local copies, waits for them, and re-layouts: 1.81 us -> none  [the longest x1 0.9 us: compact_on_device(): lax.dynamic_slice_in_dim(text_keys, give, piece, 1)]
    ppermute x2 -> x1, starting transfers between devices: 2.17 us -> 1.58 us  [compact_on_device(): other = lax.ppermute(given, 'row', [(i, i ^ 1) for i in range(rows)])]
    pallas_call x2 -> x3, Pallas kernels: 2.66 us -> 2.91 us  [the longest x1 1.37 us: compact_on_device(): pl.pallas_call(final_kernel, out_shape=(result, result), in_specs=[HBM_SP...]
  transfers between devices with their start and end apart: 10 -> 6, of which waited for: 5 -> 1; matrix products, arithmetic and copies ran while one was open for 4% -> 0% of each run, Pallas kernels for 8% -> 8%
where the time goes in v3:
time: 77.4 us; the launch traced here: 77 us
  blocking collectives  50.5 us (65%)
  Pallas kernels  17.1 us (22%)
  starting transfers between devices  5.49 us (7%)
  waiting for transfers between devices  2.42 us (3%)
    all_to_all x5, blocking collectives, exchange(): return lax.all_to_all(values, axes, split_axis=0, concat_axis=0, tiled=True)  50.5 us
    pallas_call x1, Pallas kernels, compact_on_device(): call(mlp_kernel, (rows, tile_w, width), f32, [HBM_SPEC, VMEM_SPEC] + [HBM...  7.01 us
    pallas_call x1, Pallas kernels, compact_on_device(): call(qkv_kernel, (rows * cols, 4, piece), bf16, [HBM_SPEC, VMEM_SPEC, HBM...  3.52 us
    ppermute x1, starting transfers between devices, compact_on_device(): w_x = lax.ppermute(w_out, 'col', [(i, i ^ 2) for i in range(cols)])  2.57 us
    ppermute x1, waiting for transfers between devices, compact_on_device(): across = lax.ppermute(masked, 'col', [(i, i ^ 3) for i in range(cols)])  2.41 us
    pallas_call x1, Pallas kernels, compact_on_device(): call(attention_kernel, (rows * cols, 4, piece), bf16, [HBM_SPEC, HBM_SPEC...  1.99 us
    pallas_call x1, Pallas kernels, compact_on_device(): call(out_kernel, (rows, tokens, piece), bf16, [HBM_SPEC, VMEM_SPEC, VMEM_...  1.67 us
    ppermute x1, starting transfers between devices, compact_on_device(): other = lax.ppermute(given, 'row', [(i, i ^ 1) for i in range(rows)])  1.58 us
  transfers between devices with their start and end apart: 6, of which 1 were waited for; matrix products, arithmetic and copies ran while one was open for 0% of the time, Pallas kernels for 8%

profile of v3, /device:TPU:0, one launch (start us, length us, event | category | flops | bytes accessed | tf_op | source)
XLA Modules:
  0.0 77.0 jit_solution(1765371087954647158)
XLA Ops:
  0.6 0.8 broadcast_in_dim.2
  1.4 0.5 collective-permute-start.1
  1.9 2.6 %collective-permute-start.2 = (bf16[768,384]{1,0:T(8,128)(2,1)}, bf16[768,384]{1,0:T(8,128)(2,1)S(1)}, u32[]{:S(2)}, u32[]{:S(2)}) collective-permute-start(bf16[768,384]{1,0:T(8,128)(2,1)} %w0_hbm), channel_id=1, source_target_pairs={{0,2},{1,3},{2,0},{3,1},{4,6},{5,7},{6,4},{7,5},{8,10},{9,11},{10,... | collective-permute-start | bytes 1769480 | tf_op jit(solution)/shard_map/ppermute | solution.py:524
  4.5 1.0 %shard_map.159 = bf16[2,128,384]{2,1,0:T(8,128)(2,1)S(1)} custom-call(bf16[128,768]{1,0:T(8,128)(2,1)} %own_k_hbm.1, bf16[128,768]{1,0:T(8,128)(2,1)} %own_v_hbm.1), custom_call_target="tpu_custom_call" | custom-call | tf_op jit(solution)/shard_map/pallas_call | solution.py:519
  5.4 1.6 %collective-permute-start = (bf16[2,128,384]{2,1,0:T(8,128)(2,1)S(1)}, bf16[2,128,384]{2,1,0:T(8,128)(2,1)S(1)}, u32[]{:S(2)}, u32[]{:S(2)}) collective-permute-start(bf16[2,128,384]{2,1,0:T(8,128)(2,1)S(1)} %shard_map.159), channel_id=1, source_target_pairs={{0,4},{4,0},{8,12},{12,8},{16,20},{20,16},{24,28},{28,24},{1,5},{5... | collective-permute-start | bytes 589832 | tf_op jit(solution)/shard_map/ppermute | solution.py:522
  7.0 11.8 %all_to_all.25.tokens_ref = bf16[8,2,3072]{2,1,0:T(2,128)(2,1)S(1)} all-to-all(bf16[8,2,3072]{2,1,0:T(2,128)(2,1)S(1)} %broadcast_in_dim.2), channel_id=1, replica_groups=mesh['row'=8,'col'=4] {'row'}, dimensions={0} | all-to-all | bytes 196608 | tf_op jit(solution)/shard_map/all_to_all | solution.py:501
  18.8 3.5 %shard_map.158 = bf16[32,4,384]{2,1,0:T(4,128)(2,1)S(1)} custom-call(s32[4]{0:T(128)} %step_hbm.7, bf16[8,2,3072]{2,1,0:T(2,128)(2,1)S(1)} %all_to_all.25.tokens_ref, f32[4,8,3072]{2,1,0:T(8,128)} %mod_hbm.7, bf16[3072,1152]{1,0:T(8,128)(2,1)} %w_hbm.1), custom_call_target="tpu_custom_call" | custom-call | tf_op jit(solution)/shard_map/pallas_call | solution.py:535
  22.3 0.0 collective-permute-done.other_hbm
  22.4 0.0 collective-permute-done.1.w1_hbm
  22.4 9.5 %all_to_all.26 = bf16[32,4,384]{2,1,0:T(4,128)(2,1)S(1)} all-to-all(bf16[32,4,384]{2,1,0:T(4,128)(2,1)S(1)} %shard_map.158), channel_id=1, replica_groups=mesh['row'=8,'col'=4] {'row','col'}, dimensions={0} | all-to-all | bytes 196608 | tf_op jit(solution)/shard_map/all_to_all | solution.py:501
  31.9 2.0 %shard_map.160 = bf16[32,4,384]{2,1,0:T(4,128)(2,1)S(1)} custom-call(s32[2,4]{1,0:T(2,128)} %bitcast.8, s32[2,4]{1,0:T(2,128)} %bitcast.10, bf16[8,4,4,384]{3,2,1,0:T(4,128)(2,1)S(1)} %bitcast.6, bf16[128,768]{1,0:T(8,128)(2,1)} %own_k_hbm.1, bf16[128,768]{1,0:T(8,128)(2,1)} %own_v_hbm.1, bf16[2,128,384]{2,1,0:T(8,128)(2,1)S(1)} %collective-permute-done.other_hbm, ...), custom_call_target="tpu_custom_call" | custom-call | tf_op jit(solution)/shard_map/pallas_call | solution.py:546
  33.9 0.0 collective-permute-done.2.w2_hbm
  33.9 0.2 collective-permute-start.3
  34.1 9.5 %all_to_all.27.mixed_ref = bf16[32,4,384]{2,1,0:T(4,128)(2,1)S(1)} all-to-all(bf16[32,4,384]{2,1,0:T(4,128)(2,1)S(1)} %shard_map.160), channel_id=1, replica_groups=mesh['row'=8,'col'=4] {'row','col'}, dimensions={0} | all-to-all | bytes 196608 | tf_op jit(solution)/shard_map/all_to_all | solution.py:501
  43.5 0.0 collective-permute-done.3.w3_hbm
  43.6 1.7 %shard_map.161 = bf16[8,16,384]{2,1,0:T(8,128)(2,1)S(1)} custom-call(s32[4]{0:T(128)} %step_hbm.7, bf16[32,4,384]{2,1,0:T(4,128)(2,1)S(1)} %all_to_all.27.mixed_ref, bf16[8,2,3072]{2,1,0:T(2,128)(2,1)S(1)} %all_to_all.25.tokens_ref, f32[4,8,3072]{2,1,0:T(8,128)} %mod_hbm.7, bf16[768,384]{1,0:T(8,128)(2,1)} %w0_hbm, ...), custom_call_target="tpu_custom_call" | custom-call | tf_op jit(solution)/shard_map/pallas_call | solution.py:560
  45.2 9.5 %all_to_all.28.first_ref = bf16[8,16,384]{2,1,0:T(8,128)(2,1)S(1)} all-to-all(bf16[8,16,384]{2,1,0:T(8,128)(2,1)S(1)} %shard_map.161), channel_id=1, replica_groups=mesh['row'=8,'col'=4] {'row'}, dimensions={0} | all-to-all | bytes 196608 | tf_op jit(solution)/shard_map/all_to_all | solution.py:501
  54.7 0.0 copy-start
  54.7 7.0 %shard_map.162 = f32[8,2,3072]{2,1,0:T(2,128)S(1)} custom-call(s32[4]{0:T(128)} %step_hbm.7, bf16[8,16,384]{2,1,0:T(8,128)(2,1)S(1)} %all_to_all.28.first_ref, f32[4,8,3072]{2,1,0:T(8,128)} %mod_hbm.7, bf16[3072,1536]{1,0:T(8,128)(2,1)} %w1_hbm.1, bf16[1536,3072]{1,0:T(8,128)(2,1)} %w2_hbm.1), custom_call_target="tpu_custom_call" | custom-call | tf_op jit(solution)/shard_map/pallas_call | solution.py:576
  61.8 10.2 %all_to_all.29.terms_ref = f32[8,2,3072]{2,1,0:T(2,128)S(1)} all-to-all(f32[8,2,3072]{2,1,0:T(2,128)S(1)} %shard_map.162), channel_id=1, replica_groups=mesh['row'=8,'col'=4] {'row'}, dimensions={0} | all-to-all | bytes 393216 | tf_op jit(solution)/shard_map/all_to_all | solution.py:501
  72.0 1.4 %shard_map.163 = (f32[2,64]{1,0:T(2,128)S(1)}, f32[2,64]{1,0:T(2,128)S(1)}) custom-call(s32[4]{0:T(128)} %step_hbm.7, s32[2,4]{1,0:T(2,128)} %bitcast.9, f32[8,2,3072]{2,1,0:T(2,128)S(1)} %all_to_all.29.terms_ref, f32[4,8,3072]{2,1,0:T(8,128)} %mod_hbm.7, bf16[64,3072]{1,0:T(8,128)(2,1)} %bitcast.7), custom_call_target="tpu_custom_call" | custom-call | tf_op jit(solution)/shard_map/pallas_call | solution.py:593
  73.3 0.1 collective-permute-start.5
  73.4 0.6 collective-permute-start.4
  74.0 2.4 %collective-permute-done.5.far_ref = f32[2,64]{1,0:T(2,128)S(1)} collective-permute-done((f32[2,64]{1,0:T(2,128)S(1)}, f32[2,64]{1,0:T(2,128)S(1)}, u32[]{:S(2)}, u32[]{:S(2)}) %collective-permute-start.5) | collective-permute-done | bytes 544 | tf_op jit(solution)/shard_map/ppermute | solution.py:602
  76.4 0.0 collective-permute-done.4.near_ref
  76.4 0.0 copy-done
  76.4 0.6 shard_map.164
Async XLA Ops:
  1.4 21.0 %collective-permute-start.1 = (bf16[768,384]{1,0:T(8,128)(2,1)}, bf16[768,384]{1,0:T(8,128)(2,1)S(1)}, u32[]{:S(2)}, u32[]{:S(2)}) collective-permute-start(bf16[768,384]{1,0:T(8,128)(2,1)} %w0_hbm), channel_id=1, source_target_pairs={{0,1},{1,0},{2,3},{3,2},{4,5},{5,4},{6,7},{7,6},{8,9},{9,8},{10,11... | collective-permute-start | bytes 1769480 | tf_op jit(solution)/shard_map/ppermute | solution.py:525
  1.9 32.0 %collective-permute-start.2 = (bf16[768,384]{1,0:T(8,128)(2,1)}, bf16[768,384]{1,0:T(8,128)(2,1)S(1)}, u32[]{:S(2)}, u32[]{:S(2)}) collective-permute-start(bf16[768,384]{1,0:T(8,128)(2,1)} %w0_hbm), channel_id=1, source_target_pairs={{0,2},{1,3},{2,0},{3,1},{4,6},{5,7},{6,4},{7,5},{8,10},{9,11},{10,... | collective-permute-start | bytes 1769480 | tf_op jit(solution)/shard_map/ppermute | solution.py:524
  5.4 16.9 %collective-permute-start = (bf16[2,128,384]{2,1,0:T(8,128)(2,1)S(1)}, bf16[2,128,384]{2,1,0:T(8,128)(2,1)S(1)}, u32[]{:S(2)}, u32[]{:S(2)}) collective-permute-start(bf16[2,128,384]{2,1,0:T(8,128)(2,1)S(1)} %shard_map.159), channel_id=1, source_target_pairs={{0,4},{4,0},{8,12},{12,8},{16,20},{20,16},{24,28},{28,24},{1,5},{5... | collective-permute-start | bytes 589832 | tf_op jit(solution)/shard_map/ppermute | solution.py:522
  33.9 9.7 %collective-permute-start.3 = (bf16[768,384]{1,0:T(8,128)(2,1)S(1)}, bf16[768,384]{1,0:T(8,128)(2,1)S(1)}, u32[]{:S(2)}, u32[]{:S(2)}) collective-permute-start(bf16[768,384]{1,0:T(8,128)(2,1)S(1)} %collective-permute-done.2.w2_hbm), channel_id=1, source_target_pairs={{0,1},{1,0},{2,3},{3,2},{4,5},{5,4},{6,7},{7,6},{8,9},{9,8},{10,11... | collective-permute-start | bytes 1769480 | tf_op jit(solution)/shard_map/ppermute | solution.py:558
  54.7 21.7 %copy-start = (f32[2,64]{1,0:T(2,128)S(1)}, f32[2,64]{1,0:T(2,128)}, u32[]{:S(2)}) copy-start(f32[2,64]{1,0:T(2,128)} %latent_ref.1) | copy-start | bytes 1540
  73.3 3.1 %collective-permute-start.5 = (f32[2,64]{1,0:T(2,128)S(1)}, f32[2,64]{1,0:T(2,128)S(1)}, u32[]{:S(2)}, u32[]{:S(2)}) collective-permute-start(f32[2,64]{1,0:T(2,128)S(1)} %get-tuple-element.18.masked_ref), channel_id=1, source_target_pairs={{0,3},{1,2},{2,1},{3,0},{4,7},{5,6},{6,5},{7,4},{8,11},{9,10},{10,... | collective-permute-start | bytes 1544 | tf_op jit(solution)/shard_map/ppermute | solution.py:602
  73.4 3.0 %collective-permute-start.4 = (f32[2,64]{1,0:T(2,128)S(1)}, f32[2,64]{1,0:T(2,128)S(1)}, u32[]{:S(2)}, u32[]{:S(2)}) collective-permute-start(f32[2,64]{1,0:T(2,128)S(1)} %get-tuple-element.18.masked_ref), channel_id=1, source_target_pairs={{0,1},{1,0},{2,3},{3,2},{4,5},{5,4},{6,7},{7,6},{8,9},{9,8},{10,11... | collective-permute-start | bytes 1544 | tf_op jit(solution)/shard_map/ppermute | solution.py:601

commit v4 on v3

--- a/solution.py
+++ b/solution.py
@@ -257,13 +257,11 @@
     return whole
 
 
-def qkv_kernel(step_hbm, tokens_ref, mod_hbm, w_hbm, out_ref, step_ref, order_ref, mod_ref, w_ref, sems):
+def qkv_kernel(step_hbm, tokens_ref, mod_hbm, w_ref, out_ref, step_ref, order_ref, mod_ref, sems):
     row = lax.axis_index("row")
     depth = order_ref.shape[1]
     size = out_ref.shape[2]
-    step_copy, mod_copy, *w_copies = start_copies(
-        [(step_hbm, step_ref), (mod_hbm, mod_ref)] + row_chunks(w_hbm, w_ref, QKV_CHUNKS), sems
-    )
+    step_copy, mod_copy = start_copies([(step_hbm, step_ref), (mod_hbm, mod_ref)], sems)
     for q in range(REQ):
         for g in range(2):
             order_ref[4 * q + 2 * g : 4 * q + 2 * g + 2, :] = tokens_ref[REQ * g + q].astype(f32)
@@ -274,7 +272,7 @@
     shift = per_request(mod_ref, step_ref, 0, 4, 0, depth)
     scale = per_request(mod_ref, step_ref, 1, 4, 0, depth)
     normed = (normed * (1.0 + scale) + shift).astype(bf16)
-    whole = chunked_dot(normed, w_ref, w_copies).astype(bf16)
+    whole = jnp.dot(normed, w_ref[...], preferred_element_type=f32).astype(bf16)
     for piece in range(w_ref.shape[1] // size):
         group = lax.rem(row * 3 + piece, 8)
         place = lax.rem(group, 2) * 4 + group // 2
@@ -282,11 +280,13 @@
             out_ref[8 * q + place] = whole[4 * q : 4 * q + 4, piece * size : (piece + 1) * size]
 
 
-def give_kernel(k_hbm, v_hbm, out_ref, sems):
-    size = out_ref.shape[2]
+def opening_kernel(states_hbm, k_hbm, v_hbm, spread_ref, given_ref, sems):
+    size = given_ref.shape[2]
     start = (1 - lax.rem(lax.axis_index("row"), 2)) * size
     part = pl.ds(pl.multiple_of(start, size), size)
-    for copy in start_copies([(k_hbm.at[:, part], out_ref.at[0]), (v_hbm.at[:, part], out_ref.at[1])], sems):
+    pairs = [(k_hbm.at[:, part], given_ref.at[0]), (v_hbm.at[:, part], given_ref.at[1])]
+    pairs += [(states_hbm, spread_ref.at[r]) for r in range(spread_ref.shape[0])]
+    for copy in start_copies(pairs, sems):
         copy.wait()
 
 
@@ -377,22 +377,15 @@
 
 
 def out_kernel(
-    step_hbm, mixed_ref, tokens_ref, mod_hbm, w0_hbm, w1_hbm, w2_hbm, w3_hbm, out_ref, step_ref, rows_ref, states_ref,
-    mod_ref, w_ref, sems,
+    step_hbm, mixed_ref, tokens_ref, mod_hbm, own_hbm, w1_ref, w2_ref, w3_ref, out_ref, step_ref, rows_ref, states_ref,
+    mod_ref, w0_ref, sems,
 ):
     row = lax.axis_index("row")
     col = lax.axis_index("col")
-    depth, width = w0_hbm.shape
+    depth, width = own_hbm.shape
     piece = mixed_ref.shape[2]
     start = pl.multiple_of(row * width, width)
-    step_copy, mod_copy, *w_copies = start_copies(
-        [(step_hbm, step_ref), (mod_hbm, mod_ref)]
-        + [
-            (w_hbm, w_ref.at[pl.ds(pl.multiple_of(jnp.bitwise_xor(col, d) * depth, depth), depth), :])
-            for d, w_hbm in enumerate((w0_hbm, w1_hbm, w2_hbm, w3_hbm))
-        ],
-        sems,
-    )
+    w_copy, step_copy, mod_copy = start_copies([(own_hbm, w0_ref), (step_hbm, step_ref), (mod_hbm, mod_ref)], sems)
     for r in range(8):
         for s in range(4):
             at = (2 * s + r % 2) * piece
@@ -400,27 +393,30 @@
     for q in range(REQ):
         for g in range(2):
             states_ref[4 * q + 2 * g : 4 * q + 2 * g + 2, :] = tokens_ref[REQ * g + q, :, pl.ds(start, width)].astype(f32)
-    mixed = rows_ref[...].astype(bf16)
+
+    def share(d, w_ref):
+        at = pl.multiple_of(jnp.bitwise_xor(col, d) * depth, depth)
+        return jnp.dot(rows_ref[:, pl.ds(at, depth)].astype(bf16), w_ref[...], preferred_element_type=f32)
+
+    attended = share(1, w1_ref) + share(2, w2_ref) + share(3, w3_ref)
+    w_copy.wait()
+    attended = attended + share(0, w0_ref)
     step_copy.wait()
     mod_copy.wait()
     gate = per_request(mod_ref, step_ref, 2, 4, start, width)
-    for copy in w_copies:
-        copy.wait()
-    attended = jnp.dot(mixed, w_ref[...], preferred_element_type=f32)
     first = (states_ref[...] + gate * attended).astype(bf16)
     for r in range(8):
         out_ref[r] = first
 
 
 def mlp_kernel(
-    step_hbm, first_ref, mod_hbm, w1_hbm, w2_hbm, out_ref, step_ref, rows_ref, mod_ref, w1_ref, w2_ref, sems
+    step_hbm, first_ref, mod_hbm, w1_ref, w2_hbm, out_ref, own_ref, step_ref, rows_ref, mod_ref, w2_ref, sems
 ):
     row = lax.axis_index("row")
     depth = rows_ref.shape[1]
     piece = first_ref.shape[2]
     step_copy, mod_copy, *w_copies = start_copies(
         [(step_hbm, step_ref), (mod_hbm, mod_ref)]
-        + row_chunks(w1_hbm, w1_ref, FC_CHUNKS)
         + row_chunks(w2_hbm, w2_ref, FC_CHUNKS),
         sems,
     )
@@ -432,18 +428,24 @@
     shift = per_request(mod_ref, step_ref, 3, 4, 0, depth)
     scale = per_request(mod_ref, step_ref, 4, 4, 0, depth)
     normed = (normed * (1.0 + scale) + shift).astype(bf16)
-    hidden = jax.nn.gelu(chunked_dot(normed, w1_ref, w_copies[:FC_CHUNKS]), approximate=True).astype(bf16)
-    added = chunked_dot(hidden, w2_ref, w_copies[FC_CHUNKS:])
+    own = rows_ref[0:2, :]
+    for q in range(REQ):
+        for g in range(2):
+            own = jnp.where(row == REQ * g + q, rows_ref[4 * q + 2 * g : 4 * q + 2 * g + 2, :], own)
+    own_ref[...] = own
+    hidden = jax.nn.gelu(
+        jnp.dot(normed, w1_ref[...], preferred_element_type=f32), approximate=True
+    ).astype(bf16)
+    added = chunked_dot(hidden, w2_ref, w_copies)
     gate = per_request(mod_ref, step_ref, 5, 4, 0, depth)
-    mine = jnp.where(row == 0, 1.0, 0.0)
-    term = gate * added + mine * rows_ref[...]
+    term = (gate * added).astype(out_ref.dtype)
     for q in range(REQ):
         for g in range(2):
             out_ref[REQ * g + q] = term[4 * q + 2 * g : 4 * q + 2 * g + 2, :]
 
 
 def final_kernel(
-    step_hbm, size_hbm, terms_ref, mod_hbm, w_hbm, out_ref, live_ref, step_ref, size_ref, mod_ref, w_ref, sems
+    step_hbm, size_hbm, terms_ref, first_ref, mod_hbm, w_hbm, out_ref, live_ref, step_ref, size_ref, mod_ref, w_ref, sems
 ):
     row = lax.axis_index("row")
     col = lax.axis_index("col")
@@ -451,9 +453,9 @@
     step_copy, size_copy, mod_copy, w_copy = start_copies(
         [(step_hbm, step_ref), (size_hbm, size_ref), (mod_hbm, mod_ref), (w_hbm, w_ref)], sems
     )
-    second = terms_ref[0]
-    for r in range(1, 8):
-        second = second + terms_ref[r]
+    second = first_ref[...]
+    for r in range(8):
+        second = second + terms_ref[r].astype(f32)
     normed = norm_rows(second)
     step_copy.wait()
     mod_copy.wait()
@@ -514,15 +516,22 @@
     tokens = rows * tile_w
     both = ("row", "col")
 
-    spread, w_out = lax.optimization_barrier((jnp.broadcast_to(image_states[None], (rows, tile_w, width)), w_out))
-    gathered = exchange(spread, "row")
-    given = call(
-        give_kernel, (2, text_keys.shape[0], piece), bf16, [HBM_SPEC] * 2, [pltpu.SemaphoreType.DMA((2,))], limit=4 << 20
-    )(stay(text_keys), stay(text_values))
+    near = [(i, i ^ 1) for i in range(cols)]
+    spread, given = pl.pallas_call(
+        opening_kernel,
+        out_shape=(
+            jax.ShapeDtypeStruct((rows, tile_w, width), bf16),
+            jax.ShapeDtypeStruct((2, text_keys.shape[0], piece), bf16),
+        ),
+        in_specs=[HBM_SPEC] * 3,
+        out_specs=(VMEM_SPEC, VMEM_SPEC),
+        scratch_shapes=[pltpu.SemaphoreType.DMA((rows + 2,))],
+        compiler_params=pltpu.CompilerParams(vmem_limit_bytes=4 << 20),
+    )(stay(image_states), stay(text_keys), stay(text_values))
     other = lax.ppermute(given, "row", [(i, i ^ 1) for i in range(rows)])
-    near = [(i, i ^ 1) for i in range(cols)]
     w_x = lax.ppermute(w_out, "col", [(i, i ^ 2) for i in range(cols)])
     w_k = lax.ppermute(w_out, "col", near)
+    gathered = exchange(spread, "row")
 
     sems = lambda count: pltpu.SemaphoreType.DMA((count,))
     mod_space = pltpu.VMEM(mod_table.shape, f32)
@@ -536,10 +545,10 @@
         qkv_kernel,
         (rows * cols, 4, piece),
         bf16,
-        [HBM_SPEC, VMEM_SPEC, HBM_SPEC, HBM_SPEC],
-        [steps_space, pltpu.VMEM((tokens, width), f32), mod_space, pltpu.VMEM(w_qkv.shape, bf16), sems(QKV_CHUNKS + 2)],
-        limit=16 << 20,
-    )(steps, gathered, mods, stay(w_qkv))
+        [HBM_SPEC, VMEM_SPEC, HBM_SPEC, VMEM_SPEC],
+        [steps_space, pltpu.VMEM((tokens, width), f32), mod_space, sems(2)],
+        limit=8 << 20,
+    )(steps, gathered, mods, lax.ppermute(w_qkv, "col", near))
     pieces, other, w_k = lax.optimization_barrier((pieces, other, w_k))
     got = exchange(pieces, both).reshape(rows, cols, 4, piece)
     text_space = pltpu.VMEM((2 * text_keys.shape[0], piece), bf16)
@@ -561,43 +570,45 @@
         out_kernel,
         (rows, tokens, piece),
         bf16,
-        [HBM_SPEC, VMEM_SPEC, VMEM_SPEC] + [HBM_SPEC] * 5,
+        [HBM_SPEC, VMEM_SPEC, VMEM_SPEC, HBM_SPEC, HBM_SPEC] + [VMEM_SPEC] * 3,
         [
             steps_space,
             pltpu.VMEM((tokens, width), f32),
             pltpu.VMEM((tokens, piece), f32),
             mod_space,
-            pltpu.VMEM((width, piece), bf16),
-            sems(6),
+            pltpu.VMEM(w_out.shape, bf16),
+            sems(3),
         ],
-        limit=16 << 20,
+        limit=8 << 20,
     )(steps, all_mixed, gathered, mods, stay(w_out), w_k, w_x, w_xk)
     all_first = exchange(first, "row")
-    terms = call(
+    terms, first_own = pl.pallas_call(
         mlp_kernel,
-        (rows, tile_w, width),
-        f32,
-        [HBM_SPEC, VMEM_SPEC] + [HBM_SPEC] * 3,
-        [
+        out_shape=(
+            jax.ShapeDtypeStruct((rows, tile_w, width), bf16),
+            jax.ShapeDtypeStruct((tile_w, width), f32),
+        ),
+        in_specs=[HBM_SPEC, VMEM_SPEC, HBM_SPEC, VMEM_SPEC, HBM_SPEC],
+        out_specs=(VMEM_SPEC, VMEM_SPEC),
+        scratch_shapes=[
             steps_space,
             pltpu.VMEM((tokens, width), f32),
             mod_space,
-            pltpu.VMEM(w_fc1.shape, bf16),
             pltpu.VMEM(w_fc2.shape, bf16),
-            sems(2 * FC_CHUNKS + 2),
+            sems(FC_CHUNKS + 2),
         ],
-        limit=40 << 20,
-    )(steps, all_first, mods, stay(w_fc1), stay(w_fc2))
+        compiler_params=pltpu.CompilerParams(vmem_limit_bytes=16 << 20),
+    )(steps, all_first, mods, w_fc1, stay(w_fc2))
     all_terms = exchange(terms, "row")
     result = jax.ShapeDtypeStruct(latent.shape, f32)
     masked, live = pl.pallas_call(
         final_kernel,
         out_shape=(result, result),
-        in_specs=[HBM_SPEC, HBM_SPEC, VMEM_SPEC, HBM_SPEC, HBM_SPEC],
+        in_specs=[HBM_SPEC, HBM_SPEC, VMEM_SPEC, VMEM_SPEC, HBM_SPEC, HBM_SPEC],
         out_specs=(VMEM_SPEC, VMEM_SPEC),
         scratch_shapes=[steps_space, sizes_space, mod_space, pltpu.VMEM(w_final.shape[::-1], bf16), sems(4)],
         compiler_params=pltpu.CompilerParams(vmem_limit_bytes=8 << 20),
-    )(steps, sizes, all_terms, mods, stay(w_final.T))
+    )(steps, sizes, all_terms, first_own, mods, stay(w_final.T))
     beside = lax.ppermute(masked, "col", near)
     across = lax.ppermute(masked, "col", [(i, i ^ 3) for i in range(cols)])
     return pl.pallas_call(

time: 77.4 us -> 72.7 us (0.939)
  Pallas kernels: 17.1 us -> 12.8 us
  starting transfers between devices: 5.49 us -> 6.41 us
    pallas_call x2, Pallas kernels: 7.96 us -> 5.44 us  [the longest x1 4.27 us: compact_on_device(): pl.pallas_call(mlp_kernel, out_shape=(jax.ShapeDtypeStruct((rows, tile_w,...]
    pallas_call x1, Pallas kernels: 3.52 us -> 2.05 us  [compact_on_device(): call(qkv_kernel, (rows * cols, 4, piece), bf16, [HBM_SPEC, VMEM_SPEC, HBM...]
  transfers between devices with their start and end apart: 6 -> 7, of which waited for: 1 -> 2; matrix products, arithmetic and copies ran while one was open for 0% -> 0% of each run, Pallas kernels for 8% -> 7%
where the time goes in v4:
time: 72.7 us; the launch traced here: 72.3 us
  blocking collectives  49.8 us (69%)
  Pallas kernels  12.8 us (18%)
  starting transfers between devices  6.41 us (9%)
  waiting for transfers between devices  2.49 us (3%)
  between operations  0.73 us (1%)
    all_to_all x5, blocking collectives, exchange(): return lax.all_to_all(values, axes, split_axis=0, concat_axis=0, tiled=True)  49.8 us
    pallas_call x1, Pallas kernels, compact_on_device(): pl.pallas_call(mlp_kernel, out_shape=(jax.ShapeDtypeStruct((rows, tile_w,...  4.27 us
    ppermute x1, starting transfers between devices, compact_on_device(): w_x = lax.ppermute(w_out, 'col', [(i, i ^ 2) for i in range(cols)])  2.92 us
    ppermute x1, starting transfers between devices, compact_on_device(): other = lax.ppermute(given, 'row', [(i, i ^ 1) for i in range(rows)])  2.06 us
    pallas_call x1, Pallas kernels, compact_on_device(): call(qkv_kernel, (rows * cols, 4, piece), bf16, [HBM_SPEC, VMEM_SPEC, HBM...  2.05 us
    pallas_call x1, Pallas kernels, compact_on_device(): call(attention_kernel, (rows * cols, 4, piece), bf16, [HBM_SPEC, HBM_SPEC...  1.99 us
    ppermute x1, waiting for transfers between devices, compact_on_device(): across = lax.ppermute(masked, 'col', [(i, i ^ 3) for i in range(cols)])  1.93 us
  transfers between devices with their start and end apart: 7, of which 2 were waited for; matrix products, arithmetic and copies ran while one was open for 0% of the time, Pallas kernels for 7%

profile of v4, /device:TPU:0, one launch (start us, length us, event | category | flops | bytes accessed | tf_op | source)
XLA Modules:
  0.0 72.3 jit_solution(13726301532420497525)
XLA Ops:
  0.6 0.0 copy-start
  0.6 0.5 collective-permute-start
  1.2 0.1 collective-permute-start.2
  1.2 2.9 %collective-permute-start.3 = (bf16[768,384]{1,0:T(8,128)(2,1)}, bf16[768,384]{1,0:T(8,128)(2,1)S(1)}, u32[]{:S(2)}, u32[]{:S(2)}) collective-permute-start(bf16[768,384]{1,0:T(8,128)(2,1)} %own_hbm.1), channel_id=1, source_target_pairs={{0,2},{1,3},{2,0},{3,1},{4,6},{5,7},{6,4},{7,5},{8,10},{9,11},{10,... | collective-permute-start | bytes 1769480 | tf_op jit(solution)/shard_map/ppermute | solution.py:532
  4.2 1.2 %shard_map.158 = (bf16[8,2,3072]{2,1,0:T(2,128)(2,1)S(1)}, bf16[2,128,384]{2,1,0:T(8,128)(2,1)S(1)}) custom-call(bf16[2,3072]{1,0:T(2,128)(2,1)} %states_hbm.1, bf16[128,768]{1,0:T(8,128)(2,1)} %own_k_hbm.1, bf16[128,768]{1,0:T(8,128)(2,1)} %own_v_hbm.1), custom_call_target="tpu_custom_call" | custom-call | tf_op jit(solution)/shard_map/pallas_call | solution.py:520
  5.3 2.1 %collective-permute-start.1 = (bf16[2,128,384]{2,1,0:T(8,128)(2,1)S(1)}, bf16[2,128,384]{2,1,0:T(8,128)(2,1)S(1)}, u32[]{:S(2)}, u32[]{:S(2)}) collective-permute-start(bf16[2,128,384]{2,1,0:T(8,128)(2,1)S(1)} %get-tuple-element.14), channel_id=1, source_target_pairs={{0,4},{4,0},{8,12},{12,8},{16,20},{20,16},{24,28},{28,24},{1,5},{5... | collective-permute-start | bytes 589832 | tf_op jit(solution)/shard_map/ppermute | solution.py:531
  7.4 11.8 %all_to_all.25.tokens_ref = bf16[8,2,3072]{2,1,0:T(2,128)(2,1)S(1)} all-to-all(bf16[8,2,3072]{2,1,0:T(2,128)(2,1)S(1)} %get-tuple-element.13), channel_id=1, replica_groups=mesh['row'=8,'col'=4] {'row'}, dimensions={0} | all-to-all | bytes 196608 | tf_op jit(solution)/shard_map/all_to_all | solution.py:503
  19.2 0.0 collective-permute-done.w_ref
  19.2 2.1 %shard_map.159 = bf16[32,4,384]{2,1,0:T(4,128)(2,1)S(1)} custom-call(s32[4]{0:T(128)} %step_hbm.7, bf16[8,2,3072]{2,1,0:T(2,128)(2,1)S(1)} %all_to_all.25.tokens_ref, f32[4,8,3072]{2,1,0:T(8,128)} %mod_hbm.7, bf16[3072,1152]{1,0:T(8,128)(2,1)S(1)} %collective-permute-done.w_ref), custom_call_target="tpu_custom_call" | custom-call | tf_op jit(solution)/shard_map/pallas_call | solution.py:544
  21.2 0.0 collective-permute-done.1.other_hbm
  21.3 0.0 collective-permute-done.2.w1_ref
  21.3 9.5 %all_to_all.26 = bf16[32,4,384]{2,1,0:T(4,128)(2,1)S(1)} all-to-all(bf16[32,4,384]{2,1,0:T(4,128)(2,1)S(1)} %shard_map.159), channel_id=1, replica_groups=mesh['row'=8,'col'=4] {'row','col'}, dimensions={0} | all-to-all | bytes 196608 | tf_op jit(solution)/shard_map/all_to_all | solution.py:503
  30.8 2.0 %shard_map.160 = bf16[32,4,384]{2,1,0:T(4,128)(2,1)S(1)} custom-call(s32[2,4]{1,0:T(2,128)} %bitcast.8, s32[2,4]{1,0:T(2,128)} %bitcast.10, bf16[8,4,4,384]{3,2,1,0:T(4,128)(2,1)S(1)} %bitcast.6, bf16[128,768]{1,0:T(8,128)(2,1)} %own_k_hbm.1, bf16[128,768]{1,0:T(8,128)(2,1)} %own_v_hbm.1, bf16[2,128,384]{2,1,0:T(8,128)(2,1)S(1)} %collective-permute-done.1.other_hbm, ...), custom_call_target="tpu_custom_call" | custom-call | tf_op jit(solution)/shard_map/pallas_call | solution.py:555
  32.8 0.0 collective-permute-done.3.w2_ref
  32.8 0.2 collective-permute-start.4
  33.0 9.5 %all_to_all.27.mixed_ref = bf16[32,4,384]{2,1,0:T(4,128)(2,1)S(1)} all-to-all(bf16[32,4,384]{2,1,0:T(4,128)(2,1)S(1)} %shard_map.160), channel_id=1, replica_groups=mesh['row'=8,'col'=4] {'row','col'}, dimensions={0} | all-to-all | bytes 196608 | tf_op jit(solution)/shard_map/all_to_all | solution.py:503
  42.5 0.0 collective-permute-done.4.w3_ref
  42.5 1.4 %shard_map.161 = bf16[8,16,384]{2,1,0:T(8,128)(2,1)S(1)} custom-call(s32[4]{0:T(128)} %step_hbm.7, bf16[32,4,384]{2,1,0:T(4,128)(2,1)S(1)} %all_to_all.27.mixed_ref, bf16[8,2,3072]{2,1,0:T(2,128)(2,1)S(1)} %all_to_all.25.tokens_ref, f32[4,8,3072]{2,1,0:T(8,128)} %mod_hbm.7, bf16[768,384]{1,0:T(8,128)(2,1)} %own_hbm.1, ...), custom_call_target="tpu_custom_call" | custom-call | tf_op jit(solution)/shard_map/pallas_call | solution.py:569
  43.9 9.5 %all_to_all.28.first_ref = bf16[8,16,384]{2,1,0:T(8,128)(2,1)S(1)} all-to-all(bf16[8,16,384]{2,1,0:T(8,128)(2,1)S(1)} %shard_map.161), channel_id=1, replica_groups=mesh['row'=8,'col'=4] {'row'}, dimensions={0} | all-to-all | bytes 196608 | tf_op jit(solution)/shard_map/all_to_all | solution.py:503
  53.4 0.0 copy-done
  53.4 0.0 copy-start.1
  53.4 4.3 %shard_map.162 = (bf16[8,2,3072]{2,1,0:T(2,128)(2,1)S(1)}, f32[2,3072]{1,0:T(2,128)S(1)}) custom-call(s32[4]{0:T(128)} %step_hbm.7, bf16[8,16,384]{2,1,0:T(8,128)(2,1)S(1)} %all_to_all.28.first_ref, f32[4,8,3072]{2,1,0:T(8,128)} %mod_hbm.7, bf16[3072,1536]{1,0:T(8,128)(2,1)S(1)} %copy-done, bf16[1536,3072]{1,0:T(8,128)(2,1)} %w2_hbm.1), custom_call_target="tpu_custom_call" | custom-call | tf_op jit(solution)/shard_map/pallas_call | solution.py:585
  57.6 9.5 %all_to_all.29.terms_ref = bf16[8,2,3072]{2,1,0:T(2,128)(2,1)S(1)} all-to-all(bf16[8,2,3072]{2,1,0:T(2,128)(2,1)S(1)} %get-tuple-element.20), channel_id=1, replica_groups=mesh['row'=8,'col'=4] {'row'}, dimensions={0} | all-to-all | bytes 196608 | tf_op jit(solution)/shard_map/all_to_all | solution.py:503
  67.2 1.4 %shard_map.163 = (f32[2,64]{1,0:T(2,128)S(1)}, f32[2,64]{1,0:T(2,128)S(1)}) custom-call(s32[4]{0:T(128)} %step_hbm.7, s32[2,4]{1,0:T(2,128)} %bitcast.9, bf16[8,2,3072]{2,1,0:T(2,128)(2,1)S(1)} %all_to_all.29.terms_ref, f32[2,3072]{1,0:T(2,128)S(1)} %get-tuple-element.21.first_ref, f32[4,8,3072]{2,1,0:T(8,128)} %mod_hbm.7, bf16[64,3072]{1,0:T(8,128)(2,1)} %bitcast.7), custom_call_target="tpu_custom_call" | custom-call | tf_op jit(solution)/shard_map/pallas_call | solution.py:604
  68.5 0.1 collective-permute-start.5
  68.6 0.6 collective-permute-start.6
  69.2 0.5 collective-permute-done.5.near_ref
  69.7 1.9 %collective-permute-done.6.far_ref = f32[2,64]{1,0:T(2,128)S(1)} collective-permute-done((f32[2,64]{1,0:T(2,128)S(1)}, f32[2,64]{1,0:T(2,128)S(1)}, u32[]{:S(2)}, u32[]{:S(2)}) %collective-permute-start.6) | collective-permute-done | bytes 544 | tf_op jit(solution)/shard_map/ppermute | solution.py:613
  71.7 0.0 copy-done.1
  71.7 0.6 shard_map.164
Async XLA Ops:
  0.6 52.7 %copy-start = (bf16[3072,1536]{1,0:T(8,128)(2,1)S(1)}, bf16[3072,1536]{1,0:T(8,128)(2,1)}, u32[]{:S(2)}) copy-start(bf16[3072,1536]{1,0:T(8,128)(2,1)} %w1_ref.1) | copy-start | bytes 28311556
  0.6 18.5 %collective-permute-start = (bf16[3072,1152]{1,0:T(8,128)(2,1)}, bf16[3072,1152]{1,0:T(8,128)(2,1)S(1)}, u32[]{:S(2)}, u32[]{:S(2)}) collective-permute-start(bf16[3072,1152]{1,0:T(8,128)(2,1)} %param.23), channel_id=1, source_target_pairs={{0,1},{1,0},{2,3},{3,2},{4,5},{5,4},{6,7},{7,6},{8,9},{9,8},{10,11... | collective-permute-start | bytes 21233672 | tf_op jit(solution)/shard_map/ppermute | solution.py:551
  1.2 20.1 %collective-permute-start.2 = (bf16[768,384]{1,0:T(8,128)(2,1)}, bf16[768,384]{1,0:T(8,128)(2,1)S(1)}, u32[]{:S(2)}, u32[]{:S(2)}) collective-permute-start(bf16[768,384]{1,0:T(8,128)(2,1)} %own_hbm.1), channel_id=1, source_target_pairs={{0,1},{1,0},{2,3},{3,2},{4,5},{5,4},{6,7},{7,6},{8,9},{9,8},{10,11... | collective-permute-start | bytes 1769480 | tf_op jit(solution)/shard_map/ppermute | solution.py:533
  1.2 31.5 %collective-permute-start.3 = (bf16[768,384]{1,0:T(8,128)(2,1)}, bf16[768,384]{1,0:T(8,128)(2,1)S(1)}, u32[]{:S(2)}, u32[]{:S(2)}) collective-permute-start(bf16[768,384]{1,0:T(8,128)(2,1)} %own_hbm.1), channel_id=1, source_target_pairs={{0,2},{1,3},{2,0},{3,1},{4,6},{5,7},{6,4},{7,5},{8,10},{9,11},{10,... | collective-permute-start | bytes 1769480 | tf_op jit(solution)/shard_map/ppermute | solution.py:532
  5.3 15.9 %collective-permute-start.1 = (bf16[2,128,384]{2,1,0:T(8,128)(2,1)S(1)}, bf16[2,128,384]{2,1,0:T(8,128)(2,1)S(1)}, u32[]{:S(2)}, u32[]{:S(2)}) collective-permute-start(bf16[2,128,384]{2,1,0:T(8,128)(2,1)S(1)} %get-tuple-element.14), channel_id=1, source_target_pairs={{0,4},{4,0},{8,12},{12,8},{16,20},{20,16},{24,28},{28,24},{1,5},{5... | collective-permute-start | bytes 589832 | tf_op jit(solution)/shard_map/ppermute | solution.py:531
  32.8 9.7 %collective-permute-start.4 = (bf16[768,384]{1,0:T(8,128)(2,1)S(1)}, bf16[768,384]{1,0:T(8,128)(2,1)S(1)}, u32[]{:S(2)}, u32[]{:S(2)}) collective-permute-start(bf16[768,384]{1,0:T(8,128)(2,1)S(1)} %collective-permute-done.3.w2_ref), channel_id=1, source_target_pairs={{0,1},{1,0},{2,3},{3,2},{4,5},{5,4},{6,7},{7,6},{8,9},{9,8},{10,11... | collective-permute-start | bytes 1769480 | tf_op jit(solution)/shard_map/ppermute | solution.py:567
  53.4 18.3 %copy-start.1 = (f32[2,64]{1,0:T(2,128)S(1)}, f32[2,64]{1,0:T(2,128)}, u32[]{:S(2)}) copy-start(f32[2,64]{1,0:T(2,128)} %latent_ref.1) | copy-start | bytes 1540
  68.5 1.2 %collective-permute-start.5 = (f32[2,64]{1,0:T(2,128)S(1)}, f32[2,64]{1,0:T(2,128)S(1)}, u32[]{:S(2)}, u32[]{:S(2)}) collective-permute-start(f32[2,64]{1,0:T(2,128)S(1)} %get-tuple-element.22.masked_ref), channel_id=1, source_target_pairs={{0,1},{1,0},{2,3},{3,2},{4,5},{5,4},{6,7},{7,6},{8,9},{9,8},{10,11... | collective-permute-start | bytes 1544 | tf_op jit(solution)/shard_map/ppermute | solution.py:612
  68.6 3.1 %collective-permute-start.6 = (f32[2,64]{1,0:T(2,128)S(1)}, f32[2,64]{1,0:T(2,128)S(1)}, u32[]{:S(2)}, u32[]{:S(2)}) collective-permute-start(f32[2,64]{1,0:T(2,128)S(1)} %get-tuple-element.22.masked_ref), channel_id=1, source_target_pairs={{0,3},{1,2},{2,1},{3,0},{4,7},{5,6},{6,5},{7,4},{8,11},{9,10},{10,... | collective-permute-start | bytes 1544 | tf_op jit(solution)/shard_map/ppermute | solution.py:613

commit v5 on v0

--- a/solution.py
+++ b/solution.py
@@ -1,6 +1,10 @@
+import math
+
 import jax
 import jax.numpy as jnp
 from jax import lax
+from jax.experimental import pallas as pl
+from jax.experimental.pallas import tpu as pltpu
 from jax.sharding import PartitionSpec as P
 
 REQ = 4
@@ -199,6 +203,397 @@
     return (velocity, next_latent)
 
 
+bf16 = jnp.bfloat16
+FC_PARTS = 3
+f32 = jnp.float32
+VMEM_SPEC = pl.BlockSpec(memory_space=pltpu.VMEM)
+HBM_SPEC = pl.BlockSpec(memory_space=pltpu.HBM)
+
+
+def start_copies(pairs, sems):
+    copies = [pltpu.make_async_copy(source, target, sems.at[i]) for i, (source, target) in enumerate(pairs)]
+    for copy in copies:
+        copy.start()
+    return copies
+
+
+def part_rows(hbm, index):
+    size = hbm.shape[0] // FC_PARTS
+    return hbm.at[pl.ds(index * size, size), :]
+
+
+def lane_mean(values):
+    return jnp.mean(values, -1, keepdims=True)
+
+
+def norm_rows(values):
+    centred = values - lane_mean(values)
+    return centred * lax.rsqrt(lane_mean(centred * centred) + eps_norm)
+
+
+def per_request(mod_ref, step_ref, slot, rows_each, start, size):
+    pieces = [
+        jnp.broadcast_to(mod_ref[step_ref[q], pl.ds(slot, 1), pl.ds(start, size)], (rows_each, size))
+        for q in range(REQ)
+    ]
+    row = lax.broadcasted_iota(jnp.int32, (REQ * rows_each, size), 0) // rows_each
+    whole = jnp.concatenate([pieces[0]] * REQ, 0)
+    for q in range(1, REQ):
+        whole = jnp.where(row == q, jnp.concatenate([pieces[q]] * REQ, 0), whole)
+    return whole
+
+
+def qkv_kernel(
+    step_hbm, size_hbm, offset_hbm, tokens_ref, mod_hbm, w_ref, fc2_hbm, text_k_hbm, text_v_hbm, q_gain_hbm, k_gain_hbm,
+    out_ref, fc2_ref, text_ref, turn_ref, mask_ref, states_ref, gate_ref,
+    step_ref, size_ref, offset_ref, q_gain_ref, k_gain_ref, order_ref, mod_ref, sems,
+):
+    row = lax.axis_index("row")
+    depth = order_ref.shape[1]
+    size = out_ref.shape[2]
+    here = pl.ds(pl.multiple_of(lax.rem(row, 2) * size, size), size)
+    copies = start_copies(
+        [
+            (step_hbm, step_ref),
+            (size_hbm, size_ref),
+            (offset_hbm, offset_ref),
+            (q_gain_hbm, q_gain_ref),
+            (k_gain_hbm, k_gain_ref),
+            (mod_hbm, mod_ref),
+            (text_k_hbm.at[:, here], text_ref.at[0]),
+            (text_v_hbm.at[:, here], text_ref.at[1]),
+            (part_rows(fc2_hbm, 0), fc2_ref),
+        ],
+        sems,
+    )
+    for q in range(REQ):
+        for g in range(2):
+            order_ref[4 * q + 2 * g : 4 * q + 2 * g + 2, :] = tokens_ref[REQ * g + q].astype(f32)
+    out_ref[...] = jnp.zeros_like(out_ref)
+    normed = norm_rows(order_ref[...])
+    for copy in copies[:6]:
+        copy.wait()
+    shift = per_request(mod_ref, step_ref, 0, 4, 0, depth)
+    scale = per_request(mod_ref, step_ref, 1, 4, 0, depth)
+    normed = (normed * (1.0 + scale) + shift).astype(bf16)
+    whole = jnp.dot(normed, w_ref[...], preferred_element_type=f32).astype(bf16)
+    start = pl.multiple_of(row * size, size)
+    states_ref[...] = order_ref[:, pl.ds(start, size)]
+    gate_ref[...] = per_request(mod_ref, step_ref, 2, 4, start, size)
+    turn_tables(row // 2, size_ref, offset_ref, q_gain_ref, k_gain_ref, turn_ref, mask_ref)
+    for piece in range(w_ref.shape[1] // size):
+        group = lax.rem(row * 3 + piece, 8)
+        place = lax.rem(group, 2) * 4 + group // 2
+        for q in range(REQ):
+            out_ref[8 * q + place] = whole[4 * q : 4 * q + 4, piece * size : (piece + 1) * size]
+    for copy in copies[6:]:
+        copy.wait()
+
+
+def swap_pairs(values):
+    count = values.shape[-1]
+    even = lax.rem(lax.broadcasted_iota(jnp.int32, values.shape, 1), 2) == 0
+    return jnp.where(even, pltpu.roll(values, count - 1, 1), pltpu.roll(values, 1, 1))
+
+
+def turn_tables(req, size_ref, offset_ref, q_gain_ref, k_gain_ref, turn_ref, mask_ref):
+    _, count, head = turn_ref.shape
+    token = lax.broadcasted_iota(jnp.int32, (count, 1), 0)
+    pos_h = lax.rem(token, 4) // 2
+    pos_w = (token // 4) * 2 + lax.rem(token, 2)
+    lane = lax.broadcasted_iota(jnp.int32, (count, head), 1)
+    pair = lane // 2
+    time_half = head // 16
+    axis_dim = (head - head // 8) // 2
+    half = axis_dim // 2
+    in_h = (pair >= time_half) & (pair < time_half + half)
+    index = jnp.where(in_h, pair - time_half, pair - time_half - half).astype(f32)
+    frequency = jnp.exp(index * f32(-2.0 * math.log(10000.0) / axis_dim))
+    spot = jnp.where(in_h, pos_h + offset_ref[0, req], pos_w + offset_ref[1, req]).astype(f32)
+    angle = jnp.where(pair < time_half, 0.0, spot * frequency)
+    cosine = jnp.cos(angle)
+    sine = jnp.sin(angle)
+    sine = jnp.where(lax.rem(lane, 2) == 0, -sine, sine)
+    for i, gain_ref in enumerate((q_gain_ref, k_gain_ref)):
+        gain = jnp.broadcast_to(gain_ref[...], (count, head))
+        turn_ref[2 * i] = gain * cosine
+        turn_ref[2 * i + 1] = swap_pairs(gain) * sine
+    key = lax.broadcasted_iota(jnp.int32, (count, count), 1)
+    live = (lax.rem(key, 4) // 2 < size_ref[0, req]) & ((key // 4) * 2 + lax.rem(key, 2) < size_ref[1, req])
+    mask_ref[...] = jnp.where(live, 1.0, 0.0)
+
+
+def opening_kernel(states_hbm, k_hbm, v_hbm, spread_ref, given_ref, sems):
+    size = given_ref.shape[2]
+    start = (1 - lax.rem(lax.axis_index("row"), 2)) * size
+    part = pl.ds(pl.multiple_of(start, size), size)
+    states_copy, *text_copies = start_copies(
+        [(states_hbm, spread_ref.at[0]), (k_hbm.at[:, part], given_ref.at[0]), (v_hbm.at[:, part], given_ref.at[1])], sems
+    )
+    states_copy.wait()
+    states = spread_ref[0]
+    for r in range(1, spread_ref.shape[0]):
+        spread_ref[r] = states
+    for copy in text_copies:
+        copy.wait()
+
+
+def attention_kernel(
+    rows_ref, text_ref, other_ref, turn_ref, mask_ref, w_hbm, out_ref, w_ref, q_ref, k_ref, v_ref, sems
+):
+    (w_copy,) = start_copies([(w_hbm, w_ref)], sems)
+    group = 2 * lax.axis_index("col") + lax.rem(lax.axis_index("row"), 2)
+    count, width = q_ref.shape
+    head = turn_ref.shape[2]
+    for which, ref in enumerate((q_ref, k_ref, v_ref)):
+        source = (8 * which + group) // 3
+        for s in range(4):
+            ref[4 * s : 4 * s + 4, :] = rows_ref[source, s].astype(f32)
+
+    def turned(values, which):
+        values = values * lax.rsqrt(lane_mean(values * values) + eps_norm)
+        return (values * turn_ref[2 * which] + swap_pairs(values) * turn_ref[2 * which + 1]).astype(bf16)
+
+    key_ok = mask_ref[...] > 0.0
+    contract = (((1,), (1,)), ((), ()))
+    scale = head ** (-0.5)
+    for h in range(width // head):
+        cols = slice(h * head, (h + 1) * head)
+        q = turned(q_ref[:, cols], 0)
+        k = turned(k_ref[:, cols], 1)
+        v = v_ref[:, cols].astype(bf16)
+        s_own = lax.dot_general(q, text_ref[0, :, cols], contract, preferred_element_type=f32) * scale
+        s_other = lax.dot_general(q, other_ref[0, :, cols], contract, preferred_element_type=f32) * scale
+        s_image = lax.dot_general(q, k, contract, preferred_element_type=f32) * scale
+        s_image = jnp.where(key_ok, s_image, mask_floor)
+        top = jnp.maximum(
+            jnp.max(jnp.maximum(s_own, s_other), -1, keepdims=True), jnp.max(s_image, -1, keepdims=True)
+        )
+        w_own = jnp.exp(s_own - top)
+        w_other = jnp.exp(s_other - top)
+        w_image = jnp.where(key_ok, jnp.exp(s_image - top), 0.0)
+        total = jnp.sum(w_own + w_other, -1, keepdims=True) + jnp.sum(w_image, -1, keepdims=True)
+        summed = (
+            jnp.dot(w_own.astype(bf16), text_ref[1, :, cols], preferred_element_type=f32)
+            + jnp.dot(w_other.astype(bf16), other_ref[1, :, cols], preferred_element_type=f32)
+            + jnp.dot(w_image.astype(bf16), v, preferred_element_type=f32)
+        )
+        mixed = (summed / total).astype(bf16)
+        for s in range(4):
+            for r in range(8):
+                out_ref[4 * r + s, :, cols] = mixed[4 * s : 4 * s + 4, :]
+    w_copy.wait()
+
+
+def out_kernel(mixed_ref, states_ref, gate_ref, w0_ref, w1_ref, w2_ref, w3_ref, out_ref, rows_ref):
+    col = lax.axis_index("col")
+    depth = w0_ref.shape[0]
+    piece = mixed_ref.shape[2]
+    for r in range(8):
+        for s in range(4):
+            at = (2 * s + r % 2) * piece
+            rows_ref[4 * (r // 2) : 4 * (r // 2) + 4, at : at + piece] = mixed_ref[4 * r + s].astype(f32)
+    attended = 0.0
+    for d, w_ref in enumerate((w0_ref, w1_ref, w2_ref, w3_ref)):
+        at = pl.multiple_of(jnp.bitwise_xor(col, d) * depth, depth)
+        share = rows_ref[:, pl.ds(at, depth)].astype(bf16)
+        attended = attended + jnp.dot(share, w_ref[...], preferred_element_type=f32)
+    first = (states_ref[...] + gate_ref[...] * attended).astype(bf16)
+    for r in range(8):
+        out_ref[r] = first
+
+
+def mlp_kernel(
+    step_hbm, size_hbm, first_ref, mod_hbm, w1_ref, w2a_ref, w2_hbm, final_hbm, out_ref, own_ref, final_ref, last_ref,
+    live_ref, step_ref, size_ref, rows_ref, mod_ref, w2b_ref, w2c_ref, sems,
+):
+    row = lax.axis_index("row")
+    depth = rows_ref.shape[1]
+    piece = first_ref.shape[2]
+    step_copy, size_copy, mod_copy, *w_copies = start_copies(
+        [
+            (step_hbm, step_ref),
+            (size_hbm, size_ref),
+            (mod_hbm, mod_ref),
+            (part_rows(w2_hbm, 1), w2b_ref),
+            (part_rows(w2_hbm, 2), w2c_ref),
+            (final_hbm, final_ref),
+        ],
+        sems,
+    )
+    for r in range(8):
+        rows_ref[:, r * piece : (r + 1) * piece] = first_ref[r].astype(f32)
+    normed = norm_rows(rows_ref[...])
+    step_copy.wait()
+    size_copy.wait()
+    mod_copy.wait()
+    shift = per_request(mod_ref, step_ref, 3, 4, 0, depth)
+    scale = per_request(mod_ref, step_ref, 4, 4, 0, depth)
+    normed = (normed * (1.0 + scale) + shift).astype(bf16)
+    own = rows_ref[0:2, :]
+    for q in range(REQ):
+        for g in range(2):
+            own = jnp.where(row == REQ * g + q, rows_ref[4 * q + 2 * g : 4 * q + 2 * g + 2, :], own)
+    own_ref[...] = own
+    req = lax.rem(row, REQ)
+    last_ref[...] = mod_ref[step_ref[req], 6:8, :]
+    grid_col = lax.axis_index("col") * live_ref.shape[0] + lax.broadcasted_iota(jnp.int32, live_ref.shape, 0)
+    live = (row // REQ < size_ref[0, req]) & (grid_col < size_ref[1, req])
+    live_ref[...] = jnp.where(live, 1.0, 0.0)
+    hidden = jax.nn.gelu(
+        jnp.dot(normed, w1_ref[...], preferred_element_type=f32), approximate=True
+    ).astype(bf16)
+    size = w2a_ref.shape[0]
+    added = 0.0
+    for i, w_ref in enumerate((w2a_ref, w2b_ref, w2c_ref)):
+        if i > 0:
+            w_copies[i - 1].wait()
+        added = added + jnp.dot(hidden[:, i * size : (i + 1) * size], w_ref[...], preferred_element_type=f32)
+    gate = per_request(mod_ref, step_ref, 5, 4, 0, depth)
+    term = (gate * added).astype(out_ref.dtype)
+    for q in range(REQ):
+        for g in range(2):
+            out_ref[REQ * g + q] = term[4 * q + 2 * g : 4 * q + 2 * g + 2, :]
+    w_copies[2].wait()
+
+
+def final_kernel(terms_ref, first_ref, last_ref, w_ref, live_ref, out_ref):
+    second = first_ref[...]
+    for r in range(8):
+        second = second + terms_ref[r].astype(f32)
+    normed = (norm_rows(second) * (1.0 + last_ref[1:2, :]) + last_ref[0:1, :]).astype(bf16)
+    raw = lax.dot_general(normed, w_ref[...], (((1,), (1,)), ((), ())), preferred_element_type=f32)
+    out_ref[...] = jnp.where(live_ref[...] > 0.0, raw, 0.0)
+
+
+def blend_kernel(masked_ref, live_ref, near_ref, far_ref, latent_ref, velocity_ref, next_ref):
+    col = lax.axis_index("col")
+    masked = masked_ref[...]
+    near = near_ref[...]
+    far = jnp.where((col == 1) | (col == 2), far_ref[...], 0.0)
+    odd = lax.rem(col, 2) == 1
+    count = masked.shape[0]
+    left = jnp.concatenate([jnp.where(odd, near, far)[count - 1 :, :], masked[: count - 1, :]], 0)
+    right = jnp.concatenate([masked[1:, :], jnp.where(odd, far, near)[:1, :]], 0)
+    velocity = jnp.where(live_ref[...] > 0.0, masked + blend * (left + right - 2.0 * masked), 0.0)
+    velocity_ref[...] = velocity
+    next_ref[...] = latent_ref[...] + -1.0 / STEPS * velocity
+
+
+def call(kernel, outs, specs, scratch=(), limit=8 << 20):
+    return pl.pallas_call(
+        kernel,
+        out_shape=tuple(jax.ShapeDtypeStruct(shape, dtype) for shape, dtype in outs),
+        in_specs=specs,
+        out_specs=(VMEM_SPEC,) * len(outs),
+        scratch_shapes=list(scratch),
+        compiler_params=pltpu.CompilerParams(vmem_limit_bytes=limit),
+    )
+
+
+def exchange(values, axes):
+    return lax.all_to_all(values, axes, split_axis=0, concat_axis=0, tiled=True)
+
+
+def compact_on_device(
+    image_states, latent, text_keys, text_values, mod_table, timestep, grid_size, rope_offset,
+    w_qkv, q_gain, k_gain, w_out, w_fc1, w_fc2, w_final,
+):
+    rows = lax.axis_size("row")
+    cols = lax.axis_size("col")
+    stay = lambda values: pltpu.with_memory_space_constraint(values, pltpu.HBM)
+    tile_w, width = image_states.shape
+    head = q_gain.shape[0]
+    piece = width // 8
+    tokens = rows * tile_w
+    both = ("row", "col")
+
+    near = [(i, i ^ 1) for i in range(cols)]
+    steps = stay(timestep)
+    sizes = stay(grid_size.T)
+    mods = stay(mod_table)
+    fc2 = stay(w_fc2)
+    sems = lambda count: pltpu.SemaphoreType.DMA((count,))
+    mod_space = pltpu.VMEM(mod_table.shape, f32)
+    steps_space = pltpu.SMEM(timestep.shape, jnp.int32)
+    sizes_space = pltpu.SMEM(grid_size.shape[::-1], jnp.int32)
+    gain_space = pltpu.VMEM((1, head), f32)
+    fc2_part = ((w_fc2.shape[0] // FC_PARTS, width), bf16)
+
+    spread, given = call(
+        opening_kernel,
+        [((rows, tile_w, width), bf16), ((2, text_keys.shape[0], piece), bf16)],
+        [HBM_SPEC] * 3,
+        [sems(3)],
+    )(stay(image_states), stay(text_keys), stay(text_values))
+    other = lax.ppermute(given, "row", [(i, i ^ 1) for i in range(rows)])
+    w_x = lax.ppermute(w_out, "col", [(i, i ^ 2) for i in range(cols)])
+    w_k = lax.ppermute(w_out, "col", near)
+    gathered = exchange(spread, "row")
+    half_rows = text_keys.shape[0]
+    pieces, fc2_a, text, turn, mask, states, gate = call(
+        qkv_kernel,
+        [
+            ((rows * cols, 4, piece), bf16),
+            fc2_part,
+            ((2, half_rows, piece), bf16),
+            ((4, tokens, head), f32),
+            ((tokens, tokens), f32),
+            ((tokens, piece), f32),
+            ((tokens, piece), f32),
+        ],
+        [HBM_SPEC] * 3 + [VMEM_SPEC, HBM_SPEC, VMEM_SPEC] + [HBM_SPEC] * 5,
+        [
+            steps_space,
+            sizes_space,
+            sizes_space,
+            gain_space,
+            gain_space,
+            pltpu.VMEM((tokens, width), f32),
+            mod_space,
+            sems(9),
+        ],
+    )(
+        steps, sizes, stay(rope_offset.T), gathered, mods, lax.ppermute(w_qkv, "col", near), fc2, stay(text_keys),
+        stay(text_values), stay(q_gain.reshape(1, head)), stay(k_gain.reshape(1, head)),
+    )
+    pieces, other, w_k = lax.optimization_barrier((pieces, other, w_k))
+    got = exchange(pieces, both).reshape(rows, cols, 4, piece)
+    mixed, w_own = call(
+        attention_kernel,
+        [((rows * cols, 4, piece), bf16), (w_out.shape, bf16)],
+        [VMEM_SPEC] * 5 + [HBM_SPEC],
+        [pltpu.VMEM((tokens, piece), f32)] * 3 + [sems(1)],
+    )(got, text, other, turn, mask, stay(w_out))
+    mixed, w_x = lax.optimization_barrier((mixed, w_x))
+    w_xk = lax.ppermute(w_x, "col", near)
+    all_mixed = exchange(mixed, both)
+    (first,) = call(
+        out_kernel, [((rows, tokens, piece), bf16)], [VMEM_SPEC] * 7, [pltpu.VMEM((tokens, width), f32)]
+    )(all_mixed, states, gate, w_own, w_k, w_x, w_xk)
+    all_first = exchange(first, "row")
+    terms, first_own, final_here, last, live = call(
+        mlp_kernel,
+        [
+            ((rows, tile_w, width), bf16),
+            ((tile_w, width), f32),
+            (w_final.shape[::-1], bf16),
+            ((2, width), f32),
+            (latent.shape, f32),
+        ],
+        [HBM_SPEC, HBM_SPEC, VMEM_SPEC, HBM_SPEC, VMEM_SPEC, VMEM_SPEC, HBM_SPEC, HBM_SPEC],
+        [steps_space, sizes_space, pltpu.VMEM((tokens, width), f32), mod_space]
+        + [pltpu.VMEM(*fc2_part)] * 2
+        + [sems(6)],
+        limit=16 << 20,
+    )(steps, sizes, all_first, mods, w_fc1, fc2_a, fc2, stay(w_final.T))
+    all_terms = exchange(terms, "row")
+    (masked,) = call(final_kernel, [(latent.shape, f32)], [VMEM_SPEC] * 5)(all_terms, first_own, last, final_here, live)
+    beside = lax.ppermute(masked, "col", near)
+    across = lax.ppermute(masked, "col", [(i, i ^ 3) for i in range(cols)])
+    return call(blend_kernel, [(latent.shape, f32)] * 2, [VMEM_SPEC] * 5)(masked, live, beside, across, latent)
+
+
 def solution(mesh):
     placed = (
         P(("row", "col"), None),
@@ -217,8 +612,9 @@
         P("row", None),
         P(),
     )
+    compact = mesh.shape["row"] == 2 * REQ and mesh.shape["col"] == 4
     return jax.shard_map(
-        on_device,
+        compact_on_device if compact else on_device,
         mesh=mesh,
         in_specs=placed,
         out_specs=(P(("row", "col"), None), P(("row", "col"), None)),

time: 415 us -> 69.5 us (0.17)
  waiting for transfers between devices: 211 us -> 2.45 us
  local copies, waits for them, and re-layouts: 38.6 us -> 0.02 us
  blocking collectives: 88.4 us -> 50.1 us
  other arithmetic: 24.4 us -> 0.01 us
  matrix products: 19.5 us -> 0 us
  between operations: 18 us -> 0.73 us
  Pallas kernels: 0 us -> 9.97 us
  starting transfers between devices: 11.7 us -> 5.88 us
    all_gather x3 -> x0, waiting for transfers between devices: 135 us -> none  [the longest x1 77.1 us: on_device(): lax.all_gather(w_out, 'row', axis=1, tiled=True)]
    psum x1 -> x0, waiting for transfers between devices: 66.9 us -> none  [on_device(): every_sum = lax.psum(every_term, 'row')]
    all_gather x2 -> x0, blocking collectives: 62.9 us -> none  [the longest x1 32.3 us: on_device(): lax.all_gather(normed, 'row', axis=0, tiled=True)]
    all_to_all x2 -> x5, blocking collectives: 14.6 us -> 50.1 us  [exchange(): return lax.all_to_all(values, axes, split_axis=0, concat_axis=0, tiled=True)]
    dot_general x5 -> x0, matrix products: 19.5 us -> none  [the longest x1 9.61 us: on_device(): every_term = jnp.dot(hidden, w_fc2, preferred_element_type=jnp.float32)]
    mul x10 -> x0, local copies, waits for them, and re-layouts: 18.3 us -> none  [the longest x2 5.06 us: norm_rope(): even_part * cos_wide - odd_part * sin_wide]
    unnamed x1 -> x0, blocking collectives: 11 us -> none
    pallas_call x0 -> x7, Pallas kernels: none -> 9.97 us  [the longest x1 4.01 us: compact_on_device(): call(mlp_kernel, [((rows, tile_w, width), bf16), ((tile_w, width), f32),...]
  transfers between devices with their start and end apart: 8 -> 7, of which waited for: 7 -> 2; matrix products, arithmetic and copies ran while one was open for 6% -> 0% of each run, Pallas kernels for 0% -> 7%
where the time goes in v5:
time: 69.5 us; the launch traced here: 69.1 us
  blocking collectives  50.1 us (72%)
  Pallas kernels  9.97 us (14%)
  starting transfers between devices  5.88 us (8%)
  waiting for transfers between devices  2.45 us (4%)
  between operations  0.73 us (1%)
    all_to_all x5, blocking collectives, exchange(): return lax.all_to_all(values, axes, split_axis=0, concat_axis=0, tiled=True)  50.1 us
    pallas_call x1, Pallas kernels, compact_on_device(): call(mlp_kernel, [((rows, tile_w, width), bf16), ((tile_w, width), f32),...  4.01 us
    ppermute x1, starting transfers between devices, compact_on_device(): w_x = lax.ppermute(w_out, 'col', [(i, i ^ 2) for i in range(cols)])  2.92 us
    pallas_call x1, Pallas kernels, compact_on_device(): call(qkv_kernel, [((rows * cols, 4, piece), bf16), fc2_part, ((2, half_ro...  2.45 us
    ppermute x1, waiting for transfers between devices, compact_on_device(): across = lax.ppermute(masked, 'col', [(i, i ^ 3) for i in range(cols)])  1.88 us
    ppermute x1, starting transfers between devices, compact_on_device(): other = lax.ppermute(given, 'row', [(i, i ^ 1) for i in range(rows)])  1.58 us
  transfers between devices with their start and end apart: 7, of which 2 were waited for; matrix products, arithmetic and copies ran while one was open for 0% of the time, Pallas kernels for 7%

profile of v5, /device:TPU:0, one launch (start us, length us, event | category | flops | bytes accessed | tf_op | source)
XLA Modules:
  0.0 69.1 jit_solution(7839517588431685591)
XLA Ops:
  0.6 0.5 collective-permute-start
  1.1 0.1 collective-permute-start.2
  1.2 2.9 %collective-permute-start.3 = (bf16[768,384]{1,0:T(8,128)(2,1)}, bf16[768,384]{1,0:T(8,128)(2,1)S(1)}, u32[]{:S(2)}, u32[]{:S(2)}) collective-permute-start(bf16[768,384]{1,0:T(8,128)(2,1)} %w_hbm.1), channel_id=1, source_target_pairs={{0,2},{1,3},{2,0},{3,1},{4,6},{5,7},{6,4},{7,5},{8,10},{9,11},{10,... | collective-permute-start | bytes 1769480 | tf_op jit(solution)/shard_map/ppermute | solution.py:530
  4.1 1.0 %shard_map.158 = (bf16[8,2,3072]{2,1,0:T(2,128)(2,1)S(1)}, bf16[2,128,384]{2,1,0:T(8,128)(2,1)S(1)}) custom-call(bf16[2,3072]{1,0:T(2,128)(2,1)} %states_hbm.1, bf16[128,768]{1,0:T(8,128)(2,1)} %text_k_hbm.1, bf16[128,768]{1,0:T(8,128)(2,1)} %text_v_hbm.1), custom_call_target="tpu_custom_call" | custom-call | tf_op jit(solution)/shard_map/pallas_call | solution.py:523
  5.1 1.6 %collective-permute-start.1 = (bf16[2,128,384]{2,1,0:T(8,128)(2,1)S(1)}, bf16[2,128,384]{2,1,0:T(8,128)(2,1)S(1)}, u32[]{:S(2)}, u32[]{:S(2)}) collective-permute-start(bf16[2,128,384]{2,1,0:T(8,128)(2,1)S(1)} %get-tuple-element.25), channel_id=1, source_target_pairs={{0,4},{4,0},{8,12},{12,8},{16,20},{20,16},{24,28},{28,24},{1,5},{5... | collective-permute-start | bytes 589832 | tf_op jit(solution)/shard_map/ppermute | solution.py:529
  6.7 11.8 %all_to_all.25.tokens_ref = bf16[8,2,3072]{2,1,0:T(2,128)(2,1)S(1)} all-to-all(bf16[8,2,3072]{2,1,0:T(2,128)(2,1)S(1)} %get-tuple-element.23), channel_id=1, replica_groups=mesh['row'=8,'col'=4] {'row'}, dimensions={0} | all-to-all | bytes 196608 | tf_op jit(solution)/shard_map/all_to_all | solution.py:495
  18.5 0.0 collective-permute-done.w_ref
  18.5 0.0 slice-start
  18.5 2.5 %shard_map.159 = (bf16[32,4,384]{2,1,0:T(4,128)(2,1)S(1)}, bf16[512,3072]{1,0:T(8,128)(2,1)S(1)}, bf16[2,128,384]{2,1,0:T(8,128)(2,1)S(1)}, f32[4,16,128]{2,1,0:...) custom-call(s32[4]{0:T(128)} %step_hbm.3, s32[2,4]{1,0:T(2,128)} %bitcast.10, ...), custom_call_target="tpu_custom_call" | custom-call | tf_op jit(solution)/shard_map/pallas_call | solution.py:534
  21.0 0.0 collective-permute-done.1.other_ref
  21.0 0.0 collective-permute-done.2.w1_ref
  21.0 9.8 %all_to_all.26 = bf16[32,4,384]{2,1,0:T(4,128)(2,1)S(1)} all-to-all(bf16[32,4,384]{2,1,0:T(4,128)(2,1)S(1)} %get-tuple-element.26), channel_id=1, replica_groups=mesh['row'=8,'col'=4] {'row','col'}, dimensions={0} | all-to-all | bytes 196608 | tf_op jit(solution)/shard_map/all_to_all | solution.py:495
  30.8 1.1 %shard_map.160 = (bf16[32,4,384]{2,1,0:T(4,128)(2,1)S(1)}, bf16[768,384]{1,0:T(8,128)(2,1)S(1)}) custom-call(bf16[8,4,4,384]{3,2,1,0:T(4,128)(2,1)S(1)} %bitcast.8, bf16[2,128,384]{2,1,0:T(8,128)(2,1)S(1)} %get-tuple-element.27.text_ref, bf16[2,128,384]{2,1,0:T(8,128)(2,1)S(1)} %collective-permute-done.1.other_ref, ...), custom_call_target="tpu_custom_call" | custom-call | tf_op jit(solution)/shard_map/pallas_call | solution.py:562
  31.9 0.0 collective-permute-done.3.w2_ref
  31.9 0.2 collective-permute-start.4
  32.0 9.5 %all_to_all.27.mixed_ref = bf16[32,4,384]{2,1,0:T(4,128)(2,1)S(1)} all-to-all(bf16[32,4,384]{2,1,0:T(4,128)(2,1)S(1)} %get-tuple-element.32), channel_id=1, replica_groups=mesh['row'=8,'col'=4] {'row','col'}, dimensions={0} | all-to-all | bytes 196608 | tf_op jit(solution)/shard_map/all_to_all | solution.py:495
  41.5 0.0 collective-permute-done.4.w3_ref
  41.5 0.5 shard_map.161
  42.0 9.5 %all_to_all.28.first_ref = bf16[8,16,384]{2,1,0:T(8,128)(2,1)S(1)} all-to-all(bf16[8,16,384]{2,1,0:T(8,128)(2,1)S(1)} %shard_map.161), channel_id=1, replica_groups=mesh['row'=8,'col'=4] {'row'}, dimensions={0} | all-to-all | bytes 196608 | tf_op jit(solution)/shard_map/all_to_all | solution.py:495
  51.5 0.0 slice-done
  51.5 0.0 slice-done.1
  51.5 0.0 slice-done.2
  51.5 0.0 copy-start
  51.5 4.0 %shard_map.162 = (bf16[8,2,3072]{2,1,0:T(2,128)(2,1)S(1)}, f32[2,3072]{1,0:T(2,128)S(1)}, bf16[64,3072]{1,0:T(8,128)(2,1)S(1)}, f32[2,3072]{1,0:T(2,128)S(1)}, f32[2,64]{1,0:T(2,128)S(1)}) custom-call(s32[4]{0:T(128)} %step_hbm.3, s32[2,4]{1,0:T(2,128)} %bitcast.11, bf16[8,16,384]{2,1,0:T(8,128)(2,1)S(1)} %all_to_all.28.first_ref, f32[4,8,3072]{2,1,0:T(8,128)} %mod_hbm.3, ...), custom_call_target="tpu_custom_call" | custom-call | tf_op jit(solution)/shard_map/pallas_call | solution.py:575
  55.6 9.5 %all_to_all.29.terms_ref = bf16[8,2,3072]{2,1,0:T(2,128)(2,1)S(1)} all-to-all(bf16[8,2,3072]{2,1,0:T(2,128)(2,1)S(1)} %get-tuple-element.39), channel_id=1, replica_groups=mesh['row'=8,'col'=4] {'row'}, dimensions={0} | all-to-all | bytes 196608 | tf_op jit(solution)/shard_map/all_to_all | solution.py:495
  65.1 0.4 shard_map.163.masked_ref
  65.5 0.0 collective-permute-start.5
  65.5 0.6 collective-permute-start.6
  66.1 0.6 collective-permute-done.5.near_ref
  66.7 1.9 %collective-permute-done.6.far_ref = f32[2,64]{1,0:T(2,128)S(1)} collective-permute-done((f32[2,64]{1,0:T(2,128)S(1)}, f32[2,64]{1,0:T(2,128)S(1)}, u32[]{:S(2)}, u32[]{:S(2)}) %collective-permute-start.6) | collective-permute-done | bytes 544 | tf_op jit(solution)/shard_map/ppermute | solution.py:593
  68.5 0.0 copy-done
  68.5 0.6 shard_map.164
  (3 shorter events, 0.0 us)
Async XLA Ops:
  0.6 17.9 %collective-permute-start = (bf16[3072,1152]{1,0:T(8,128)(2,1)}, bf16[3072,1152]{1,0:T(8,128)(2,1)S(1)}, u32[]{:S(2)}, u32[]{:S(2)}) collective-permute-start(bf16[3072,1152]{1,0:T(8,128)(2,1)} %param.23), channel_id=1, source_target_pairs={{0,1},{1,0},{2,3},{3,2},{4,5},{5,4},{6,7},{7,6},{8,9},{9,8},{10,11... | collective-permute-start | bytes 21233672 | tf_op jit(solution)/shard_map/ppermute | solution.py:557
  1.1 19.8 %collective-permute-start.2 = (bf16[768,384]{1,0:T(8,128)(2,1)}, bf16[768,384]{1,0:T(8,128)(2,1)S(1)}, u32[]{:S(2)}, u32[]{:S(2)}) collective-permute-start(bf16[768,384]{1,0:T(8,128)(2,1)} %w_hbm.1), channel_id=1, source_target_pairs={{0,1},{1,0},{2,3},{3,2},{4,5},{5,4},{6,7},{7,6},{8,9},{9,8},{10,11... | collective-permute-start | bytes 1769480 | tf_op jit(solution)/shard_map/ppermute | solution.py:531
  1.2 30.6 %collective-permute-start.3 = (bf16[768,384]{1,0:T(8,128)(2,1)}, bf16[768,384]{1,0:T(8,128)(2,1)S(1)}, u32[]{:S(2)}, u32[]{:S(2)}) collective-permute-start(bf16[768,384]{1,0:T(8,128)(2,1)} %w_hbm.1), channel_id=1, source_target_pairs={{0,2},{1,3},{2,0},{3,1},{4,6},{5,7},{6,4},{7,5},{8,10},{9,11},{10,... | collective-permute-start | bytes 1769480 | tf_op jit(solution)/shard_map/ppermute | solution.py:530
  5.1 15.8 %collective-permute-start.1 = (bf16[2,128,384]{2,1,0:T(8,128)(2,1)S(1)}, bf16[2,128,384]{2,1,0:T(8,128)(2,1)S(1)}, u32[]{:S(2)}, u32[]{:S(2)}) collective-permute-start(bf16[2,128,384]{2,1,0:T(8,128)(2,1)S(1)} %get-tuple-element.25), channel_id=1, source_target_pairs={{0,4},{4,0},{8,12},{12,8},{16,20},{20,16},{24,28},{28,24},{1,5},{5... | collective-permute-start | bytes 589832 | tf_op jit(solution)/shard_map/ppermute | solution.py:529
  18.5 33.0 %slice-start = ((s8[9437184]{0:T(1024)(128)(4,1)}), s8[4194304]{0:T(1024)(128)(4,1)S(1)}, s32[]{:S(2)}) async-start(s8[9437184]{0:T(1024)(128)(4,1)} %bitcast.6), calls=%async_computation.5 | async-start | bytes 8388608
  18.5 33.0 %slice-start.1 = ((s8[9437184]{0:T(1024)(128)(4,1)}), s8[4194304]{0:T(1024)(128)(4,1)S(1)}, s32[]{:S(2)}) async-start(s8[9437184]{0:T(1024)(128)(4,1)} %bitcast.6), calls=%async_computation.6 | async-start | bytes 8388608
  18.5 33.0 %slice-start.2 = ((s8[9437184]{0:T(1024)(128)(4,1)}), s8[1048576]{0:T(1024)(128)(4,1)S(1)}, s32[]{:S(2)}) async-start(s8[9437184]{0:T(1024)(128)(4,1)} %bitcast.6), calls=%async_computation.7 | async-start | bytes 2097152
  31.9 9.7 %collective-permute-start.4 = (bf16[768,384]{1,0:T(8,128)(2,1)S(1)}, bf16[768,384]{1,0:T(8,128)(2,1)S(1)}, u32[]{:S(2)}, u32[]{:S(2)}) collective-permute-start(bf16[768,384]{1,0:T(8,128)(2,1)S(1)} %collective-permute-done.3.w2_ref), channel_id=1, source_target_pairs={{0,1},{1,0},{2,3},{3,2},{4,5},{5,4},{6,7},{7,6},{8,9},{9,8},{10,11... | collective-permute-start | bytes 1769480 | tf_op jit(solution)/shard_map/ppermute | solution.py:569
  51.5 17.0 %copy-start = (f32[2,64]{1,0:T(2,128)S(1)}, f32[2,64]{1,0:T(2,128)}, u32[]{:S(2)}) copy-start(f32[2,64]{1,0:T(2,128)} %latent_ref.1) | copy-start | bytes 1540
  65.5 1.2 %collective-permute-start.5 = (f32[2,64]{1,0:T(2,128)S(1)}, f32[2,64]{1,0:T(2,128)S(1)}, u32[]{:S(2)}, u32[]{:S(2)}) collective-permute-start(f32[2,64]{1,0:T(2,128)S(1)} %shard_map.163.masked_ref), channel_id=1, source_target_pairs={{0,1},{1,0},{2,3},{3,2},{4,5},{5,4},{6,7},{7,6},{8,9},{9,8},{10,11... | collective-permute-start | bytes 1544 | tf_op jit(solution)/shard_map/ppermute | solution.py:592
  65.5 3.0 %collective-permute-start.6 = (f32[2,64]{1,0:T(2,128)S(1)}, f32[2,64]{1,0:T(2,128)S(1)}, u32[]{:S(2)}, u32[]{:S(2)}) collective-permute-start(f32[2,64]{1,0:T(2,128)S(1)} %shard_map.163.masked_ref), channel_id=1, source_target_pairs={{0,3},{1,2},{2,1},{3,0},{4,7},{5,6},{6,5},{7,4},{8,11},{9,10},{10,... | collective-permute-start | bytes 1544 | tf_op jit(solution)/shard_map/ppermute | solution.py:593

commit v6 on v5

--- a/solution.py
+++ b/solution.py
@@ -244,9 +244,8 @@
 
 
 def qkv_kernel(
-    step_hbm, size_hbm, offset_hbm, tokens_ref, mod_hbm, w_ref, fc2_hbm, text_k_hbm, text_v_hbm, q_gain_hbm, k_gain_hbm,
-    out_ref, fc2_ref, text_ref, turn_ref, mask_ref, states_ref, gate_ref,
-    step_ref, size_ref, offset_ref, q_gain_ref, k_gain_ref, order_ref, mod_ref, sems,
+    step_hbm, tokens_ref, mod_ref, w_ref, fc2_hbm, text_k_hbm, text_v_hbm, out_ref, fc2_ref, text_ref, states_ref, gate_ref,
+    step_ref, order_ref, sems,
 ):
     row = lax.axis_index("row")
     depth = order_ref.shape[1]
@@ -255,11 +254,6 @@
     copies = start_copies(
         [
             (step_hbm, step_ref),
-            (size_hbm, size_ref),
-            (offset_hbm, offset_ref),
-            (q_gain_hbm, q_gain_ref),
-            (k_gain_hbm, k_gain_ref),
-            (mod_hbm, mod_ref),
             (text_k_hbm.at[:, here], text_ref.at[0]),
             (text_v_hbm.at[:, here], text_ref.at[1]),
             (part_rows(fc2_hbm, 0), fc2_ref),
@@ -271,7 +265,7 @@
             order_ref[4 * q + 2 * g : 4 * q + 2 * g + 2, :] = tokens_ref[REQ * g + q].astype(f32)
     out_ref[...] = jnp.zeros_like(out_ref)
     normed = norm_rows(order_ref[...])
-    for copy in copies[:6]:
+    for copy in copies[:1]:
         copy.wait()
     shift = per_request(mod_ref, step_ref, 0, 4, 0, depth)
     scale = per_request(mod_ref, step_ref, 1, 4, 0, depth)
@@ -280,13 +274,12 @@
     start = pl.multiple_of(row * size, size)
     states_ref[...] = order_ref[:, pl.ds(start, size)]
     gate_ref[...] = per_request(mod_ref, step_ref, 2, 4, start, size)
-    turn_tables(row // 2, size_ref, offset_ref, q_gain_ref, k_gain_ref, turn_ref, mask_ref)
     for piece in range(w_ref.shape[1] // size):
         group = lax.rem(row * 3 + piece, 8)
         place = lax.rem(group, 2) * 4 + group // 2
         for q in range(REQ):
             out_ref[8 * q + place] = whole[4 * q : 4 * q + 4, piece * size : (piece + 1) * size]
-    for copy in copies[6:]:
+    for copy in copies[1:]:
         copy.wait()
 
 
@@ -323,12 +316,25 @@
     mask_ref[...] = jnp.where(live, 1.0, 0.0)
 
 
-def opening_kernel(states_hbm, k_hbm, v_hbm, spread_ref, given_ref, sems):
+def opening_kernel(
+    states_hbm, k_hbm, v_hbm, mod_hbm, size_hbm, offset_hbm, q_gain_hbm, k_gain_hbm,
+    spread_ref, given_ref, mod_ref, turn_ref, mask_ref, size_ref, offset_ref, q_gain_ref, k_gain_ref, sems,
+):
     size = given_ref.shape[2]
     start = (1 - lax.rem(lax.axis_index("row"), 2)) * size
     part = pl.ds(pl.multiple_of(start, size), size)
     states_copy, *text_copies = start_copies(
-        [(states_hbm, spread_ref.at[0]), (k_hbm.at[:, part], given_ref.at[0]), (v_hbm.at[:, part], given_ref.at[1])], sems
+        [
+            (states_hbm, spread_ref.at[0]),
+            (k_hbm.at[:, part], given_ref.at[0]),
+            (v_hbm.at[:, part], given_ref.at[1]),
+            (mod_hbm, mod_ref),
+            (size_hbm, size_ref),
+            (offset_hbm, offset_ref),
+            (q_gain_hbm, q_gain_ref),
+            (k_gain_hbm, k_gain_ref),
+        ],
+        sems,
     )
     states_copy.wait()
     states = spread_ref[0]
@@ -336,6 +342,7 @@
         spread_ref[r] = states
     for copy in text_copies:
         copy.wait()
+    turn_tables(lax.axis_index("row") // 2, size_ref, offset_ref, q_gain_ref, k_gain_ref, turn_ref, mask_ref)
 
 
 def attention_kernel(
@@ -404,17 +411,16 @@
 
 
 def mlp_kernel(
-    step_hbm, size_hbm, first_ref, mod_hbm, w1_ref, w2a_ref, w2_hbm, final_hbm, out_ref, own_ref, final_ref, last_ref,
-    live_ref, step_ref, size_ref, rows_ref, mod_ref, w2b_ref, w2c_ref, sems,
+    step_hbm, size_hbm, first_ref, mod_ref, w1_ref, w2a_ref, w2_hbm, final_hbm, out_ref, own_ref, final_ref, last_ref,
+    live_ref, step_ref, size_ref, rows_ref, w2b_ref, w2c_ref, sems,
 ):
     row = lax.axis_index("row")
     depth = rows_ref.shape[1]
     piece = first_ref.shape[2]
-    step_copy, size_copy, mod_copy, *w_copies = start_copies(
+    step_copy, size_copy, *w_copies = start_copies(
         [
             (step_hbm, step_ref),
             (size_hbm, size_ref),
-            (mod_hbm, mod_ref),
             (part_rows(w2_hbm, 1), w2b_ref),
             (part_rows(w2_hbm, 2), w2c_ref),
             (final_hbm, final_ref),
@@ -426,7 +432,6 @@
     normed = norm_rows(rows_ref[...])
     step_copy.wait()
     size_copy.wait()
-    mod_copy.wait()
     shift = per_request(mod_ref, step_ref, 3, 4, 0, depth)
     scale = per_request(mod_ref, step_ref, 4, 4, 0, depth)
     normed = (normed * (1.0 + scale) + shift).astype(bf16)
@@ -511,51 +516,50 @@
     near = [(i, i ^ 1) for i in range(cols)]
     steps = stay(timestep)
     sizes = stay(grid_size.T)
-    mods = stay(mod_table)
     fc2 = stay(w_fc2)
     sems = lambda count: pltpu.SemaphoreType.DMA((count,))
-    mod_space = pltpu.VMEM(mod_table.shape, f32)
     steps_space = pltpu.SMEM(timestep.shape, jnp.int32)
     sizes_space = pltpu.SMEM(grid_size.shape[::-1], jnp.int32)
     gain_space = pltpu.VMEM((1, head), f32)
     fc2_part = ((w_fc2.shape[0] // FC_PARTS, width), bf16)
 
-    spread, given = call(
+    spread, given, mods, turn, mask = call(
         opening_kernel,
-        [((rows, tile_w, width), bf16), ((2, text_keys.shape[0], piece), bf16)],
-        [HBM_SPEC] * 3,
-        [sems(3)],
-    )(stay(image_states), stay(text_keys), stay(text_values))
+        [
+            ((rows, tile_w, width), bf16),
+            ((2, text_keys.shape[0], piece), bf16),
+            (mod_table.shape, f32),
+            ((4, tokens, head), f32),
+            ((tokens, tokens), f32),
+        ],
+        [HBM_SPEC] * 8,
+        [sizes_space, sizes_space, gain_space, gain_space, sems(8)],
+    )(
+        stay(image_states), stay(text_keys), stay(text_values), stay(mod_table), sizes, stay(rope_offset.T),
+        stay(q_gain.reshape(1, head)), stay(k_gain.reshape(1, head)),
+    )
     other = lax.ppermute(given, "row", [(i, i ^ 1) for i in range(rows)])
     w_x = lax.ppermute(w_out, "col", [(i, i ^ 2) for i in range(cols)])
     w_k = lax.ppermute(w_out, "col", near)
     gathered = exchange(spread, "row")
     half_rows = text_keys.shape[0]
-    pieces, fc2_a, text, turn, mask, states, gate = call(
+    pieces, fc2_a, text, states, gate = call(
         qkv_kernel,
         [
             ((rows * cols, 4, piece), bf16),
             fc2_part,
             ((2, half_rows, piece), bf16),
-            ((4, tokens, head), f32),
-            ((tokens, tokens), f32),
             ((tokens, piece), f32),
             ((tokens, piece), f32),
         ],
-        [HBM_SPEC] * 3 + [VMEM_SPEC, HBM_SPEC, VMEM_SPEC] + [HBM_SPEC] * 5,
+        [HBM_SPEC] + [VMEM_SPEC] * 3 + [HBM_SPEC] * 3,
         [
             steps_space,
-            sizes_space,
-            sizes_space,
-            gain_space,
-            gain_space,
             pltpu.VMEM((tokens, width), f32),
-            mod_space,
-            sems(9),
+            sems(4),
         ],
     )(
-        steps, sizes, stay(rope_offset.T), gathered, mods, lax.ppermute(w_qkv, "col", near), fc2, stay(text_keys),
-        stay(text_values), stay(q_gain.reshape(1, head)), stay(k_gain.reshape(1, head)),
+        steps, gathered, mods, lax.ppermute(w_qkv, "col", near), fc2, stay(text_keys), stay(text_values),
     )
     pieces, other, w_k = lax.optimization_barrier((pieces, other, w_k))
     got = exchange(pieces, both).reshape(rows, cols, 4, piece)
@@ -581,10 +585,10 @@
             ((2, width), f32),
             (latent.shape, f32),
         ],
-        [HBM_SPEC, HBM_SPEC, VMEM_SPEC, HBM_SPEC, VMEM_SPEC, VMEM_SPEC, HBM_SPEC, HBM_SPEC],
-        [steps_space, sizes_space, pltpu.VMEM((tokens, width), f32), mod_space]
+        [HBM_SPEC, HBM_SPEC] + [VMEM_SPEC] * 4 + [HBM_SPEC, HBM_SPEC],
+        [steps_space, sizes_space, pltpu.VMEM((tokens, width), f32)]
         + [pltpu.VMEM(*fc2_part)] * 2
-        + [sems(6)],
+        + [sems(5)],
         limit=16 << 20,
     )(steps, sizes, all_first, mods, w_fc1, fc2_a, fc2, stay(w_final.T))
     all_terms = exchange(terms, "row")

time: 69.5 us -> 69.2 us (level)
  no operation moved by 1% of the time
where the time goes in v6:
time: 69.2 us; the launch traced here: 68.8 us
  blocking collectives  50.1 us (72%)
  Pallas kernels  9.65 us (14%)
  starting transfers between devices  5.88 us (8%)
  waiting for transfers between devices  2.45 us (4%)
  between operations  0.73 us (1%)
    all_to_all x5, blocking collectives, exchange(): return lax.all_to_all(values, axes, split_axis=0, concat_axis=0, tiled=True)  50.1 us
    pallas_call x1, Pallas kernels, compact_on_device(): call(mlp_kernel, [((rows, tile_w, width), bf16), ((tile_w, width), f32),...  3.61 us
    ppermute x1, starting transfers between devices, compact_on_device(): w_x = lax.ppermute(w_out, 'col', [(i, i ^ 2) for i in range(cols)])  2.92 us
    pallas_call x1, Pallas kernels, compact_on_device(): call(qkv_kernel, [((rows * cols, 4, piece), bf16), fc2_part, ((2, half_ro...  2.25 us
    ppermute x1, waiting for transfers between devices, compact_on_device(): across = lax.ppermute(masked, 'col', [(i, i ^ 3) for i in range(cols)])  1.88 us
    ppermute x1, starting transfers between devices, compact_on_device(): other = lax.ppermute(given, 'row', [(i, i ^ 1) for i in range(rows)])  1.58 us
  transfers between devices with their start and end apart: 7, of which 2 were waited for; matrix products, arithmetic and copies ran while one was open for 0% of the time, Pallas kernels for 7%

profile of v6, /device:TPU:0, one launch (start us, length us, event | category | flops | bytes accessed | tf_op | source)
XLA Modules:
  0.0 68.8 jit_solution(7301719132271128225)
XLA Ops:
  0.6 0.5 collective-permute-start
  1.1 0.1 collective-permute-start.2
  1.2 2.9 %collective-permute-start.3 = (bf16[768,384]{1,0:T(8,128)(2,1)}, bf16[768,384]{1,0:T(8,128)(2,1)S(1)}, u32[]{:S(2)}, u32[]{:S(2)}) collective-permute-start(bf16[768,384]{1,0:T(8,128)(2,1)} %w_hbm.1), channel_id=1, source_target_pairs={{0,2},{1,3},{2,0},{3,1},{4,6},{5,7},{6,4},{7,5},{8,10},{9,11},{10,... | collective-permute-start | bytes 1769480 | tf_op jit(solution)/shard_map/ppermute | solution.py:542
  4.1 1.3 %shard_map.158 = (bf16[8,2,3072]{2,1,0:T(2,128)(2,1)S(1)}, bf16[2,128,384]{2,1,0:T(8,128)(2,1)S(1)}, f32[4,8,3072]{2,1,0:T(8,128)S(1)}, f32[4,16,128]{2,1,0:T(8,128)S(1)}, f32[16,16]{1,0:T(8,128)S(1)}) custom-call(bf16[2,3072]{1,0:T(2,128)(2,1)} %states_hbm.1, bf16[128,768]{1,0:T(8,128)(2,1)} %text_k_hbm.1, bf16[128,768]{1,0:T(8,128)(2,1)} %text_v_hbm.1, ...), custom_call_target="tpu_custom_call" | custom-call | tf_op jit(solution)/shard_map/pallas_call | solution.py:526
  5.4 1.6 %collective-permute-start.1 = (bf16[2,128,384]{2,1,0:T(8,128)(2,1)S(1)}, bf16[2,128,384]{2,1,0:T(8,128)(2,1)S(1)}, u32[]{:S(2)}, u32[]{:S(2)}) collective-permute-start(bf16[2,128,384]{2,1,0:T(8,128)(2,1)S(1)} %get-tuple-element.27), channel_id=1, source_target_pairs={{0,4},{4,0},{8,12},{12,8},{16,20},{20,16},{24,28},{28,24},{1,5},{5... | collective-permute-start | bytes 589832 | tf_op jit(solution)/shard_map/ppermute | solution.py:541
  7.0 11.8 %all_to_all.25.tokens_ref = bf16[8,2,3072]{2,1,0:T(2,128)(2,1)S(1)} all-to-all(bf16[8,2,3072]{2,1,0:T(2,128)(2,1)S(1)} %get-tuple-element.24), channel_id=1, replica_groups=mesh['row'=8,'col'=4] {'row'}, dimensions={0} | all-to-all | bytes 196608 | tf_op jit(solution)/shard_map/all_to_all | solution.py:500
  18.8 0.0 collective-permute-done.w_ref
  18.8 0.0 slice-start
  18.8 2.3 %shard_map.159 = (bf16[32,4,384]{2,1,0:T(4,128)(2,1)S(1)}, bf16[512,3072]{1,0:T(8,128)(2,1)S(1)}, bf16[2,128,384]{2,1,0:T(8,128)(2,1)S(1)}, f32[16,384]{1,0:T(8,128)S(1)}, f32[16,384]{1,0:T(8,128)S(1)}) custom-call(s32[4]{0:T(128)} %step_hbm.3, bf16[8,2,3072]{2,1,0:T(2,128)(2,1)S(1)} %all_to_all.25.tokens_ref, f32[4,8,3072]{2,1,0:T(8,128)S(1)} %get-tuple-element.25.mod_ref, ...), custom_call_target="tpu_custom_call" | custom-call | tf_op jit(solution)/shard_map/pallas_call | solution.py:546
  21.1 0.0 collective-permute-done.1.other_ref
  21.1 0.0 collective-permute-done.2.w1_ref
  21.1 9.8 %all_to_all.26 = bf16[32,4,384]{2,1,0:T(4,128)(2,1)S(1)} all-to-all(bf16[32,4,384]{2,1,0:T(4,128)(2,1)S(1)} %get-tuple-element.28), channel_id=1, replica_groups=mesh['row'=8,'col'=4] {'row','col'}, dimensions={0} | all-to-all | bytes 196608 | tf_op jit(solution)/shard_map/all_to_all | solution.py:500
  30.9 1.1 %shard_map.160 = (bf16[32,4,384]{2,1,0:T(4,128)(2,1)S(1)}, bf16[768,384]{1,0:T(8,128)(2,1)S(1)}) custom-call(bf16[8,4,4,384]{3,2,1,0:T(4,128)(2,1)S(1)} %bitcast.8, bf16[2,128,384]{2,1,0:T(8,128)(2,1)S(1)} %get-tuple-element.29.text_ref, bf16[2,128,384]{2,1,0:T(8,128)(2,1)S(1)} %collective-permute-done.1.other_ref, ...), custom_call_target="tpu_custom_call" | custom-call | tf_op jit(solution)/shard_map/pallas_call | solution.py:566
  31.9 0.0 collective-permute-done.3.w2_ref
  32.0 0.2 collective-permute-start.4
  32.1 9.5 %all_to_all.27.mixed_ref = bf16[32,4,384]{2,1,0:T(4,128)(2,1)S(1)} all-to-all(bf16[32,4,384]{2,1,0:T(4,128)(2,1)S(1)} %get-tuple-element.34), channel_id=1, replica_groups=mesh['row'=8,'col'=4] {'row','col'}, dimensions={0} | all-to-all | bytes 196608 | tf_op jit(solution)/shard_map/all_to_all | solution.py:500
  41.6 0.0 collective-permute-done.4.w3_ref
  41.6 0.4 shard_map.161
  42.1 9.5 %all_to_all.28.first_ref = bf16[8,16,384]{2,1,0:T(8,128)(2,1)S(1)} all-to-all(bf16[8,16,384]{2,1,0:T(8,128)(2,1)S(1)} %shard_map.161), channel_id=1, replica_groups=mesh['row'=8,'col'=4] {'row'}, dimensions={0} | all-to-all | bytes 196608 | tf_op jit(solution)/shard_map/all_to_all | solution.py:500
  51.6 0.0 slice-done
  51.6 0.0 slice-done.1
  51.6 0.0 slice-done.2
  51.6 0.0 copy-start
  51.6 3.6 %shard_map.162 = (bf16[8,2,3072]{2,1,0:T(2,128)(2,1)S(1)}, f32[2,3072]{1,0:T(2,128)S(1)}, bf16[64,3072]{1,0:T(8,128)(2,1)S(1)}, f32[2,3072]{1,0:T(2,128)S(1)}, f32[2,64]{1,0:T(2,128)S(1)}) custom-call(s32[4]{0:T(128)} %step_hbm.3, s32[2,4]{1,0:T(2,128)} %bitcast.11, bf16[8,16,384]{2,1,0:T(8,128)(2,1)S(1)} %all_to_all.28.first_ref, ...), custom_call_target="tpu_custom_call" | custom-call | tf_op jit(solution)/shard_map/pallas_call | solution.py:579
  55.3 9.5 %all_to_all.29.terms_ref = bf16[8,2,3072]{2,1,0:T(2,128)(2,1)S(1)} all-to-all(bf16[8,2,3072]{2,1,0:T(2,128)(2,1)S(1)} %get-tuple-element.41), channel_id=1, replica_groups=mesh['row'=8,'col'=4] {'row'}, dimensions={0} | all-to-all | bytes 196608 | tf_op jit(solution)/shard_map/all_to_all | solution.py:500
  64.8 0.4 shard_map.163.masked_ref
  65.2 0.0 collective-permute-start.5
  65.2 0.6 collective-permute-start.6
  65.8 0.6 collective-permute-done.5.near_ref
  66.3 1.9 %collective-permute-done.6.far_ref = f32[2,64]{1,0:T(2,128)S(1)} collective-permute-done((f32[2,64]{1,0:T(2,128)S(1)}, f32[2,64]{1,0:T(2,128)S(1)}, u32[]{:S(2)}, u32[]{:S(2)}) %collective-permute-start.6) | collective-permute-done | bytes 544 | tf_op jit(solution)/shard_map/ppermute | solution.py:597
  68.2 0.0 copy-done
  68.2 0.6 shard_map.164
  (3 shorter events, 0.0 us)
Async XLA Ops:
  0.6 18.2 %collective-permute-start = (bf16[3072,1152]{1,0:T(8,128)(2,1)}, bf16[3072,1152]{1,0:T(8,128)(2,1)S(1)}, u32[]{:S(2)}, u32[]{:S(2)}) collective-permute-start(bf16[3072,1152]{1,0:T(8,128)(2,1)} %param.23), channel_id=1, source_target_pairs={{0,1},{1,0},{2,3},{3,2},{4,5},{5,4},{6,7},{7,6},{8,9},{9,8},{10,11... | collective-permute-start | bytes 21233672 | tf_op jit(solution)/shard_map/ppermute | solution.py:562
  1.1 19.9 %collective-permute-start.2 = (bf16[768,384]{1,0:T(8,128)(2,1)}, bf16[768,384]{1,0:T(8,128)(2,1)S(1)}, u32[]{:S(2)}, u32[]{:S(2)}) collective-permute-start(bf16[768,384]{1,0:T(8,128)(2,1)} %w_hbm.1), channel_id=1, source_target_pairs={{0,1},{1,0},{2,3},{3,2},{4,5},{5,4},{6,7},{7,6},{8,9},{9,8},{10,11... | collective-permute-start | bytes 1769480 | tf_op jit(solution)/shard_map/ppermute | solution.py:543
  1.2 30.7 %collective-permute-start.3 = (bf16[768,384]{1,0:T(8,128)(2,1)}, bf16[768,384]{1,0:T(8,128)(2,1)S(1)}, u32[]{:S(2)}, u32[]{:S(2)}) collective-permute-start(bf16[768,384]{1,0:T(8,128)(2,1)} %w_hbm.1), channel_id=1, source_target_pairs={{0,2},{1,3},{2,0},{3,1},{4,6},{5,7},{6,4},{7,5},{8,10},{9,11},{10,... | collective-permute-start | bytes 1769480 | tf_op jit(solution)/shard_map/ppermute | solution.py:542
  5.4 15.6 %collective-permute-start.1 = (bf16[2,128,384]{2,1,0:T(8,128)(2,1)S(1)}, bf16[2,128,384]{2,1,0:T(8,128)(2,1)S(1)}, u32[]{:S(2)}, u32[]{:S(2)}) collective-permute-start(bf16[2,128,384]{2,1,0:T(8,128)(2,1)S(1)} %get-tuple-element.27), channel_id=1, source_target_pairs={{0,4},{4,0},{8,12},{12,8},{16,20},{20,16},{24,28},{28,24},{1,5},{5... | collective-permute-start | bytes 589832 | tf_op jit(solution)/shard_map/ppermute | solution.py:541
  18.8 32.8 %slice-start = ((s8[9437184]{0:T(1024)(128)(4,1)}), s8[4194304]{0:T(1024)(128)(4,1)S(1)}, s32[]{:S(2)}) async-start(s8[9437184]{0:T(1024)(128)(4,1)} %bitcast.6), calls=%async_computation.5 | async-start | bytes 8388608
  18.8 32.8 %slice-start.1 = ((s8[9437184]{0:T(1024)(128)(4,1)}), s8[4194304]{0:T(1024)(128)(4,1)S(1)}, s32[]{:S(2)}) async-start(s8[9437184]{0:T(1024)(128)(4,1)} %bitcast.6), calls=%async_computation.6 | async-start | bytes 8388608
  18.8 32.8 %slice-start.2 = ((s8[9437184]{0:T(1024)(128)(4,1)}), s8[1048576]{0:T(1024)(128)(4,1)S(1)}, s32[]{:S(2)}) async-start(s8[9437184]{0:T(1024)(128)(4,1)} %bitcast.6), calls=%async_computation.7 | async-start | bytes 2097152
  32.0 9.7 %collective-permute-start.4 = (bf16[768,384]{1,0:T(8,128)(2,1)S(1)}, bf16[768,384]{1,0:T(8,128)(2,1)S(1)}, u32[]{:S(2)}, u32[]{:S(2)}) collective-permute-start(bf16[768,384]{1,0:T(8,128)(2,1)S(1)} %collective-permute-done.3.w2_ref), channel_id=1, source_target_pairs={{0,1},{1,0},{2,3},{3,2},{4,5},{5,4},{6,7},{7,6},{8,9},{9,8},{10,11... | collective-permute-start | bytes 1769480 | tf_op jit(solution)/shard_map/ppermute | solution.py:573
  51.6 16.6 %copy-start = (f32[2,64]{1,0:T(2,128)S(1)}, f32[2,64]{1,0:T(2,128)}, u32[]{:S(2)}) copy-start(f32[2,64]{1,0:T(2,128)} %latent_ref.1) | copy-start | bytes 1540
  65.2 1.2 %collective-permute-start.5 = (f32[2,64]{1,0:T(2,128)S(1)}, f32[2,64]{1,0:T(2,128)S(1)}, u32[]{:S(2)}, u32[]{:S(2)}) collective-permute-start(f32[2,64]{1,0:T(2,128)S(1)} %shard_map.163.masked_ref), channel_id=1, source_target_pairs={{0,1},{1,0},{2,3},{3,2},{4,5},{5,4},{6,7},{7,6},{8,9},{9,8},{10,11... | collective-permute-start | bytes 1544 | tf_op jit(solution)/shard_map/ppermute | solution.py:596
  65.2 3.0 %collective-permute-start.6 = (f32[2,64]{1,0:T(2,128)S(1)}, f32[2,64]{1,0:T(2,128)S(1)}, u32[]{:S(2)}, u32[]{:S(2)}) collective-permute-start(f32[2,64]{1,0:T(2,128)S(1)} %shard_map.163.masked_ref), channel_id=1, source_target_pairs={{0,3},{1,2},{2,1},{3,0},{4,7},{5,6},{6,5},{7,4},{8,11},{9,10},{10,... | collective-permute-start | bytes 1544 | tf_op jit(solution)/shard_map/ppermute | solution.py:597

commit v7 on v6

--- a/solution.py
+++ b/solution.py
@@ -276,9 +276,9 @@
     gate_ref[...] = per_request(mod_ref, step_ref, 2, 4, start, size)
     for piece in range(w_ref.shape[1] // size):
         group = lax.rem(row * 3 + piece, 8)
-        place = lax.rem(group, 2) * 4 + group // 2
+        place = (group // 2) * 8 + lax.rem(group, 2)
         for q in range(REQ):
-            out_ref[8 * q + place] = whole[4 * q : 4 * q + 4, piece * size : (piece + 1) * size]
+            out_ref[2 * q + place] = whole[4 * q : 4 * q + 4, piece * size : (piece + 1) * size]
     for copy in copies[1:]:
         copy.wait()
 
@@ -355,7 +355,7 @@
     for which, ref in enumerate((q_ref, k_ref, v_ref)):
         source = (8 * which + group) // 3
         for s in range(4):
-            ref[4 * s : 4 * s + 4, :] = rows_ref[source, s].astype(f32)
+            ref[4 * s : 4 * s + 4, :] = rows_ref[s, source].astype(f32)
 
     def turned(values, which):
         values = values * lax.rsqrt(lane_mean(values * values) + eps_norm)
@@ -388,7 +388,7 @@
         mixed = (summed / total).astype(bf16)
         for s in range(4):
             for r in range(8):
-                out_ref[4 * r + s, :, cols] = mixed[4 * s : 4 * s + 4, :]
+                out_ref[8 * s + r, :, cols] = mixed[4 * s : 4 * s + 4, :]
     w_copy.wait()
 
 
@@ -399,7 +399,7 @@
     for r in range(8):
         for s in range(4):
             at = (2 * s + r % 2) * piece
-            rows_ref[4 * (r // 2) : 4 * (r // 2) + 4, at : at + piece] = mixed_ref[4 * r + s].astype(f32)
+            rows_ref[4 * (r // 2) : 4 * (r // 2) + 4, at : at + piece] = mixed_ref[8 * s + r].astype(f32)
     attended = 0.0
     for d, w_ref in enumerate((w0_ref, w1_ref, w2_ref, w3_ref)):
         at = pl.multiple_of(jnp.bitwise_xor(col, d) * depth, depth)
@@ -511,7 +511,7 @@
     head = q_gain.shape[0]
     piece = width // 8
     tokens = rows * tile_w
-    both = ("row", "col")
+    both = ("col", "row")
 
     near = [(i, i ^ 1) for i in range(cols)]
     steps = stay(timestep)
@@ -562,7 +562,7 @@
         steps, gathered, mods, lax.ppermute(w_qkv, "col", near), fc2, stay(text_keys), stay(text_values),
     )
     pieces, other, w_k = lax.optimization_barrier((pieces, other, w_k))
-    got = exchange(pieces, both).reshape(rows, cols, 4, piece)
+    got = exchange(pieces, both).reshape(cols, rows, 4, piece)
     mixed, w_own = call(
         attention_kernel,
         [((rows * cols, 4, piece), bf16), (w_out.shape, bf16)],

time: 69.2 us -> 68.8 us (level)
  no operation moved by 1% of the time
where the time goes in v7:
time: 68.8 us; the launch traced here: 68.5 us
  blocking collectives  49.7 us (72%)
  Pallas kernels  9.65 us (14%)
  starting transfers between devices  6.06 us (9%)
  waiting for transfers between devices  2.27 us (3%)
  between operations  0.73 us (1%)
    all_to_all x5, blocking collectives, exchange(): return lax.all_to_all(values, axes, split_axis=0, concat_axis=0, tiled=True)  49.7 us
    pallas_call x1, Pallas kernels, compact_on_device(): call(mlp_kernel, [((rows, tile_w, width), bf16), ((tile_w, width), f32),...  3.61 us
    ppermute x1, starting transfers between devices, compact_on_device(): w_x = lax.ppermute(w_out, 'col', [(i, i ^ 2) for i in range(cols)])  2.92 us
    pallas_call x1, Pallas kernels, compact_on_device(): call(qkv_kernel, [((rows * cols, 4, piece), bf16), fc2_part, ((2, half_ro...  2.25 us
    ppermute x1, waiting for transfers between devices, compact_on_device(): across = lax.ppermute(masked, 'col', [(i, i ^ 3) for i in range(cols)])  1.88 us
    ppermute x1, starting transfers between devices, compact_on_device(): other = lax.ppermute(given, 'row', [(i, i ^ 1) for i in range(rows)])  1.58 us
  transfers between devices with their start and end apart: 7, of which 2 were waited for; matrix products, arithmetic and copies ran while one was open for 0% of the time, Pallas kernels for 7%

profile of v7, /device:TPU:0, one launch (start us, length us, event | category | flops | bytes accessed | tf_op | source)
XLA Modules:
  0.0 68.5 jit_solution(1588152253311509796)
XLA Ops:
  0.6 0.5 collective-permute-start
  1.1 0.1 collective-permute-start.2
  1.2 2.9 %collective-permute-start.3 = (bf16[768,384]{1,0:T(8,128)(2,1)}, bf16[768,384]{1,0:T(8,128)(2,1)S(1)}, u32[]{:S(2)}, u32[]{:S(2)}) collective-permute-start(bf16[768,384]{1,0:T(8,128)(2,1)} %w_hbm.1), channel_id=1, source_target_pairs={{0,2},{1,3},{2,0},{3,1},{4,6},{5,7},{6,4},{7,5},{8,10},{9,11},{10,... | collective-permute-start | bytes 1769480 | tf_op jit(solution)/shard_map/ppermute | solution.py:542
  4.1 1.3 %shard_map.158 = (bf16[8,2,3072]{2,1,0:T(2,128)(2,1)S(1)}, bf16[2,128,384]{2,1,0:T(8,128)(2,1)S(1)}, f32[4,8,3072]{2,1,0:T(8,128)S(1)}, f32[4,16,128]{2,1,0:T(8,128)S(1)}, f32[16,16]{1,0:T(8,128)S(1)}) custom-call(bf16[2,3072]{1,0:T(2,128)(2,1)} %states_hbm.1, bf16[128,768]{1,0:T(8,128)(2,1)} %text_k_hbm.1, bf16[128,768]{1,0:T(8,128)(2,1)} %text_v_hbm.1, ...), custom_call_target="tpu_custom_call" | custom-call | tf_op jit(solution)/shard_map/pallas_call | solution.py:526
  5.4 1.6 %collective-permute-start.1 = (bf16[2,128,384]{2,1,0:T(8,128)(2,1)S(1)}, bf16[2,128,384]{2,1,0:T(8,128)(2,1)S(1)}, u32[]{:S(2)}, u32[]{:S(2)}) collective-permute-start(bf16[2,128,384]{2,1,0:T(8,128)(2,1)S(1)} %get-tuple-element.27), channel_id=1, source_target_pairs={{0,4},{4,0},{8,12},{12,8},{16,20},{20,16},{24,28},{28,24},{1,5},{5... | collective-permute-start | bytes 589832 | tf_op jit(solution)/shard_map/ppermute | solution.py:541
  7.0 11.8 %all_to_all.25.tokens_ref = bf16[8,2,3072]{2,1,0:T(2,128)(2,1)S(1)} all-to-all(bf16[8,2,3072]{2,1,0:T(2,128)(2,1)S(1)} %get-tuple-element.24), channel_id=1, replica_groups=mesh['row'=8,'col'=4] {'row'}, dimensions={0} | all-to-all | bytes 196608 | tf_op jit(solution)/shard_map/all_to_all | solution.py:500
  18.8 0.0 collective-permute-done.w_ref
  18.8 0.0 slice-start
  18.8 2.3 %shard_map.159 = (bf16[32,4,384]{2,1,0:T(4,128)(2,1)S(1)}, bf16[512,3072]{1,0:T(8,128)(2,1)S(1)}, bf16[2,128,384]{2,1,0:T(8,128)(2,1)S(1)}, f32[16,384]{1,0:T(8,128)S(1)}, f32[16,384]{1,0:T(8,128)S(1)}) custom-call(s32[4]{0:T(128)} %step_hbm.3, bf16[8,2,3072]{2,1,0:T(2,128)(2,1)S(1)} %all_to_all.25.tokens_ref, f32[4,8,3072]{2,1,0:T(8,128)S(1)} %get-tuple-element.25.mod_ref, ...), custom_call_target="tpu_custom_call" | custom-call | tf_op jit(solution)/shard_map/pallas_call | solution.py:546
  21.1 0.0 collective-permute-done.1.other_ref
  21.1 0.0 collective-permute-done.2.w1_ref
  21.1 9.5 %all_to_all.26 = bf16[32,4,384]{2,1,0:T(4,128)(2,1)S(1)} all-to-all(bf16[32,4,384]{2,1,0:T(4,128)(2,1)S(1)} %get-tuple-element.28), channel_id=1, replica_groups=mesh['row'=8,'col'=4] {'col','row'}, dimensions={0} | all-to-all | bytes 196608 | tf_op jit(solution)/shard_map/all_to_all | solution.py:500
  30.6 1.1 %shard_map.160 = (bf16[32,4,384]{2,1,0:T(4,128)(2,1)S(1)}, bf16[768,384]{1,0:T(8,128)(2,1)S(1)}) custom-call(bf16[4,8,4,384]{3,2,1,0:T(4,128)(2,1)S(1)} %bitcast.8, bf16[2,128,384]{2,1,0:T(8,128)(2,1)S(1)} %get-tuple-element.29.text_ref, bf16[2,128,384]{2,1,0:T(8,128)(2,1)S(1)} %collective-permute-done.1.other_ref, ...), custom_call_target="tpu_custom_call" | custom-call | tf_op jit(solution)/shard_map/pallas_call | solution.py:566
  31.7 0.0 collective-permute-done.3.w2_ref
  31.7 0.2 collective-permute-start.4
  31.9 9.2 %all_to_all.27.mixed_ref = bf16[32,4,384]{2,1,0:T(4,128)(2,1)S(1)} all-to-all(bf16[32,4,384]{2,1,0:T(4,128)(2,1)S(1)} %get-tuple-element.34), channel_id=1, replica_groups=mesh['row'=8,'col'=4] {'col','row'}, dimensions={0} | all-to-all | bytes 196608 | tf_op jit(solution)/shard_map/all_to_all | solution.py:500
  41.1 0.0 collective-permute-done.4.w3_ref
  41.1 0.4 shard_map.161
  41.6 9.7 %all_to_all.28.first_ref = bf16[8,16,384]{2,1,0:T(8,128)(2,1)S(1)} all-to-all(bf16[8,16,384]{2,1,0:T(8,128)(2,1)S(1)} %shard_map.161), channel_id=1, replica_groups=mesh['row'=8,'col'=4] {'row'}, dimensions={0} | all-to-all | bytes 196608 | tf_op jit(solution)/shard_map/all_to_all | solution.py:500
  51.3 0.0 slice-done
  51.3 0.0 slice-done.1
  51.3 0.0 slice-done.2
  51.3 0.0 copy-start
  51.3 3.6 %shard_map.162 = (bf16[8,2,3072]{2,1,0:T(2,128)(2,1)S(1)}, f32[2,3072]{1,0:T(2,128)S(1)}, bf16[64,3072]{1,0:T(8,128)(2,1)S(1)}, f32[2,3072]{1,0:T(2,128)S(1)}, f32[2,64]{1,0:T(2,128)S(1)}) custom-call(s32[4]{0:T(128)} %step_hbm.3, s32[2,4]{1,0:T(2,128)} %bitcast.11, bf16[8,16,384]{2,1,0:T(8,128)(2,1)S(1)} %all_to_all.28.first_ref, ...), custom_call_target="tpu_custom_call" | custom-call | tf_op jit(solution)/shard_map/pallas_call | solution.py:579
  54.9 9.5 %all_to_all.29.terms_ref = bf16[8,2,3072]{2,1,0:T(2,128)(2,1)S(1)} all-to-all(bf16[8,2,3072]{2,1,0:T(2,128)(2,1)S(1)} %get-tuple-element.41), channel_id=1, replica_groups=mesh['row'=8,'col'=4] {'row'}, dimensions={0} | all-to-all | bytes 196608 | tf_op jit(solution)/shard_map/all_to_all | solution.py:500
  64.4 0.4 shard_map.163.masked_ref
  64.8 0.0 collective-permute-start.5
  64.8 0.8 %collective-permute-start.6 = (f32[2,64]{1,0:T(2,128)S(1)}, f32[2,64]{1,0:T(2,128)S(1)}, u32[]{:S(2)}, u32[]{:S(2)}) collective-permute-start(f32[2,64]{1,0:T(2,128)S(1)} %shard_map.163.masked_ref), channel_id=1, source_target_pairs={{0,3},{1,2},{2,1},{3,0},{4,7},{5,6},{6,5},{7,4},{8,11},{9,10},{10,... | collective-permute-start | bytes 1544 | tf_op jit(solution)/shard_map/ppermute | solution.py:597
  65.6 0.4 collective-permute-done.5.near_ref
  66.0 1.9 %collective-permute-done.6.far_ref = f32[2,64]{1,0:T(2,128)S(1)} collective-permute-done((f32[2,64]{1,0:T(2,128)S(1)}, f32[2,64]{1,0:T(2,128)S(1)}, u32[]{:S(2)}, u32[]{:S(2)}) %collective-permute-start.6) | collective-permute-done | bytes 544 | tf_op jit(solution)/shard_map/ppermute | solution.py:597
  67.9 0.0 copy-done
  67.9 0.6 shard_map.164
  (3 shorter events, 0.0 us)
Async XLA Ops:
  0.6 18.2 %collective-permute-start = (bf16[3072,1152]{1,0:T(8,128)(2,1)}, bf16[3072,1152]{1,0:T(8,128)(2,1)S(1)}, u32[]{:S(2)}, u32[]{:S(2)}) collective-permute-start(bf16[3072,1152]{1,0:T(8,128)(2,1)} %param.23), channel_id=1, source_target_pairs={{0,1},{1,0},{2,3},{3,2},{4,5},{5,4},{6,7},{7,6},{8,9},{9,8},{10,11... | collective-permute-start | bytes 21233672 | tf_op jit(solution)/shard_map/ppermute | solution.py:562
  1.1 19.9 %collective-permute-start.2 = (bf16[768,384]{1,0:T(8,128)(2,1)}, bf16[768,384]{1,0:T(8,128)(2,1)S(1)}, u32[]{:S(2)}, u32[]{:S(2)}) collective-permute-start(bf16[768,384]{1,0:T(8,128)(2,1)} %w_hbm.1), channel_id=1, source_target_pairs={{0,1},{1,0},{2,3},{3,2},{4,5},{5,4},{6,7},{7,6},{8,9},{9,8},{10,11... | collective-permute-start | bytes 1769480 | tf_op jit(solution)/shard_map/ppermute | solution.py:543
  1.2 30.5 %collective-permute-start.3 = (bf16[768,384]{1,0:T(8,128)(2,1)}, bf16[768,384]{1,0:T(8,128)(2,1)S(1)}, u32[]{:S(2)}, u32[]{:S(2)}) collective-permute-start(bf16[768,384]{1,0:T(8,128)(2,1)} %w_hbm.1), channel_id=1, source_target_pairs={{0,2},{1,3},{2,0},{3,1},{4,6},{5,7},{6,4},{7,5},{8,10},{9,11},{10,... | collective-permute-start | bytes 1769480 | tf_op jit(solution)/shard_map/ppermute | solution.py:542
  5.4 15.6 %collective-permute-start.1 = (bf16[2,128,384]{2,1,0:T(8,128)(2,1)S(1)}, bf16[2,128,384]{2,1,0:T(8,128)(2,1)S(1)}, u32[]{:S(2)}, u32[]{:S(2)}) collective-permute-start(bf16[2,128,384]{2,1,0:T(8,128)(2,1)S(1)} %get-tuple-element.27), channel_id=1, source_target_pairs={{0,4},{4,0},{8,12},{12,8},{16,20},{20,16},{24,28},{28,24},{1,5},{5... | collective-permute-start | bytes 589832 | tf_op jit(solution)/shard_map/ppermute | solution.py:541
  18.8 32.5 %slice-start = ((s8[9437184]{0:T(1024)(128)(4,1)}), s8[4194304]{0:T(1024)(128)(4,1)S(1)}, s32[]{:S(2)}) async-start(s8[9437184]{0:T(1024)(128)(4,1)} %bitcast.6), calls=%async_computation.5 | async-start | bytes 8388608
  18.8 32.5 %slice-start.1 = ((s8[9437184]{0:T(1024)(128)(4,1)}), s8[4194304]{0:T(1024)(128)(4,1)S(1)}, s32[]{:S(2)}) async-start(s8[9437184]{0:T(1024)(128)(4,1)} %bitcast.6), calls=%async_computation.6 | async-start | bytes 8388608
  18.8 32.5 %slice-start.2 = ((s8[9437184]{0:T(1024)(128)(4,1)}), s8[1048576]{0:T(1024)(128)(4,1)S(1)}, s32[]{:S(2)}) async-start(s8[9437184]{0:T(1024)(128)(4,1)} %bitcast.6), calls=%async_computation.7 | async-start | bytes 2097152
  31.7 9.4 %collective-permute-start.4 = (bf16[768,384]{1,0:T(8,128)(2,1)S(1)}, bf16[768,384]{1,0:T(8,128)(2,1)S(1)}, u32[]{:S(2)}, u32[]{:S(2)}) collective-permute-start(bf16[768,384]{1,0:T(8,128)(2,1)S(1)} %collective-permute-done.3.w2_ref), channel_id=1, source_target_pairs={{0,1},{1,0},{2,3},{3,2},{4,5},{5,4},{6,7},{7,6},{8,9},{9,8},{10,11... | collective-permute-start | bytes 1769480 | tf_op jit(solution)/shard_map/ppermute | solution.py:573
  51.3 16.6 %copy-start = (f32[2,64]{1,0:T(2,128)S(1)}, f32[2,64]{1,0:T(2,128)}, u32[]{:S(2)}) copy-start(f32[2,64]{1,0:T(2,128)} %latent_ref.1) | copy-start | bytes 1540
  64.8 1.2 %collective-permute-start.5 = (f32[2,64]{1,0:T(2,128)S(1)}, f32[2,64]{1,0:T(2,128)S(1)}, u32[]{:S(2)}, u32[]{:S(2)}) collective-permute-start(f32[2,64]{1,0:T(2,128)S(1)} %shard_map.163.masked_ref), channel_id=1, source_target_pairs={{0,1},{1,0},{2,3},{3,2},{4,5},{5,4},{6,7},{7,6},{8,9},{9,8},{10,11... | collective-permute-start | bytes 1544 | tf_op jit(solution)/shard_map/ppermute | solution.py:596
  64.8 3.0 %collective-permute-start.6 = (f32[2,64]{1,0:T(2,128)S(1)}, f32[2,64]{1,0:T(2,128)S(1)}, u32[]{:S(2)}, u32[]{:S(2)}) collective-permute-start(f32[2,64]{1,0:T(2,128)S(1)} %shard_map.163.masked_ref), channel_id=1, source_target_pairs={{0,3},{1,2},{2,1},{3,0},{4,7},{5,6},{6,5},{7,4},{8,11},{9,10},{10,... | collective-permute-start | bytes 1544 | tf_op jit(solution)/shard_map/ppermute | solution.py:597

commit v8 on v7

--- a/solution.py
+++ b/solution.py
@@ -232,14 +232,12 @@
 
 
 def per_request(mod_ref, step_ref, slot, rows_each, start, size):
-    pieces = [
-        jnp.broadcast_to(mod_ref[step_ref[q], pl.ds(slot, 1), pl.ds(start, size)], (rows_each, size))
-        for q in range(REQ)
-    ]
-    row = lax.broadcasted_iota(jnp.int32, (REQ * rows_each, size), 0) // rows_each
-    whole = jnp.concatenate([pieces[0]] * REQ, 0)
-    for q in range(1, REQ):
-        whole = jnp.where(row == q, jnp.concatenate([pieces[q]] * REQ, 0), whole)
+    shape = (REQ * rows_each, size)
+    row = lax.broadcasted_iota(jnp.int32, shape, 0) // rows_each
+    whole = None
+    for q in range(REQ):
+        vector = jnp.broadcast_to(mod_ref[step_ref[q], pl.ds(slot, 1), pl.ds(start, size)], shape)
+        whole = vector if whole is None else jnp.where(row == q, vector, whole)
     return whole
 
 

time: 68.8 us -> 68.8 us (level)
  no operation moved by 1% of the time
where the time goes in v8:
time: 68.8 us; the launch traced here: 68.5 us
  blocking collectives  49.7 us (72%)
  Pallas kernels  9.65 us (14%)
  starting transfers between devices  6.06 us (9%)
  waiting for transfers between devices  2.27 us (3%)
  between operations  0.73 us (1%)
    all_to_all x5, blocking collectives, exchange(): return lax.all_to_all(values, axes, split_axis=0, concat_axis=0, tiled=True)  49.7 us
    pallas_call x1, Pallas kernels, compact_on_device(): call(mlp_kernel, [((rows, tile_w, width), bf16), ((tile_w, width), f32),...  3.61 us
    ppermute x1, starting transfers between devices, compact_on_device(): w_x = lax.ppermute(w_out, 'col', [(i, i ^ 2) for i in range(cols)])  2.92 us
    pallas_call x1, Pallas kernels, compact_on_device(): call(qkv_kernel, [((rows * cols, 4, piece), bf16), fc2_part, ((2, half_ro...  2.25 us
    ppermute x1, waiting for transfers between devices, compact_on_device(): across = lax.ppermute(masked, 'col', [(i, i ^ 3) for i in range(cols)])  1.88 us
    ppermute x1, starting transfers between devices, compact_on_device(): other = lax.ppermute(given, 'row', [(i, i ^ 1) for i in range(rows)])  1.58 us
  transfers between devices with their start and end apart: 7, of which 2 were waited for; matrix products, arithmetic and copies ran while one was open for 0% of the time, Pallas kernels for 7%

profile of v8, /device:TPU:0, one launch (start us, length us, event | category | flops | bytes accessed | tf_op | source)
XLA Modules:
  0.0 68.5 jit_solution(3117804658132664216)
XLA Ops:
  0.6 0.5 collective-permute-start
  1.1 0.1 collective-permute-start.2
  1.2 2.9 %collective-permute-start.3 = (bf16[768,384]{1,0:T(8,128)(2,1)}, bf16[768,384]{1,0:T(8,128)(2,1)S(1)}, u32[]{:S(2)}, u32[]{:S(2)}) collective-permute-start(bf16[768,384]{1,0:T(8,128)(2,1)} %w_hbm.1), channel_id=1, source_target_pairs={{0,2},{1,3},{2,0},{3,1},{4,6},{5,7},{6,4},{7,5},{8,10},{9,11},{10,... | collective-permute-start | bytes 1769480 | tf_op jit(solution)/shard_map/ppermute | solution.py:540
  4.1 1.3 %shard_map.158 = (bf16[8,2,3072]{2,1,0:T(2,128)(2,1)S(1)}, bf16[2,128,384]{2,1,0:T(8,128)(2,1)S(1)}, f32[4,8,3072]{2,1,0:T(8,128)S(1)}, f32[4,16,128]{2,1,0:T(8,128)S(1)}, f32[16,16]{1,0:T(8,128)S(1)}) custom-call(bf16[2,3072]{1,0:T(2,128)(2,1)} %states_hbm.1, bf16[128,768]{1,0:T(8,128)(2,1)} %text_k_hbm.1, bf16[128,768]{1,0:T(8,128)(2,1)} %text_v_hbm.1, ...), custom_call_target="tpu_custom_call" | custom-call | tf_op jit(solution)/shard_map/pallas_call | solution.py:524
  5.4 1.6 %collective-permute-start.1 = (bf16[2,128,384]{2,1,0:T(8,128)(2,1)S(1)}, bf16[2,128,384]{2,1,0:T(8,128)(2,1)S(1)}, u32[]{:S(2)}, u32[]{:S(2)}) collective-permute-start(bf16[2,128,384]{2,1,0:T(8,128)(2,1)S(1)} %get-tuple-element.27), channel_id=1, source_target_pairs={{0,4},{4,0},{8,12},{12,8},{16,20},{20,16},{24,28},{28,24},{1,5},{5... | collective-permute-start | bytes 589832 | tf_op jit(solution)/shard_map/ppermute | solution.py:539
  7.0 11.8 %all_to_all.25.tokens_ref = bf16[8,2,3072]{2,1,0:T(2,128)(2,1)S(1)} all-to-all(bf16[8,2,3072]{2,1,0:T(2,128)(2,1)S(1)} %get-tuple-element.24), channel_id=1, replica_groups=mesh['row'=8,'col'=4] {'row'}, dimensions={0} | all-to-all | bytes 196608 | tf_op jit(solution)/shard_map/all_to_all | solution.py:498
  18.8 0.0 collective-permute-done.w_ref
  18.8 0.0 slice-start
  18.8 2.3 %shard_map.159 = (bf16[32,4,384]{2,1,0:T(4,128)(2,1)S(1)}, bf16[512,3072]{1,0:T(8,128)(2,1)S(1)}, bf16[2,128,384]{2,1,0:T(8,128)(2,1)S(1)}, f32[16,384]{1,0:T(8,128)S(1)}, f32[16,384]{1,0:T(8,128)S(1)}) custom-call(s32[4]{0:T(128)} %step_hbm.3, bf16[8,2,3072]{2,1,0:T(2,128)(2,1)S(1)} %all_to_all.25.tokens_ref, f32[4,8,3072]{2,1,0:T(8,128)S(1)} %get-tuple-element.25.mod_ref, ...), custom_call_target="tpu_custom_call" | custom-call | tf_op jit(solution)/shard_map/pallas_call | solution.py:544
  21.1 0.0 collective-permute-done.1.other_ref
  21.1 0.0 collective-permute-done.2.w1_ref
  21.1 9.5 %all_to_all.26 = bf16[32,4,384]{2,1,0:T(4,128)(2,1)S(1)} all-to-all(bf16[32,4,384]{2,1,0:T(4,128)(2,1)S(1)} %get-tuple-element.28), channel_id=1, replica_groups=mesh['row'=8,'col'=4] {'col','row'}, dimensions={0} | all-to-all | bytes 196608 | tf_op jit(solution)/shard_map/all_to_all | solution.py:498
  30.6 1.1 %shard_map.160 = (bf16[32,4,384]{2,1,0:T(4,128)(2,1)S(1)}, bf16[768,384]{1,0:T(8,128)(2,1)S(1)}) custom-call(bf16[4,8,4,384]{3,2,1,0:T(4,128)(2,1)S(1)} %bitcast.8, bf16[2,128,384]{2,1,0:T(8,128)(2,1)S(1)} %get-tuple-element.29.text_ref, bf16[2,128,384]{2,1,0:T(8,128)(2,1)S(1)} %collective-permute-done.1.other_ref, ...), custom_call_target="tpu_custom_call" | custom-call | tf_op jit(solution)/shard_map/pallas_call | solution.py:564
  31.7 0.0 collective-permute-done.3.w2_ref
  31.7 0.2 collective-permute-start.4
  31.9 9.2 %all_to_all.27.mixed_ref = bf16[32,4,384]{2,1,0:T(4,128)(2,1)S(1)} all-to-all(bf16[32,4,384]{2,1,0:T(4,128)(2,1)S(1)} %get-tuple-element.34), channel_id=1, replica_groups=mesh['row'=8,'col'=4] {'col','row'}, dimensions={0} | all-to-all | bytes 196608 | tf_op jit(solution)/shard_map/all_to_all | solution.py:498
  41.1 0.0 collective-permute-done.4.w3_ref
  41.1 0.4 shard_map.161
  41.6 9.7 %all_to_all.28.first_ref = bf16[8,16,384]{2,1,0:T(8,128)(2,1)S(1)} all-to-all(bf16[8,16,384]{2,1,0:T(8,128)(2,1)S(1)} %shard_map.161), channel_id=1, replica_groups=mesh['row'=8,'col'=4] {'row'}, dimensions={0} | all-to-all | bytes 196608 | tf_op jit(solution)/shard_map/all_to_all | solution.py:498
  51.3 0.0 slice-done
  51.3 0.0 slice-done.1
  51.3 0.0 slice-done.2
  51.3 0.0 copy-start
  51.3 3.6 %shard_map.162 = (bf16[8,2,3072]{2,1,0:T(2,128)(2,1)S(1)}, f32[2,3072]{1,0:T(2,128)S(1)}, bf16[64,3072]{1,0:T(8,128)(2,1)S(1)}, f32[2,3072]{1,0:T(2,128)S(1)}, f32[2,64]{1,0:T(2,128)S(1)}) custom-call(s32[4]{0:T(128)} %step_hbm.3, s32[2,4]{1,0:T(2,128)} %bitcast.11, bf16[8,16,384]{2,1,0:T(8,128)(2,1)S(1)} %all_to_all.28.first_ref, ...), custom_call_target="tpu_custom_call" | custom-call | tf_op jit(solution)/shard_map/pallas_call | solution.py:577
  54.9 9.5 %all_to_all.29.terms_ref = bf16[8,2,3072]{2,1,0:T(2,128)(2,1)S(1)} all-to-all(bf16[8,2,3072]{2,1,0:T(2,128)(2,1)S(1)} %get-tuple-element.41), channel_id=1, replica_groups=mesh['row'=8,'col'=4] {'row'}, dimensions={0} | all-to-all | bytes 196608 | tf_op jit(solution)/shard_map/all_to_all | solution.py:498
  64.4 0.4 shard_map.163.masked_ref
  64.8 0.0 collective-permute-start.5
  64.8 0.8 %collective-permute-start.6 = (f32[2,64]{1,0:T(2,128)S(1)}, f32[2,64]{1,0:T(2,128)S(1)}, u32[]{:S(2)}, u32[]{:S(2)}) collective-permute-start(f32[2,64]{1,0:T(2,128)S(1)} %shard_map.163.masked_ref), channel_id=1, source_target_pairs={{0,3},{1,2},{2,1},{3,0},{4,7},{5,6},{6,5},{7,4},{8,11},{9,10},{10,... | collective-permute-start | bytes 1544 | tf_op jit(solution)/shard_map/ppermute | solution.py:595
  65.6 0.4 collective-permute-done.5.near_ref
  66.0 1.9 %collective-permute-done.6.far_ref = f32[2,64]{1,0:T(2,128)S(1)} collective-permute-done((f32[2,64]{1,0:T(2,128)S(1)}, f32[2,64]{1,0:T(2,128)S(1)}, u32[]{:S(2)}, u32[]{:S(2)}) %collective-permute-start.6) | collective-permute-done | bytes 544 | tf_op jit(solution)/shard_map/ppermute | solution.py:595
  67.9 0.0 copy-done
  67.9 0.6 shard_map.164
  (3 shorter events, 0.0 us)
Async XLA Ops:
  0.6 18.2 %collective-permute-start = (bf16[3072,1152]{1,0:T(8,128)(2,1)}, bf16[3072,1152]{1,0:T(8,128)(2,1)S(1)}, u32[]{:S(2)}, u32[]{:S(2)}) collective-permute-start(bf16[3072,1152]{1,0:T(8,128)(2,1)} %param.23), channel_id=1, source_target_pairs={{0,1},{1,0},{2,3},{3,2},{4,5},{5,4},{6,7},{7,6},{8,9},{9,8},{10,11... | collective-permute-start | bytes 21233672 | tf_op jit(solution)/shard_map/ppermute | solution.py:560
  1.1 19.9 %collective-permute-start.2 = (bf16[768,384]{1,0:T(8,128)(2,1)}, bf16[768,384]{1,0:T(8,128)(2,1)S(1)}, u32[]{:S(2)}, u32[]{:S(2)}) collective-permute-start(bf16[768,384]{1,0:T(8,128)(2,1)} %w_hbm.1), channel_id=1, source_target_pairs={{0,1},{1,0},{2,3},{3,2},{4,5},{5,4},{6,7},{7,6},{8,9},{9,8},{10,11... | collective-permute-start | bytes 1769480 | tf_op jit(solution)/shard_map/ppermute | solution.py:541
  1.2 30.5 %collective-permute-start.3 = (bf16[768,384]{1,0:T(8,128)(2,1)}, bf16[768,384]{1,0:T(8,128)(2,1)S(1)}, u32[]{:S(2)}, u32[]{:S(2)}) collective-permute-start(bf16[768,384]{1,0:T(8,128)(2,1)} %w_hbm.1), channel_id=1, source_target_pairs={{0,2},{1,3},{2,0},{3,1},{4,6},{5,7},{6,4},{7,5},{8,10},{9,11},{10,... | collective-permute-start | bytes 1769480 | tf_op jit(solution)/shard_map/ppermute | solution.py:540
  5.4 15.6 %collective-permute-start.1 = (bf16[2,128,384]{2,1,0:T(8,128)(2,1)S(1)}, bf16[2,128,384]{2,1,0:T(8,128)(2,1)S(1)}, u32[]{:S(2)}, u32[]{:S(2)}) collective-permute-start(bf16[2,128,384]{2,1,0:T(8,128)(2,1)S(1)} %get-tuple-element.27), channel_id=1, source_target_pairs={{0,4},{4,0},{8,12},{12,8},{16,20},{20,16},{24,28},{28,24},{1,5},{5... | collective-permute-start | bytes 589832 | tf_op jit(solution)/shard_map/ppermute | solution.py:539
  18.8 32.5 %slice-start = ((s8[9437184]{0:T(1024)(128)(4,1)}), s8[4194304]{0:T(1024)(128)(4,1)S(1)}, s32[]{:S(2)}) async-start(s8[9437184]{0:T(1024)(128)(4,1)} %bitcast.6), calls=%async_computation.5 | async-start | bytes 8388608
  18.8 32.5 %slice-start.1 = ((s8[9437184]{0:T(1024)(128)(4,1)}), s8[4194304]{0:T(1024)(128)(4,1)S(1)}, s32[]{:S(2)}) async-start(s8[9437184]{0:T(1024)(128)(4,1)} %bitcast.6), calls=%async_computation.6 | async-start | bytes 8388608
  18.8 32.5 %slice-start.2 = ((s8[9437184]{0:T(1024)(128)(4,1)}), s8[1048576]{0:T(1024)(128)(4,1)S(1)}, s32[]{:S(2)}) async-start(s8[9437184]{0:T(1024)(128)(4,1)} %bitcast.6), calls=%async_computation.7 | async-start | bytes 2097152
  31.7 9.4 %collective-permute-start.4 = (bf16[768,384]{1,0:T(8,128)(2,1)S(1)}, bf16[768,384]{1,0:T(8,128)(2,1)S(1)}, u32[]{:S(2)}, u32[]{:S(2)}) collective-permute-start(bf16[768,384]{1,0:T(8,128)(2,1)S(1)} %collective-permute-done.3.w2_ref), channel_id=1, source_target_pairs={{0,1},{1,0},{2,3},{3,2},{4,5},{5,4},{6,7},{7,6},{8,9},{9,8},{10,11... | collective-permute-start | bytes 1769480 | tf_op jit(solution)/shard_map/ppermute | solution.py:571
  51.3 16.6 %copy-start = (f32[2,64]{1,0:T(2,128)S(1)}, f32[2,64]{1,0:T(2,128)}, u32[]{:S(2)}) copy-start(f32[2,64]{1,0:T(2,128)} %latent_ref.1) | copy-start | bytes 1540
  64.8 1.2 %collective-permute-start.5 = (f32[2,64]{1,0:T(2,128)S(1)}, f32[2,64]{1,0:T(2,128)S(1)}, u32[]{:S(2)}, u32[]{:S(2)}) collective-permute-start(f32[2,64]{1,0:T(2,128)S(1)} %shard_map.163.masked_ref), channel_id=1, source_target_pairs={{0,1},{1,0},{2,3},{3,2},{4,5},{5,4},{6,7},{7,6},{8,9},{9,8},{10,11... | collective-permute-start | bytes 1544 | tf_op jit(solution)/shard_map/ppermute | solution.py:594
  64.8 3.0 %collective-permute-start.6 = (f32[2,64]{1,0:T(2,128)S(1)}, f32[2,64]{1,0:T(2,128)S(1)}, u32[]{:S(2)}, u32[]{:S(2)}) collective-permute-start(f32[2,64]{1,0:T(2,128)S(1)} %shard_map.163.masked_ref), channel_id=1, source_target_pairs={{0,3},{1,2},{2,1},{3,0},{4,7},{5,6},{6,5},{7,4},{8,11},{9,10},{10,... | collective-permute-start | bytes 1544 | tf_op jit(solution)/shard_map/ppermute | solution.py:595

commit v9 on v8

--- a/solution.py
+++ b/solution.py
@@ -338,9 +338,11 @@
     states = spread_ref[0]
     for r in range(1, spread_ref.shape[0]):
         spread_ref[r] = states
-    for copy in text_copies:
+    for copy in text_copies[3:]:
         copy.wait()
     turn_tables(lax.axis_index("row") // 2, size_ref, offset_ref, q_gain_ref, k_gain_ref, turn_ref, mask_ref)
+    for copy in text_copies[:3]:
+        copy.wait()
 
 
 def attention_kernel(

time: 68.8 us -> 68.8 us (level)
  no operation moved by 1% of the time
where the time goes in v9:
time: 68.8 us; the launch traced here: 68.4 us
  blocking collectives  49.7 us (72%)
  Pallas kernels  9.56 us (14%)
  starting transfers between devices  6.06 us (9%)
  waiting for transfers between devices  2.27 us (3%)
  between operations  0.73 us (1%)
    all_to_all x5, blocking collectives, exchange(): return lax.all_to_all(values, axes, split_axis=0, concat_axis=0, tiled=True)  49.7 us
    pallas_call x1, Pallas kernels, compact_on_device(): call(mlp_kernel, [((rows, tile_w, width), bf16), ((tile_w, width), f32),...  3.61 us
    ppermute x1, starting transfers between devices, compact_on_device(): w_x = lax.ppermute(w_out, 'col', [(i, i ^ 2) for i in range(cols)])  2.92 us
    pallas_call x1, Pallas kernels, compact_on_device(): call(qkv_kernel, [((rows * cols, 4, piece), bf16), fc2_part, ((2, half_ro...  2.25 us
    ppermute x1, waiting for transfers between devices, compact_on_device(): across = lax.ppermute(masked, 'col', [(i, i ^ 3) for i in range(cols)])  1.88 us
    ppermute x1, starting transfers between devices, compact_on_device(): other = lax.ppermute(given, 'row', [(i, i ^ 1) for i in range(rows)])  1.58 us
  transfers between devices with their start and end apart: 7, of which 2 were waited for; matrix products, arithmetic and copies ran while one was open for 0% of the time, Pallas kernels for 7%

profile of v9, /device:TPU:0, one launch (start us, length us, event | category | flops | bytes accessed | tf_op | source)
XLA Modules:
  0.0 68.4 jit_solution(15316613692593939366)
XLA Ops:
  0.6 0.5 collective-permute-start
  1.1 0.1 collective-permute-start.2
  1.2 2.9 %collective-permute-start.3 = (bf16[768,384]{1,0:T(8,128)(2,1)}, bf16[768,384]{1,0:T(8,128)(2,1)S(1)}, u32[]{:S(2)}, u32[]{:S(2)}) collective-permute-start(bf16[768,384]{1,0:T(8,128)(2,1)} %w_hbm.1), channel_id=1, source_target_pairs={{0,2},{1,3},{2,0},{3,1},{4,6},{5,7},{6,4},{7,5},{8,10},{9,11},{10,... | collective-permute-start | bytes 1769480 | tf_op jit(solution)/shard_map/ppermute | solution.py:542
  4.1 1.2 %shard_map.158 = (bf16[8,2,3072]{2,1,0:T(2,128)(2,1)S(1)}, bf16[2,128,384]{2,1,0:T(8,128)(2,1)S(1)}, f32[4,8,3072]{2,1,0:T(8,128)S(1)}, f32[4,16,128]{2,1,0:T(8,128)S(1)}, f32[16,16]{1,0:T(8,128)S(1)}) custom-call(bf16[2,3072]{1,0:T(2,128)(2,1)} %states_hbm.1, bf16[128,768]{1,0:T(8,128)(2,1)} %text_k_hbm.1, bf16[128,768]{1,0:T(8,128)(2,1)} %text_v_hbm.1, ...), custom_call_target="tpu_custom_call" | custom-call | tf_op jit(solution)/shard_map/pallas_call | solution.py:526
  5.3 1.6 %collective-permute-start.1 = (bf16[2,128,384]{2,1,0:T(8,128)(2,1)S(1)}, bf16[2,128,384]{2,1,0:T(8,128)(2,1)S(1)}, u32[]{:S(2)}, u32[]{:S(2)}) collective-permute-start(bf16[2,128,384]{2,1,0:T(8,128)(2,1)S(1)} %get-tuple-element.27), channel_id=1, source_target_pairs={{0,4},{4,0},{8,12},{12,8},{16,20},{20,16},{24,28},{28,24},{1,5},{5... | collective-permute-start | bytes 589832 | tf_op jit(solution)/shard_map/ppermute | solution.py:541
  6.9 11.8 %all_to_all.25.tokens_ref = bf16[8,2,3072]{2,1,0:T(2,128)(2,1)S(1)} all-to-all(bf16[8,2,3072]{2,1,0:T(2,128)(2,1)S(1)} %get-tuple-element.24), channel_id=1, replica_groups=mesh['row'=8,'col'=4] {'row'}, dimensions={0} | all-to-all | bytes 196608 | tf_op jit(solution)/shard_map/all_to_all | solution.py:500
  18.7 0.0 collective-permute-done.w_ref
  18.7 0.0 slice-start
  18.7 2.3 %shard_map.159 = (bf16[32,4,384]{2,1,0:T(4,128)(2,1)S(1)}, bf16[512,3072]{1,0:T(8,128)(2,1)S(1)}, bf16[2,128,384]{2,1,0:T(8,128)(2,1)S(1)}, f32[16,384]{1,0:T(8,128)S(1)}, f32[16,384]{1,0:T(8,128)S(1)}) custom-call(s32[4]{0:T(128)} %step_hbm.3, bf16[8,2,3072]{2,1,0:T(2,128)(2,1)S(1)} %all_to_all.25.tokens_ref, f32[4,8,3072]{2,1,0:T(8,128)S(1)} %get-tuple-element.25.mod_ref, ...), custom_call_target="tpu_custom_call" | custom-call | tf_op jit(solution)/shard_map/pallas_call | solution.py:546
  21.0 0.0 collective-permute-done.1.other_ref
  21.0 0.0 collective-permute-done.2.w1_ref
  21.0 9.5 %all_to_all.26 = bf16[32,4,384]{2,1,0:T(4,128)(2,1)S(1)} all-to-all(bf16[32,4,384]{2,1,0:T(4,128)(2,1)S(1)} %get-tuple-element.28), channel_id=1, replica_groups=mesh['row'=8,'col'=4] {'col','row'}, dimensions={0} | all-to-all | bytes 196608 | tf_op jit(solution)/shard_map/all_to_all | solution.py:500
  30.5 1.1 %shard_map.160 = (bf16[32,4,384]{2,1,0:T(4,128)(2,1)S(1)}, bf16[768,384]{1,0:T(8,128)(2,1)S(1)}) custom-call(bf16[4,8,4,384]{3,2,1,0:T(4,128)(2,1)S(1)} %bitcast.8, bf16[2,128,384]{2,1,0:T(8,128)(2,1)S(1)} %get-tuple-element.29.text_ref, bf16[2,128,384]{2,1,0:T(8,128)(2,1)S(1)} %collective-permute-done.1.other_ref, ...), custom_call_target="tpu_custom_call" | custom-call | tf_op jit(solution)/shard_map/pallas_call | solution.py:566
  31.6 0.0 collective-permute-done.3.w2_ref
  31.6 0.2 collective-permute-start.4
  31.8 9.2 %all_to_all.27.mixed_ref = bf16[32,4,384]{2,1,0:T(4,128)(2,1)S(1)} all-to-all(bf16[32,4,384]{2,1,0:T(4,128)(2,1)S(1)} %get-tuple-element.34), channel_id=1, replica_groups=mesh['row'=8,'col'=4] {'col','row'}, dimensions={0} | all-to-all | bytes 196608 | tf_op jit(solution)/shard_map/all_to_all | solution.py:500
  41.0 0.0 collective-permute-done.4.w3_ref
  41.0 0.4 shard_map.161
  41.5 9.7 %all_to_all.28.first_ref = bf16[8,16,384]{2,1,0:T(8,128)(2,1)S(1)} all-to-all(bf16[8,16,384]{2,1,0:T(8,128)(2,1)S(1)} %shard_map.161), channel_id=1, replica_groups=mesh['row'=8,'col'=4] {'row'}, dimensions={0} | all-to-all | bytes 196608 | tf_op jit(solution)/shard_map/all_to_all | solution.py:500
  51.2 0.0 slice-done
  51.2 0.0 slice-done.1
  51.2 0.0 slice-done.2
  51.2 0.0 copy-start
  51.2 3.6 %shard_map.162 = (bf16[8,2,3072]{2,1,0:T(2,128)(2,1)S(1)}, f32[2,3072]{1,0:T(2,128)S(1)}, bf16[64,3072]{1,0:T(8,128)(2,1)S(1)}, f32[2,3072]{1,0:T(2,128)S(1)}, f32[2,64]{1,0:T(2,128)S(1)}) custom-call(s32[4]{0:T(128)} %step_hbm.3, s32[2,4]{1,0:T(2,128)} %bitcast.11, bf16[8,16,384]{2,1,0:T(8,128)(2,1)S(1)} %all_to_all.28.first_ref, ...), custom_call_target="tpu_custom_call" | custom-call | tf_op jit(solution)/shard_map/pallas_call | solution.py:579
  54.8 9.5 %all_to_all.29.terms_ref = bf16[8,2,3072]{2,1,0:T(2,128)(2,1)S(1)} all-to-all(bf16[8,2,3072]{2,1,0:T(2,128)(2,1)S(1)} %get-tuple-element.41), channel_id=1, replica_groups=mesh['row'=8,'col'=4] {'row'}, dimensions={0} | all-to-all | bytes 196608 | tf_op jit(solution)/shard_map/all_to_all | solution.py:500
  64.3 0.4 shard_map.163.masked_ref
  64.7 0.0 collective-permute-start.5
  64.8 0.8 %collective-permute-start.6 = (f32[2,64]{1,0:T(2,128)S(1)}, f32[2,64]{1,0:T(2,128)S(1)}, u32[]{:S(2)}, u32[]{:S(2)}) collective-permute-start(f32[2,64]{1,0:T(2,128)S(1)} %shard_map.163.masked_ref), channel_id=1, source_target_pairs={{0,3},{1,2},{2,1},{3,0},{4,7},{5,6},{6,5},{7,4},{8,11},{9,10},{10,... | collective-permute-start | bytes 1544 | tf_op jit(solution)/shard_map/ppermute | solution.py:597
  65.5 0.4 collective-permute-done.5.near_ref
  65.9 1.9 %collective-permute-done.6.far_ref = f32[2,64]{1,0:T(2,128)S(1)} collective-permute-done((f32[2,64]{1,0:T(2,128)S(1)}, f32[2,64]{1,0:T(2,128)S(1)}, u32[]{:S(2)}, u32[]{:S(2)}) %collective-permute-start.6) | collective-permute-done | bytes 544 | tf_op jit(solution)/shard_map/ppermute | solution.py:597
  67.8 0.0 copy-done
  67.8 0.6 shard_map.164
  (3 shorter events, 0.0 us)
Async XLA Ops:
  0.6 18.1 %collective-permute-start = (bf16[3072,1152]{1,0:T(8,128)(2,1)}, bf16[3072,1152]{1,0:T(8,128)(2,1)S(1)}, u32[]{:S(2)}, u32[]{:S(2)}) collective-permute-start(bf16[3072,1152]{1,0:T(8,128)(2,1)} %param.23), channel_id=1, source_target_pairs={{0,1},{1,0},{2,3},{3,2},{4,5},{5,4},{6,7},{7,6},{8,9},{9,8},{10,11... | collective-permute-start | bytes 21233672 | tf_op jit(solution)/shard_map/ppermute | solution.py:562
  1.1 19.8 %collective-permute-start.2 = (bf16[768,384]{1,0:T(8,128)(2,1)}, bf16[768,384]{1,0:T(8,128)(2,1)S(1)}, u32[]{:S(2)}, u32[]{:S(2)}) collective-permute-start(bf16[768,384]{1,0:T(8,128)(2,1)} %w_hbm.1), channel_id=1, source_target_pairs={{0,1},{1,0},{2,3},{3,2},{4,5},{5,4},{6,7},{7,6},{8,9},{9,8},{10,11... | collective-permute-start | bytes 1769480 | tf_op jit(solution)/shard_map/ppermute | solution.py:543
  1.2 30.4 %collective-permute-start.3 = (bf16[768,384]{1,0:T(8,128)(2,1)}, bf16[768,384]{1,0:T(8,128)(2,1)S(1)}, u32[]{:S(2)}, u32[]{:S(2)}) collective-permute-start(bf16[768,384]{1,0:T(8,128)(2,1)} %w_hbm.1), channel_id=1, source_target_pairs={{0,2},{1,3},{2,0},{3,1},{4,6},{5,7},{6,4},{7,5},{8,10},{9,11},{10,... | collective-permute-start | bytes 1769480 | tf_op jit(solution)/shard_map/ppermute | solution.py:542
  5.3 15.6 %collective-permute-start.1 = (bf16[2,128,384]{2,1,0:T(8,128)(2,1)S(1)}, bf16[2,128,384]{2,1,0:T(8,128)(2,1)S(1)}, u32[]{:S(2)}, u32[]{:S(2)}) collective-permute-start(bf16[2,128,384]{2,1,0:T(8,128)(2,1)S(1)} %get-tuple-element.27), channel_id=1, source_target_pairs={{0,4},{4,0},{8,12},{12,8},{16,20},{20,16},{24,28},{28,24},{1,5},{5... | collective-permute-start | bytes 589832 | tf_op jit(solution)/shard_map/ppermute | solution.py:541
  18.7 32.5 %slice-start = ((s8[9437184]{0:T(1024)(128)(4,1)}), s8[4194304]{0:T(1024)(128)(4,1)S(1)}, s32[]{:S(2)}) async-start(s8[9437184]{0:T(1024)(128)(4,1)} %bitcast.6), calls=%async_computation.5 | async-start | bytes 8388608
  18.7 32.5 %slice-start.1 = ((s8[9437184]{0:T(1024)(128)(4,1)}), s8[4194304]{0:T(1024)(128)(4,1)S(1)}, s32[]{:S(2)}) async-start(s8[9437184]{0:T(1024)(128)(4,1)} %bitcast.6), calls=%async_computation.6 | async-start | bytes 8388608
  18.7 32.5 %slice-start.2 = ((s8[9437184]{0:T(1024)(128)(4,1)}), s8[1048576]{0:T(1024)(128)(4,1)S(1)}, s32[]{:S(2)}) async-start(s8[9437184]{0:T(1024)(128)(4,1)} %bitcast.6), calls=%async_computation.7 | async-start | bytes 2097152
  31.6 9.4 %collective-permute-start.4 = (bf16[768,384]{1,0:T(8,128)(2,1)S(1)}, bf16[768,384]{1,0:T(8,128)(2,1)S(1)}, u32[]{:S(2)}, u32[]{:S(2)}) collective-permute-start(bf16[768,384]{1,0:T(8,128)(2,1)S(1)} %collective-permute-done.3.w2_ref), channel_id=1, source_target_pairs={{0,1},{1,0},{2,3},{3,2},{4,5},{5,4},{6,7},{7,6},{8,9},{9,8},{10,11... | collective-permute-start | bytes 1769480 | tf_op jit(solution)/shard_map/ppermute | solution.py:573
  51.2 16.6 %copy-start = (f32[2,64]{1,0:T(2,128)S(1)}, f32[2,64]{1,0:T(2,128)}, u32[]{:S(2)}) copy-start(f32[2,64]{1,0:T(2,128)} %latent_ref.1) | copy-start | bytes 1540
  64.7 1.2 %collective-permute-start.5 = (f32[2,64]{1,0:T(2,128)S(1)}, f32[2,64]{1,0:T(2,128)S(1)}, u32[]{:S(2)}, u32[]{:S(2)}) collective-permute-start(f32[2,64]{1,0:T(2,128)S(1)} %shard_map.163.masked_ref), channel_id=1, source_target_pairs={{0,1},{1,0},{2,3},{3,2},{4,5},{5,4},{6,7},{7,6},{8,9},{9,8},{10,11... | collective-permute-start | bytes 1544 | tf_op jit(solution)/shard_map/ppermute | solution.py:596
  64.8 3.0 %collective-permute-start.6 = (f32[2,64]{1,0:T(2,128)S(1)}, f32[2,64]{1,0:T(2,128)S(1)}, u32[]{:S(2)}, u32[]{:S(2)}) collective-permute-start(f32[2,64]{1,0:T(2,128)S(1)} %shard_map.163.masked_ref), channel_id=1, source_target_pairs={{0,3},{1,2},{2,1},{3,0},{4,7},{5,6},{6,5},{7,4},{8,11},{9,10},{10,... | collective-permute-start | bytes 1544 | tf_op jit(solution)/shard_map/ppermute | solution.py:597

commit v10 on v9

--- a/solution.py
+++ b/solution.py
@@ -324,13 +324,13 @@
     states_copy, *text_copies = start_copies(
         [
             (states_hbm, spread_ref.at[0]),
-            (k_hbm.at[:, part], given_ref.at[0]),
-            (v_hbm.at[:, part], given_ref.at[1]),
-            (mod_hbm, mod_ref),
             (size_hbm, size_ref),
             (offset_hbm, offset_ref),
             (q_gain_hbm, q_gain_ref),
             (k_gain_hbm, k_gain_ref),
+            (k_hbm.at[:, part], given_ref.at[0]),
+            (v_hbm.at[:, part], given_ref.at[1]),
+            (mod_hbm, mod_ref),
         ],
         sems,
     )
@@ -338,10 +338,10 @@
     states = spread_ref[0]
     for r in range(1, spread_ref.shape[0]):
         spread_ref[r] = states
-    for copy in text_copies[3:]:
+    for copy in text_copies[:4]:
         copy.wait()
     turn_tables(lax.axis_index("row") // 2, size_ref, offset_ref, q_gain_ref, k_gain_ref, turn_ref, mask_ref)
-    for copy in text_copies[:3]:
+    for copy in text_copies[4:]:
         copy.wait()
 
 

time: 68.8 us -> 68.8 us (level)
  no operation moved by 1% of the time
where the time goes in v10:
time: 68.8 us; the launch traced here: 68.4 us
  blocking collectives  49.7 us (72%)
  Pallas kernels  9.58 us (14%)
  starting transfers between devices  6.06 us (9%)
  waiting for transfers between devices  2.27 us (3%)
  between operations  0.73 us (1%)
    all_to_all x5, blocking collectives, exchange(): return lax.all_to_all(values, axes, split_axis=0, concat_axis=0, tiled=True)  49.7 us
    pallas_call x1, Pallas kernels, compact_on_device(): call(mlp_kernel, [((rows, tile_w, width), bf16), ((tile_w, width), f32),...  3.61 us
    ppermute x1, starting transfers between devices, compact_on_device(): w_x = lax.ppermute(w_out, 'col', [(i, i ^ 2) for i in range(cols)])  2.92 us
    pallas_call x1, Pallas kernels, compact_on_device(): call(qkv_kernel, [((rows * cols, 4, piece), bf16), fc2_part, ((2, half_ro...  2.25 us
    ppermute x1, waiting for transfers between devices, compact_on_device(): across = lax.ppermute(masked, 'col', [(i, i ^ 3) for i in range(cols)])  1.88 us
    ppermute x1, starting transfers between devices, compact_on_device(): other = lax.ppermute(given, 'row', [(i, i ^ 1) for i in range(rows)])  1.58 us
  transfers between devices with their start and end apart: 7, of which 2 were waited for; matrix products, arithmetic and copies ran while one was open for 0% of the time, Pallas kernels for 7%

profile of v10, /device:TPU:0, one launch (start us, length us, event | category | flops | bytes accessed | tf_op | source)
XLA Modules:
  0.0 68.4 jit_solution(2005522509103119639)
XLA Ops:
  0.6 0.5 collective-permute-start
  1.1 0.1 collective-permute-start.2
  1.2 2.9 %collective-permute-start.3 = (bf16[768,384]{1,0:T(8,128)(2,1)}, bf16[768,384]{1,0:T(8,128)(2,1)S(1)}, u32[]{:S(2)}, u32[]{:S(2)}) collective-permute-start(bf16[768,384]{1,0:T(8,128)(2,1)} %w_hbm.1), channel_id=1, source_target_pairs={{0,2},{1,3},{2,0},{3,1},{4,6},{5,7},{6,4},{7,5},{8,10},{9,11},{10,... | collective-permute-start | bytes 1769480 | tf_op jit(solution)/shard_map/ppermute | solution.py:542
  4.1 1.2 %shard_map.158 = (bf16[8,2,3072]{2,1,0:T(2,128)(2,1)S(1)}, bf16[2,128,384]{2,1,0:T(8,128)(2,1)S(1)}, f32[4,8,3072]{2,1,0:T(8,128)S(1)}, f32[4,16,128]{2,1,0:T(8,128)S(1)}, f32[16,16]{1,0:T(8,128)S(1)}) custom-call(bf16[2,3072]{1,0:T(2,128)(2,1)} %states_hbm.1, bf16[128,768]{1,0:T(8,128)(2,1)} %text_k_hbm.1, bf16[128,768]{1,0:T(8,128)(2,1)} %text_v_hbm.1, ...), custom_call_target="tpu_custom_call" | custom-call | tf_op jit(solution)/shard_map/pallas_call | solution.py:526
  5.4 1.6 %collective-permute-start.1 = (bf16[2,128,384]{2,1,0:T(8,128)(2,1)S(1)}, bf16[2,128,384]{2,1,0:T(8,128)(2,1)S(1)}, u32[]{:S(2)}, u32[]{:S(2)}) collective-permute-start(bf16[2,128,384]{2,1,0:T(8,128)(2,1)S(1)} %get-tuple-element.27), channel_id=1, source_target_pairs={{0,4},{4,0},{8,12},{12,8},{16,20},{20,16},{24,28},{28,24},{1,5},{5... | collective-permute-start | bytes 589832 | tf_op jit(solution)/shard_map/ppermute | solution.py:541
  6.9 11.8 %all_to_all.25.tokens_ref = bf16[8,2,3072]{2,1,0:T(2,128)(2,1)S(1)} all-to-all(bf16[8,2,3072]{2,1,0:T(2,128)(2,1)S(1)} %get-tuple-element.24), channel_id=1, replica_groups=mesh['row'=8,'col'=4] {'row'}, dimensions={0} | all-to-all | bytes 196608 | tf_op jit(solution)/shard_map/all_to_all | solution.py:500
  18.7 0.0 collective-permute-done.w_ref
  18.7 0.0 slice-start
  18.7 2.3 %shard_map.159 = (bf16[32,4,384]{2,1,0:T(4,128)(2,1)S(1)}, bf16[512,3072]{1,0:T(8,128)(2,1)S(1)}, bf16[2,128,384]{2,1,0:T(8,128)(2,1)S(1)}, f32[16,384]{1,0:T(8,128)S(1)}, f32[16,384]{1,0:T(8,128)S(1)}) custom-call(s32[4]{0:T(128)} %step_hbm.3, bf16[8,2,3072]{2,1,0:T(2,128)(2,1)S(1)} %all_to_all.25.tokens_ref, f32[4,8,3072]{2,1,0:T(8,128)S(1)} %get-tuple-element.25.mod_ref, ...), custom_call_target="tpu_custom_call" | custom-call | tf_op jit(solution)/shard_map/pallas_call | solution.py:546
  21.0 0.0 collective-permute-done.1.other_ref
  21.0 0.0 collective-permute-done.2.w1_ref
  21.0 9.5 %all_to_all.26 = bf16[32,4,384]{2,1,0:T(4,128)(2,1)S(1)} all-to-all(bf16[32,4,384]{2,1,0:T(4,128)(2,1)S(1)} %get-tuple-element.28), channel_id=1, replica_groups=mesh['row'=8,'col'=4] {'col','row'}, dimensions={0} | all-to-all | bytes 196608 | tf_op jit(solution)/shard_map/all_to_all | solution.py:500
  30.5 1.1 %shard_map.160 = (bf16[32,4,384]{2,1,0:T(4,128)(2,1)S(1)}, bf16[768,384]{1,0:T(8,128)(2,1)S(1)}) custom-call(bf16[4,8,4,384]{3,2,1,0:T(4,128)(2,1)S(1)} %bitcast.8, bf16[2,128,384]{2,1,0:T(8,128)(2,1)S(1)} %get-tuple-element.29.text_ref, bf16[2,128,384]{2,1,0:T(8,128)(2,1)S(1)} %collective-permute-done.1.other_ref, ...), custom_call_target="tpu_custom_call" | custom-call | tf_op jit(solution)/shard_map/pallas_call | solution.py:566
  31.6 0.0 collective-permute-done.3.w2_ref
  31.6 0.2 collective-permute-start.4
  31.8 9.2 %all_to_all.27.mixed_ref = bf16[32,4,384]{2,1,0:T(4,128)(2,1)S(1)} all-to-all(bf16[32,4,384]{2,1,0:T(4,128)(2,1)S(1)} %get-tuple-element.34), channel_id=1, replica_groups=mesh['row'=8,'col'=4] {'col','row'}, dimensions={0} | all-to-all | bytes 196608 | tf_op jit(solution)/shard_map/all_to_all | solution.py:500
  41.1 0.0 collective-permute-done.4.w3_ref
  41.1 0.4 shard_map.161
  41.5 9.7 %all_to_all.28.first_ref = bf16[8,16,384]{2,1,0:T(8,128)(2,1)S(1)} all-to-all(bf16[8,16,384]{2,1,0:T(8,128)(2,1)S(1)} %shard_map.161), channel_id=1, replica_groups=mesh['row'=8,'col'=4] {'row'}, dimensions={0} | all-to-all | bytes 196608 | tf_op jit(solution)/shard_map/all_to_all | solution.py:500
  51.2 0.0 slice-done
  51.2 0.0 slice-done.1
  51.2 0.0 slice-done.2
  51.2 0.0 copy-start
  51.2 3.6 %shard_map.162 = (bf16[8,2,3072]{2,1,0:T(2,128)(2,1)S(1)}, f32[2,3072]{1,0:T(2,128)S(1)}, bf16[64,3072]{1,0:T(8,128)(2,1)S(1)}, f32[2,3072]{1,0:T(2,128)S(1)}, f32[2,64]{1,0:T(2,128)S(1)}) custom-call(s32[4]{0:T(128)} %step_hbm.3, s32[2,4]{1,0:T(2,128)} %bitcast.11, bf16[8,16,384]{2,1,0:T(8,128)(2,1)S(1)} %all_to_all.28.first_ref, ...), custom_call_target="tpu_custom_call" | custom-call | tf_op jit(solution)/shard_map/pallas_call | solution.py:579
  54.8 9.5 %all_to_all.29.terms_ref = bf16[8,2,3072]{2,1,0:T(2,128)(2,1)S(1)} all-to-all(bf16[8,2,3072]{2,1,0:T(2,128)(2,1)S(1)} %get-tuple-element.41), channel_id=1, replica_groups=mesh['row'=8,'col'=4] {'row'}, dimensions={0} | all-to-all | bytes 196608 | tf_op jit(solution)/shard_map/all_to_all | solution.py:500
  64.4 0.4 shard_map.163.masked_ref
  64.8 0.0 collective-permute-start.5
  64.8 0.8 %collective-permute-start.6 = (f32[2,64]{1,0:T(2,128)S(1)}, f32[2,64]{1,0:T(2,128)S(1)}, u32[]{:S(2)}, u32[]{:S(2)}) collective-permute-start(f32[2,64]{1,0:T(2,128)S(1)} %shard_map.163.masked_ref), channel_id=1, source_target_pairs={{0,3},{1,2},{2,1},{3,0},{4,7},{5,6},{6,5},{7,4},{8,11},{9,10},{10,... | collective-permute-start | bytes 1544 | tf_op jit(solution)/shard_map/ppermute | solution.py:597
  65.6 0.4 collective-permute-done.5.near_ref
  65.9 1.9 %collective-permute-done.6.far_ref = f32[2,64]{1,0:T(2,128)S(1)} collective-permute-done((f32[2,64]{1,0:T(2,128)S(1)}, f32[2,64]{1,0:T(2,128)S(1)}, u32[]{:S(2)}, u32[]{:S(2)}) %collective-permute-start.6) | collective-permute-done | bytes 544 | tf_op jit(solution)/shard_map/ppermute | solution.py:597
  67.8 0.0 copy-done
  67.8 0.6 shard_map.164
  (3 shorter events, 0.0 us)
Async XLA Ops:
  0.6 18.1 %collective-permute-start = (bf16[3072,1152]{1,0:T(8,128)(2,1)}, bf16[3072,1152]{1,0:T(8,128)(2,1)S(1)}, u32[]{:S(2)}, u32[]{:S(2)}) collective-permute-start(bf16[3072,1152]{1,0:T(8,128)(2,1)} %param.23), channel_id=1, source_target_pairs={{0,1},{1,0},{2,3},{3,2},{4,5},{5,4},{6,7},{7,6},{8,9},{9,8},{10,11... | collective-permute-start | bytes 21233672 | tf_op jit(solution)/shard_map/ppermute | solution.py:562
  1.1 19.9 %collective-permute-start.2 = (bf16[768,384]{1,0:T(8,128)(2,1)}, bf16[768,384]{1,0:T(8,128)(2,1)S(1)}, u32[]{:S(2)}, u32[]{:S(2)}) collective-permute-start(bf16[768,384]{1,0:T(8,128)(2,1)} %w_hbm.1), channel_id=1, source_target_pairs={{0,1},{1,0},{2,3},{3,2},{4,5},{5,4},{6,7},{7,6},{8,9},{9,8},{10,11... | collective-permute-start | bytes 1769480 | tf_op jit(solution)/shard_map/ppermute | solution.py:543
  1.2 30.4 %collective-permute-start.3 = (bf16[768,384]{1,0:T(8,128)(2,1)}, bf16[768,384]{1,0:T(8,128)(2,1)S(1)}, u32[]{:S(2)}, u32[]{:S(2)}) collective-permute-start(bf16[768,384]{1,0:T(8,128)(2,1)} %w_hbm.1), channel_id=1, source_target_pairs={{0,2},{1,3},{2,0},{3,1},{4,6},{5,7},{6,4},{7,5},{8,10},{9,11},{10,... | collective-permute-start | bytes 1769480 | tf_op jit(solution)/shard_map/ppermute | solution.py:542
  5.4 15.6 %collective-permute-start.1 = (bf16[2,128,384]{2,1,0:T(8,128)(2,1)S(1)}, bf16[2,128,384]{2,1,0:T(8,128)(2,1)S(1)}, u32[]{:S(2)}, u32[]{:S(2)}) collective-permute-start(bf16[2,128,384]{2,1,0:T(8,128)(2,1)S(1)} %get-tuple-element.27), channel_id=1, source_target_pairs={{0,4},{4,0},{8,12},{12,8},{16,20},{20,16},{24,28},{28,24},{1,5},{5... | collective-permute-start | bytes 589832 | tf_op jit(solution)/shard_map/ppermute | solution.py:541
  18.7 32.5 %slice-start = ((s8[9437184]{0:T(1024)(128)(4,1)}), s8[4194304]{0:T(1024)(128)(4,1)S(1)}, s32[]{:S(2)}) async-start(s8[9437184]{0:T(1024)(128)(4,1)} %bitcast.6), calls=%async_computation.5 | async-start | bytes 8388608
  18.7 32.5 %slice-start.1 = ((s8[9437184]{0:T(1024)(128)(4,1)}), s8[4194304]{0:T(1024)(128)(4,1)S(1)}, s32[]{:S(2)}) async-start(s8[9437184]{0:T(1024)(128)(4,1)} %bitcast.6), calls=%async_computation.6 | async-start | bytes 8388608
  18.7 32.5 %slice-start.2 = ((s8[9437184]{0:T(1024)(128)(4,1)}), s8[1048576]{0:T(1024)(128)(4,1)S(1)}, s32[]{:S(2)}) async-start(s8[9437184]{0:T(1024)(128)(4,1)} %bitcast.6), calls=%async_computation.7 | async-start | bytes 2097152
  31.6 9.4 %collective-permute-start.4 = (bf16[768,384]{1,0:T(8,128)(2,1)S(1)}, bf16[768,384]{1,0:T(8,128)(2,1)S(1)}, u32[]{:S(2)}, u32[]{:S(2)}) collective-permute-start(bf16[768,384]{1,0:T(8,128)(2,1)S(1)} %collective-permute-done.3.w2_ref), channel_id=1, source_target_pairs={{0,1},{1,0},{2,3},{3,2},{4,5},{5,4},{6,7},{7,6},{8,9},{9,8},{10,11... | collective-permute-start | bytes 1769480 | tf_op jit(solution)/shard_map/ppermute | solution.py:573
  51.2 16.6 %copy-start = (f32[2,64]{1,0:T(2,128)S(1)}, f32[2,64]{1,0:T(2,128)}, u32[]{:S(2)}) copy-start(f32[2,64]{1,0:T(2,128)} %latent_ref.1) | copy-start | bytes 1540
  64.8 1.2 %collective-permute-start.5 = (f32[2,64]{1,0:T(2,128)S(1)}, f32[2,64]{1,0:T(2,128)S(1)}, u32[]{:S(2)}, u32[]{:S(2)}) collective-permute-start(f32[2,64]{1,0:T(2,128)S(1)} %shard_map.163.masked_ref), channel_id=1, source_target_pairs={{0,1},{1,0},{2,3},{3,2},{4,5},{5,4},{6,7},{7,6},{8,9},{9,8},{10,11... | collective-permute-start | bytes 1544 | tf_op jit(solution)/shard_map/ppermute | solution.py:596
  64.8 3.0 %collective-permute-start.6 = (f32[2,64]{1,0:T(2,128)S(1)}, f32[2,64]{1,0:T(2,128)S(1)}, u32[]{:S(2)}, u32[]{:S(2)}) collective-permute-start(f32[2,64]{1,0:T(2,128)S(1)} %shard_map.163.masked_ref), channel_id=1, source_target_pairs={{0,3},{1,2},{2,1},{3,0},{4,7},{5,6},{6,5},{7,4},{8,11},{9,10},{10,... | collective-permute-start | bytes 1544 | tf_op jit(solution)/shard_map/ppermute | solution.py:597
